TPU v7x, 512 devices: a whole 4x4x16 slice. The times are simulated.
512 devices in a mesh: sx: 32 (over z_hi, x, y), sy: 16 (over z_lo, core).
Axes of the slice: x: 4, y: 4, z: 16 (z_hi: 2, z_lo: 8; z = z_hi * 8 + z_lo), core: 2. Of those that a mesh axis runs over, the one named last changes fastest.
Arguments:
- volume: bfloat16 [32, 512, 4096], P(None, 'sx', 'sy'), may hold values from -6 to 6
- w_first: bfloat16 [27, 32, 32], replicated, may hold values from -0.21875 to 0.21875
- down_weight: bfloat16 [2048, 128], replicated, may hold values from -0.125 to 0.125
- w_coarse: bfloat16 [4, 27, 128, 128], replicated, may hold values from -0.15625 to 0.15625
- w_up: bfloat16 [128, 2048], replicated, may hold values from -0.5 to 0.5
- closing_weight: bfloat16 [27, 32, 64], replicated, may hold values from -0.21875 to 0.21875
Outputs:
- result: bfloat16 [32, 512, 4096], P(None, 'sx', 'sy')
All inputs are finite; a program needn't handle non-finite values.
Results may differ from a plain program's by a relative error of at most 0.0095.
Values may be sent and summed in bfloat16 or wider, within the bound.
No kernel may reach another device: no remote copies, remote signals or barrier semaphores. Data moves between devices by JAX's collectives and lax.ppermute only.
A program may use at most 64 MiB of HBM per device.

v0:
```python
import jax
import jax.numpy as jnp
from jax import lax
from jax.sharding import PartitionSpec as P

NZ = 16


def padded_2(array, sides, width):
    for axis, dim in sides:
        size, length = (lax.axis_size(axis), array.shape[dim])
        up = [(i, (i + 1) % size) for i in range(size - 1)]
        down = [(j, i) for i, j in up]
        last = lax.slice_in_dim(array, length - width, length, axis=dim)
        leading = lax.slice_in_dim(array, 0, width, axis=dim)
        before = lax.ppermute(last, axis, up)
        after = lax.ppermute(leading, axis, down)
        array = jnp.concatenate([before, array, after], axis=dim)
    return array


def fine_conv(padded, weight):
    in_width, broadened_x, flat = padded.shape
    voxel_count_x = broadened_x - 2
    voxel_count_y = flat // NZ - 2
    out_width = weight.shape[1]
    position = lax.broadcasted_iota(jnp.int32, (1, 1, flat), 2) % NZ
    bordered = jnp.pad(padded, ((0, 0), (0, 0), (1, 1)))
    shifted_list = []
    for offset_z in (-1, 0, 1):
        shifted = bordered[:, :, 1 + offset_z : 1 + offset_z + flat]
        inside = (position + offset_z >= 0) & (position + offset_z < NZ)
        shifted_list.append(jnp.where(inside, shifted, jnp.zeros_like(shifted)))
    stacked = jnp.concatenate(shifted_list, axis=0)
    kernel = (
        weight.reshape(3, 3, 3, out_width, in_width)
        .transpose(0, 1, 3, 2, 4)
        .reshape(9, out_width, 3 * in_width)
    )
    summed = jnp.zeros((out_width, voxel_count_x, voxel_count_y * NZ), jnp.float32)
    for offset in range(9):
        along_x = offset // 3
        along_y = offset % 3
        window = stacked[
            :, along_x : along_x + voxel_count_x, along_y * NZ : (along_y + voxel_count_y) * NZ
        ]
        summed = summed + jnp.einsum(
            "ok,kxf->oxf", kernel[offset], window, preferred_element_type=jnp.float32
        )
    return summed


def coarse_conv(padded, weight):
    span_x = padded.shape[0] - 2
    span_y = padded.shape[1] - 2
    span_z = padded.shape[2]
    in_width = padded.shape[3]
    out_width = weight.shape[1]
    extended = jnp.pad(padded, ((0, 0), (0, 0), (1, 1), (0, 0)))
    pieces = []
    for along_x in range(3):
        for along_y in range(3):
            for along_z in range(3):
                pieces.append(
                    extended[
                        along_x : along_x + span_x,
                        along_y : along_y + span_y,
                        along_z : along_z + span_z,
                        :,
                    ]
                )
    gathered = jnp.concatenate(pieces, axis=3).reshape(-1, 27 * in_width)
    kernel = weight.transpose(0, 2, 1).reshape(27 * in_width, out_width)
    summed = jnp.dot(gathered, kernel, preferred_element_type=jnp.float32)
    return jax.nn.relu(summed.reshape(span_x, span_y, span_z, out_width))


def strided_reduction(skip_features, down_weight, voxel_count_x, voxel_count_y):
    width = skip_features.shape[0]
    blocks = skip_features.reshape(
        width, voxel_count_x // 4, 4, voxel_count_y // 4, 4, NZ // 4, 4
    ).transpose(1, 3, 5, 0, 2, 4, 6)
    blocks = blocks.reshape(-1, width * 64)
    summed = jnp.dot(blocks, down_weight, preferred_element_type=jnp.float32)
    return summed.reshape(voxel_count_x // 4, voxel_count_y // 4, NZ // 4, down_weight.shape[1])


def expand(coarse_features, w_up):
    span_x, span_y, span_z, in_width = coarse_features.shape
    width = w_up.shape[1] // 64
    summed = jnp.dot(
        coarse_features.reshape(-1, in_width), w_up, preferred_element_type=jnp.float32
    ).astype(jnp.bfloat16)
    summed = summed.reshape(span_x, span_y, span_z, width, 4, 4, 4).transpose(3, 0, 4, 1, 5, 2, 6)
    return summed.reshape(width, 4 * span_x, 4 * span_y * NZ)


def local(volume, w_first, down_weight, w_coarse, w_up, closing_weight):
    width = volume.shape[0]
    voxel_count_x = volume.shape[1]
    voxel_count_y = volume.shape[2] // NZ
    padded = padded_2(
        volume.reshape(width, voxel_count_x, voxel_count_y, NZ), (("sx", 1), ("sy", 2)), 1
    )
    padded = padded.reshape(width, voxel_count_x + 2, (voxel_count_y + 2) * NZ)
    skip_features = jax.nn.relu(fine_conv(padded, w_first)).astype(jnp.bfloat16)
    coarse_features = strided_reduction(
        skip_features, down_weight, voxel_count_x, voxel_count_y
    ).astype(jnp.bfloat16)
    layers = w_coarse.shape[0]
    for layer_index in range(layers):
        padded_coarse = padded_2(coarse_features, (("sx", 0), ("sy", 1)), 1)
        coarse_features = coarse_conv(padded_coarse, w_coarse[layer_index]).astype(jnp.bfloat16)
    upsampled = expand(coarse_features, w_up)
    joined = jnp.concatenate([skip_features, upsampled], axis=0)
    padded_last = padded_2(
        joined.reshape(2 * width, voxel_count_x, voxel_count_y, NZ), (("sx", 1), ("sy", 2)), 1
    )
    padded_last = padded_last.reshape(2 * width, voxel_count_x + 2, (voxel_count_y + 2) * NZ)
    return fine_conv(padded_last, closing_weight).astype(jnp.bfloat16)


def solution(mesh):
    return jax.shard_map(
        local,
        mesh=mesh,
        in_specs=(P(None, "sx", "sy"), P(), P(), P(), P(), P()),
        out_specs=P(None, "sx", "sy"),
        check_vma=False,
    )
```

profile of v0, /device:TPU:127, one launch (start us, length us, event | category | flops | bytes accessed | tf_op | source)
XLA Modules:
  0.0 279.8 jit_solution(9917489790787002000)
XLA Ops:
  0.0 1.5 copy.19
  1.6 12.3 %collective-permute-start = (bf16[32,1,16,16]{0,3,2,1:T(8,128)(2,1)S(1)}, bf16[32,1,16,16]{0,3,2,1:T(8,128)(2,1)S(1)}, u32[]{:S(2)}, u32[]{:S(2)}) collective-permute-start(bf16[32,1,16,16]{0,3,2,1:T(8,128)(2,1)S(1)} %get-tuple-element.15), channel_id=1, source_target_pairs={{0,16},{16,32},{32,48},{48,64},{64,80},{80,96},{96,112},{112,128},... | collective-permute-start | bytes 49160 | tf_op jit(solution)/shard_map/ppermute | solution.py:16
  13.9 1.9 collective-permute-start.1
  15.8 16.0 %collective-permute-done.1 = bf16[32,1,16,16]{0,3,2,1:T(8,128)(2,1)S(1)} collective-permute-done((bf16[32,1,16,16]{0,3,2,1:T(8,128)(2,1)S(1)}, bf16[32,1,16,16]{0,3,2,1:T(8,128)(2,1)S(1)}, u32[]{:S(2)}, u32[]{:S(2)}) %collective-permute-start.1) | collective-permute-done | bytes 16416 | tf_op jit(solution)/shard_map/ppermute | solution.py:17
  31.9 4.6 %collective-permute-start.2 = (bf16[32,18,1,16]{0,3,2,1:T(8,128)(2,1)S(1)}, bf16[32,18,1,16]{0,3,2,1:T(8,128)(2,1)S(1)}, u32[]{:S(2)}, u32[]{:S(2)}) collective-permute-start(bf16[32,18,1,16]{0,3,2,1:T(8,128)(2,1)S(1)} %get-tuple-element.13), channel_id=1, source_target_pairs={{0,1},{1,2},{2,3},{3,4},{4,5},{5,6},{6,7},{7,8},{8,9},{9,10},{10,1... | collective-permute-start | bytes 55304 | tf_op jit(solution)/shard_map/ppermute | solution.py:16
  36.5 3.6 %collective-permute-start.3 = (bf16[32,18,1,16]{0,3,2,1:T(8,128)(2,1)S(1)}, bf16[32,18,1,16]{0,3,2,1:T(8,128)(2,1)S(1)}, u32[]{:S(2)}, u32[]{:S(2)}) collective-permute-start(bf16[32,18,1,16]{0,3,2,1:T(8,128)(2,1)S(1)} %get-tuple-element.14), channel_id=1, source_target_pairs={{1,0},{2,1},{3,2},{4,3},{5,4},{6,5},{7,6},{8,7},{9,8},{10,9},{11,1... | collective-permute-start | bytes 55304 | tf_op jit(solution)/shard_map/ppermute | solution.py:17
  40.5 2.9 %collective-permute-done.3 = bf16[32,18,1,16]{0,3,2,1:T(8,128)(2,1)S(1)} collective-permute-done((bf16[32,18,1,16]{0,3,2,1:T(8,128)(2,1)S(1)}, bf16[32,18,1,16]{0,3,2,1:T(8,128)(2,1)S(1)}, u32[]{:S(2)}, u32[]{:S(2)}) %collective-permute-start.3) | collective-permute-done | bytes 18464 | tf_op jit(solution)/shard_map/ppermute | solution.py:17
  43.8 0.7 copy.20
  44.5 0.5 slice_select_fusion.3
  45.8 0.4 convolution_add_fusion.6
  46.9 0.4 convolution_add_fusion.3
  48.0 0.4 fusion.50
  48.4 0.5 copy.23
  48.9 11.3 %copy.25 = bf16[4,4,4,32,4,4,4]{6,5,4,3,2,1,0:T(4,128)(2,1)} copy(bf16[4,4,4,32,4,4,4]{3,6,2,5,1,4,0:T(4,128)(2,1)S(1)} %bitcast.147) | data formatting | bytes 524288 | tf_op jit(solution)/shard_map/transpose | solution.py:82
  60.2 16.7 %dot_general.103 = bf16[4,4,4,2048]{3,2,1,0:T(4,128)(2,1)S(1)} reshape(bf16[4,4,4,32,4,4,4]{6,5,4,3,2,1,0:T(4,128)(2,1)} %copy.25) | data formatting | bytes 524288 | tf_op jit(solution)/shard_map/dot_general | solution.py:84
  77.2 1.9 collective-permute-start.4
  79.1 3.4 %collective-permute-start.5 = (bf16[1,4,4,128]{3,2,1,0:T(4,128)(2,1)S(1)}, bf16[1,4,4,128]{3,2,1,0:T(4,128)(2,1)S(1)}, u32[]{:S(2)}, u32[]{:S(2)}) collective-permute-start(bf16[1,4,4,128]{3,2,1,0:T(4,128)(2,1)S(1)} %get-tuple-element.46), channel_id=1, source_target_pairs={{16,0},{32,16},{48,32},{64,48},{80,64},{96,80},{112,96},{128,112},... | collective-permute-start | bytes 12296 | tf_op jit(solution)/shard_map/ppermute | solution.py:17
  82.5 14.0 %collective-permute-done.5 = bf16[1,4,4,128]{3,2,1,0:T(4,128)(2,1)S(1)} collective-permute-done((bf16[1,4,4,128]{3,2,1,0:T(4,128)(2,1)S(1)}, bf16[1,4,4,128]{3,2,1,0:T(4,128)(2,1)S(1)}, u32[]{:S(2)}, u32[]{:S(2)}) %collective-permute-start.5) | collective-permute-done | bytes 4128 | tf_op jit(solution)/shard_map/ppermute | solution.py:17
  96.5 3.0 %collective-permute-start.6 = (bf16[6,1,4,128]{3,2,1,0:T(4,128)(2,1)S(1)}, bf16[6,1,4,128]{3,2,1,0:T(4,128)(2,1)S(1)}, u32[]{:S(2)}, u32[]{:S(2)}) collective-permute-start(bf16[6,1,4,128]{3,2,1,0:T(4,128)(2,1)S(1)} %get-tuple-element.37), channel_id=1, source_target_pairs={{0,1},{1,2},{2,3},{3,4},{4,5},{5,6},{6,7},{7,8},{8,9},{9,10},{10,1... | collective-permute-start | bytes 18440 | tf_op jit(solution)/shard_map/ppermute | solution.py:16
  99.4 2.4 collective-permute-start.7
  101.8 3.6 %slice_bitcast_fusion = (bf16[27,128,128]{1,2,0:T(8,128)(2,1)S(1)}, bf16[27,128,128]{1,2,0:T(8,128)(2,1)}, bf16[27,128,128]{1,2,0:T(8,128)(2,1)}, bf16[27,128,128]{1,2,0:T(8,128)(2,1)S(1)}) fusion(bf16[4,27,128,128]{3,2,1,0:T(8,128)(2,1)} %param.9), kind=kLoop, calls=%fused_computation.55 | loop fusion | bytes 7077888 | tf_op jit(solution)/shard_map/transpose | solution.py:73
  105.4 2.2 copy.26
  108.4 1.5 fusion.51
  109.9 1.9 collective-permute-start.8
  111.8 3.4 %collective-permute-start.9 = (bf16[1,4,4,128]{3,2,1,0:T(4,128)(2,1)S(1)}, bf16[1,4,4,128]{3,2,1,0:T(4,128)(2,1)S(1)}, u32[]{:S(2)}, u32[]{:S(2)}) collective-permute-start(bf16[1,4,4,128]{3,2,1,0:T(4,128)(2,1)S(1)} %get-tuple-element.44), channel_id=1, source_target_pairs={{16,0},{32,16},{48,32},{64,48},{80,64},{96,80},{112,96},{128,112},... | collective-permute-start | bytes 12296 | tf_op jit(solution)/shard_map/ppermute | solution.py:17
  115.2 13.9 %collective-permute-done.9 = bf16[1,4,4,128]{3,2,1,0:T(4,128)(2,1)S(1)} collective-permute-done((bf16[1,4,4,128]{3,2,1,0:T(4,128)(2,1)S(1)}, bf16[1,4,4,128]{3,2,1,0:T(4,128)(2,1)S(1)}, u32[]{:S(2)}, u32[]{:S(2)}) %collective-permute-start.9) | collective-permute-done | bytes 4128 | tf_op jit(solution)/shard_map/ppermute | solution.py:17
  129.1 5.6 %collective-permute-start.10 = (bf16[6,1,4,128]{3,2,1,0:T(4,128)(2,1)S(1)}, bf16[6,1,4,128]{3,2,1,0:T(4,128)(2,1)S(1)}, u32[]{:S(2)}, u32[]{:S(2)}) collective-permute-start(bf16[6,1,4,128]{3,2,1,0:T(4,128)(2,1)S(1)} %get-tuple-element.33), channel_id=1, source_target_pairs={{0,1},{1,2},{2,3},{3,4},{4,5},{5,6},{6,7},{7,8},{8,9},{9,10},{10,1... | collective-permute-start | bytes 18440 | tf_op jit(solution)/shard_map/ppermute | solution.py:16
  134.7 1.9 collective-permute-start.11
  136.6 2.2 copy.27
  138.8 2.0 collective-permute-done.11
  141.6 1.5 fusion.52
  143.1 1.9 collective-permute-start.12
  145.1 3.4 %collective-permute-start.13 = (bf16[1,4,4,128]{3,2,1,0:T(4,128)(2,1)S(1)}, bf16[1,4,4,128]{3,2,1,0:T(4,128)(2,1)S(1)}, u32[]{:S(2)}, u32[]{:S(2)}) collective-permute-start(bf16[1,4,4,128]{3,2,1,0:T(4,128)(2,1)S(1)} %get-tuple-element.42), channel_id=1, source_target_pairs={{16,0},{32,16},{48,32},{64,48},{80,64},{96,80},{112,96},{128,112},... | collective-permute-start | bytes 12296 | tf_op jit(solution)/shard_map/ppermute | solution.py:17
  148.4 13.9 %collective-permute-done.13 = bf16[1,4,4,128]{3,2,1,0:T(4,128)(2,1)S(1)} collective-permute-done((bf16[1,4,4,128]{3,2,1,0:T(4,128)(2,1)S(1)}, bf16[1,4,4,128]{3,2,1,0:T(4,128)(2,1)S(1)}, u32[]{:S(2)}, u32[]{:S(2)}) %collective-permute-start.13) | collective-permute-done | bytes 4128 | tf_op jit(solution)/shard_map/ppermute | solution.py:17
  162.4 4.0 %collective-permute-start.14 = (bf16[6,1,4,128]{3,2,1,0:T(4,128)(2,1)S(1)}, bf16[6,1,4,128]{3,2,1,0:T(4,128)(2,1)S(1)}, u32[]{:S(2)}, u32[]{:S(2)}) collective-permute-start(bf16[6,1,4,128]{3,2,1,0:T(4,128)(2,1)S(1)} %get-tuple-element.29), channel_id=1, source_target_pairs={{0,1},{1,2},{2,3},{3,4},{4,5},{5,6},{6,7},{7,8},{8,9},{9,10},{10,1... | collective-permute-start | bytes 18440 | tf_op jit(solution)/shard_map/ppermute | solution.py:16
  166.4 2.1 collective-permute-start.15
  168.5 1.7 copy.28
  170.2 2.4 collective-permute-done.15
  173.3 1.5 fusion.53
  174.8 1.9 collective-permute-start.16
  176.8 3.4 %collective-permute-start.17 = (bf16[1,4,4,128]{3,2,1,0:T(4,128)(2,1)S(1)}, bf16[1,4,4,128]{3,2,1,0:T(4,128)(2,1)S(1)}, u32[]{:S(2)}, u32[]{:S(2)}) collective-permute-start(bf16[1,4,4,128]{3,2,1,0:T(4,128)(2,1)S(1)} %get-tuple-element.40), channel_id=1, source_target_pairs={{16,0},{32,16},{48,32},{64,48},{80,64},{96,80},{112,96},{128,112},... | collective-permute-start | bytes 12296 | tf_op jit(solution)/shard_map/ppermute | solution.py:17
  180.1 13.9 %collective-permute-done.17 = bf16[1,4,4,128]{3,2,1,0:T(4,128)(2,1)S(1)} collective-permute-done((bf16[1,4,4,128]{3,2,1,0:T(4,128)(2,1)S(1)}, bf16[1,4,4,128]{3,2,1,0:T(4,128)(2,1)S(1)}, u32[]{:S(2)}, u32[]{:S(2)}) %collective-permute-start.17) | collective-permute-done | bytes 4128 | tf_op jit(solution)/shard_map/ppermute | solution.py:17
  194.1 3.6 %collective-permute-start.18 = (bf16[6,1,4,128]{3,2,1,0:T(4,128)(2,1)S(1)}, bf16[6,1,4,128]{3,2,1,0:T(4,128)(2,1)S(1)}, u32[]{:S(2)}, u32[]{:S(2)}) collective-permute-start(bf16[6,1,4,128]{3,2,1,0:T(4,128)(2,1)S(1)} %get-tuple-element.25), channel_id=1, source_target_pairs={{0,1},{1,2},{2,3},{3,4},{4,5},{5,6},{6,7},{7,8},{8,9},{9,10},{10,1... | collective-permute-start | bytes 18440 | tf_op jit(solution)/shard_map/ppermute | solution.py:16
  197.7 1.9 collective-permute-start.19
  199.6 1.3 copy.29
  200.9 2.9 %collective-permute-done.19 = bf16[6,1,4,128]{3,2,1,0:T(4,128)(2,1)S(1)} collective-permute-done((bf16[6,1,4,128]{3,2,1,0:T(4,128)(2,1)S(1)}, bf16[6,1,4,128]{3,2,1,0:T(4,128)(2,1)S(1)}, u32[]{:S(2)}, u32[]{:S(2)}) %collective-permute-start.19) | collective-permute-done | bytes 6176 | tf_op jit(solution)/shard_map/ppermute | solution.py:17
  205.2 19.1 %reshape.116 = bf16[4,4,4,32,4,4,4]{6,5,4,3,2,1,0:T(4,128)(2,1)} reshape(bf16[64,2048]{1,0:T(8,128)(2,1)S(1)} %convolution_convert_fusion) | data formatting | bytes 524288 | tf_op jit(solution)/shard_map/reshape | solution.py:94
  224.3 12.8 %copy.30 = bf16[32,4,4,4,4,4,4]{0,6,5,4,3,2,1:T(4,128)(2,1)S(1)} copy(bf16[32,4,4,4,4,4,4]{6,4,2,0,5,3,1:T(4,128)(2,1)} %bitcast.146) | data formatting | bytes 524288 | tf_op jit(solution)/shard_map/transpose | solution.py:94
  237.2 2.1 collective-permute-start.20
  239.3 3.4 %collective-permute-start.21 = (bf16[64,1,16,16]{0,3,2,1:T(8,128)(2,1)S(1)}, bf16[64,1,16,16]{0,3,2,1:T(8,128)(2,1)S(1)}, u32[]{:S(2)}, u32[]{:S(2)}) collective-permute-start(bf16[64,1,16,16]{0,3,2,1:T(8,128)(2,1)S(1)} %get-tuple-element.12), channel_id=1, source_target_pairs={{16,0},{32,16},{48,32},{64,48},{80,64},{96,80},{112,96},{128,112},... | collective-permute-start | bytes 98312 | tf_op jit(solution)/shard_map/ppermute | solution.py:17
  242.7 14.6 %collective-permute-done.21 = bf16[64,1,16,16]{0,3,2,1:T(8,128)(2,1)S(1)} collective-permute-done((bf16[64,1,16,16]{0,3,2,1:T(8,128)(2,1)S(1)}, bf16[64,1,16,16]{0,3,2,1:T(8,128)(2,1)S(1)}, u32[]{:S(2)}, u32[]{:S(2)}) %collective-permute-start.21) | collective-permute-done | bytes 32800 | tf_op jit(solution)/shard_map/ppermute | solution.py:17
  257.4 4.7 %collective-permute-start.22 = (bf16[64,18,1,16]{0,3,2,1:T(8,128)(2,1)S(1)}, bf16[64,18,1,16]{0,3,2,1:T(8,128)(2,1)S(1)}, u32[]{:S(2)}, u32[]{:S(2)}) collective-permute-start(bf16[64,18,1,16]{0,3,2,1:T(8,128)(2,1)S(1)} %get-tuple-element.9), channel_id=1, source_target_pairs={{0,1},{1,2},{2,3},{3,4},{4,5},{5,6},{6,7},{7,8},{8,9},{9,10},{10,1... | collective-permute-start | bytes 110600 | tf_op jit(solution)/shard_map/ppermute | solution.py:16
  262.0 1.9 collective-permute-start.23
  264.3 4.6 %collective-permute-done.23 = bf16[64,18,1,16]{0,3,2,1:T(8,128)(2,1)S(1)} collective-permute-done((bf16[64,18,1,16]{0,3,2,1:T(8,128)(2,1)S(1)}, bf16[64,18,1,16]{0,3,2,1:T(8,128)(2,1)S(1)}, u32[]{:S(2)}, u32[]{:S(2)}) %collective-permute-start.23) | collective-permute-done | bytes 36896 | tf_op jit(solution)/shard_map/ppermute | solution.py:17
  268.9 1.7 pad_maximum_fusion.3
  270.7 1.8 copy.31
  272.4 1.0 slice_select_fusion.1
  273.8 0.6 fusion.14
  274.9 0.6 fusion.21
  275.9 0.6 fusion.27
  276.6 0.6 fusion.30
  277.6 0.6 fusion.36
  278.2 0.6 fusion.47
  278.9 0.9 copy.34
  (170 shorter events, 8.4 us)
Async XLA Ops:
  0.0 204.9 %copy-start = (bf16[128,2048]{1,0:T(8,128)(2,1)S(1)}, bf16[128,2048]{1,0:T(8,128)(2,1)}, u32[]{:S(2)}) copy-start(bf16[128,2048]{1,0:T(8,128)(2,1)} %param.10) | copy-start | bytes 1572868
  0.0 40.1 %copy-start.1 = (bf16[27,32,32]{2,1,0:T(8,128)(2,1)S(1)}, bf16[27,32,32]{2,1,0:T(8,128)(2,1)}, u32[]{:S(2)}) copy-start(bf16[27,32,32]{2,1,0:T(8,128)(2,1)} %param.7) | copy-start | bytes 165892
  1.6 14.3 %collective-permute-start = (bf16[32,1,16,16]{0,3,2,1:T(8,128)(2,1)S(1)}, bf16[32,1,16,16]{0,3,2,1:T(8,128)(2,1)S(1)}, u32[]{:S(2)}, u32[]{:S(2)}) collective-permute-start(bf16[32,1,16,16]{0,3,2,1:T(8,128)(2,1)S(1)} %get-tuple-element.15), channel_id=1, source_target_pairs={{0,16},{16,32},{32,48},{48,64},{64,80},{80,96},{96,112},{112,128},... | collective-permute-start | bytes 49160 | tf_op jit(solution)/shard_map/ppermute | solution.py:16
  13.9 18.0 %collective-permute-start.1 = (bf16[32,1,16,16]{0,3,2,1:T(8,128)(2,1)S(1)}, bf16[32,1,16,16]{0,3,2,1:T(8,128)(2,1)S(1)}, u32[]{:S(2)}, u32[]{:S(2)}) collective-permute-start(bf16[32,1,16,16]{0,3,2,1:T(8,128)(2,1)S(1)} %get-tuple-element.16), channel_id=1, source_target_pairs={{16,0},{32,16},{48,32},{64,48},{80,64},{96,80},{112,96},{128,112},... | collective-permute-start | bytes 49160 | tf_op jit(solution)/shard_map/ppermute | solution.py:17
  31.9 8.6 %collective-permute-start.2 = (bf16[32,18,1,16]{0,3,2,1:T(8,128)(2,1)S(1)}, bf16[32,18,1,16]{0,3,2,1:T(8,128)(2,1)S(1)}, u32[]{:S(2)}, u32[]{:S(2)}) collective-permute-start(bf16[32,18,1,16]{0,3,2,1:T(8,128)(2,1)S(1)} %get-tuple-element.13), channel_id=1, source_target_pairs={{0,1},{1,2},{2,3},{3,4},{4,5},{5,6},{6,7},{7,8},{8,9},{9,10},{10,1... | collective-permute-start | bytes 55304 | tf_op jit(solution)/shard_map/ppermute | solution.py:16
  36.5 6.9 %collective-permute-start.3 = (bf16[32,18,1,16]{0,3,2,1:T(8,128)(2,1)S(1)}, bf16[32,18,1,16]{0,3,2,1:T(8,128)(2,1)S(1)}, u32[]{:S(2)}, u32[]{:S(2)}) collective-permute-start(bf16[32,18,1,16]{0,3,2,1:T(8,128)(2,1)S(1)} %get-tuple-element.14), channel_id=1, source_target_pairs={{1,0},{2,1},{3,2},{4,3},{5,4},{6,5},{7,6},{8,7},{9,8},{10,9},{11,1... | collective-permute-start | bytes 55304 | tf_op jit(solution)/shard_map/ppermute | solution.py:17
  60.2 16.7 %copy-start.3 = (bf16[2048,128]{1,0:T(8,128)(2,1)S(1)}, bf16[2048,128]{1,0:T(8,128)(2,1)}, u32[]{:S(2)}) copy-start(bf16[2048,128]{1,0:T(8,128)(2,1)} %param.8) | copy-start | bytes 1572868
  77.2 5.3 %collective-permute-start.4 = (bf16[1,4,4,128]{3,2,1,0:T(4,128)(2,1)S(1)}, bf16[1,4,4,128]{3,2,1,0:T(4,128)(2,1)S(1)}, u32[]{:S(2)}, u32[]{:S(2)}) collective-permute-start(bf16[1,4,4,128]{3,2,1,0:T(4,128)(2,1)S(1)} %get-tuple-element.45), channel_id=1, source_target_pairs={{0,16},{16,32},{32,48},{48,64},{64,80},{80,96},{96,112},{112,128},... | collective-permute-start | bytes 12296 | tf_op jit(solution)/shard_map/ppermute | solution.py:16
  79.1 17.3 %collective-permute-start.5 = (bf16[1,4,4,128]{3,2,1,0:T(4,128)(2,1)S(1)}, bf16[1,4,4,128]{3,2,1,0:T(4,128)(2,1)S(1)}, u32[]{:S(2)}, u32[]{:S(2)}) collective-permute-start(bf16[1,4,4,128]{3,2,1,0:T(4,128)(2,1)S(1)} %get-tuple-element.46), channel_id=1, source_target_pairs={{16,0},{32,16},{48,32},{64,48},{80,64},{96,80},{112,96},{128,112},... | collective-permute-start | bytes 12296 | tf_op jit(solution)/shard_map/ppermute | solution.py:17
  96.5 11.1 %collective-permute-start.6 = (bf16[6,1,4,128]{3,2,1,0:T(4,128)(2,1)S(1)}, bf16[6,1,4,128]{3,2,1,0:T(4,128)(2,1)S(1)}, u32[]{:S(2)}, u32[]{:S(2)}) collective-permute-start(bf16[6,1,4,128]{3,2,1,0:T(4,128)(2,1)S(1)} %get-tuple-element.37), channel_id=1, source_target_pairs={{0,1},{1,2},{2,3},{3,4},{4,5},{5,6},{6,7},{7,8},{8,9},{9,10},{10,1... | collective-permute-start | bytes 18440 | tf_op jit(solution)/shard_map/ppermute | solution.py:16
  99.4 8.2 %collective-permute-start.7 = (bf16[6,1,4,128]{3,2,1,0:T(4,128)(2,1)S(1)}, bf16[6,1,4,128]{3,2,1,0:T(4,128)(2,1)S(1)}, u32[]{:S(2)}, u32[]{:S(2)}) collective-permute-start(bf16[6,1,4,128]{3,2,1,0:T(4,128)(2,1)S(1)} %get-tuple-element.38), channel_id=1, source_target_pairs={{1,0},{2,1},{3,2},{4,3},{5,4},{6,5},{7,6},{8,7},{9,8},{10,9},{11,1... | collective-permute-start | bytes 18440 | tf_op jit(solution)/shard_map/ppermute | solution.py:17
  109.9 5.3 %collective-permute-start.8 = (bf16[1,4,4,128]{3,2,1,0:T(4,128)(2,1)S(1)}, bf16[1,4,4,128]{3,2,1,0:T(4,128)(2,1)S(1)}, u32[]{:S(2)}, u32[]{:S(2)}) collective-permute-start(bf16[1,4,4,128]{3,2,1,0:T(4,128)(2,1)S(1)} %get-tuple-element.43), channel_id=1, source_target_pairs={{0,16},{16,32},{32,48},{48,64},{64,80},{80,96},{96,112},{112,128},... | collective-permute-start | bytes 12296 | tf_op jit(solution)/shard_map/ppermute | solution.py:16
  111.8 17.3 %collective-permute-start.9 = (bf16[1,4,4,128]{3,2,1,0:T(4,128)(2,1)S(1)}, bf16[1,4,4,128]{3,2,1,0:T(4,128)(2,1)S(1)}, u32[]{:S(2)}, u32[]{:S(2)}) collective-permute-start(bf16[1,4,4,128]{3,2,1,0:T(4,128)(2,1)S(1)} %get-tuple-element.44), channel_id=1, source_target_pairs={{16,0},{32,16},{48,32},{64,48},{80,64},{96,80},{112,96},{128,112},... | collective-permute-start | bytes 12296 | tf_op jit(solution)/shard_map/ppermute | solution.py:17
  129.1 9.7 %collective-permute-start.10 = (bf16[6,1,4,128]{3,2,1,0:T(4,128)(2,1)S(1)}, bf16[6,1,4,128]{3,2,1,0:T(4,128)(2,1)S(1)}, u32[]{:S(2)}, u32[]{:S(2)}) collective-permute-start(bf16[6,1,4,128]{3,2,1,0:T(4,128)(2,1)S(1)} %get-tuple-element.33), channel_id=1, source_target_pairs={{0,1},{1,2},{2,3},{3,4},{4,5},{5,6},{6,7},{7,8},{8,9},{9,10},{10,1... | collective-permute-start | bytes 18440 | tf_op jit(solution)/shard_map/ppermute | solution.py:16
  134.7 6.2 %collective-permute-start.11 = (bf16[6,1,4,128]{3,2,1,0:T(4,128)(2,1)S(1)}, bf16[6,1,4,128]{3,2,1,0:T(4,128)(2,1)S(1)}, u32[]{:S(2)}, u32[]{:S(2)}) collective-permute-start(bf16[6,1,4,128]{3,2,1,0:T(4,128)(2,1)S(1)} %get-tuple-element.34), channel_id=1, source_target_pairs={{1,0},{2,1},{3,2},{4,3},{5,4},{6,5},{7,6},{8,7},{9,8},{10,9},{11,1... | collective-permute-start | bytes 18440 | tf_op jit(solution)/shard_map/ppermute | solution.py:17
  143.1 5.3 %collective-permute-start.12 = (bf16[1,4,4,128]{3,2,1,0:T(4,128)(2,1)S(1)}, bf16[1,4,4,128]{3,2,1,0:T(4,128)(2,1)S(1)}, u32[]{:S(2)}, u32[]{:S(2)}) collective-permute-start(bf16[1,4,4,128]{3,2,1,0:T(4,128)(2,1)S(1)} %get-tuple-element.41), channel_id=1, source_target_pairs={{0,16},{16,32},{32,48},{48,64},{64,80},{80,96},{96,112},{112,128},... | collective-permute-start | bytes 12296 | tf_op jit(solution)/shard_map/ppermute | solution.py:16
  145.1 17.3 %collective-permute-start.13 = (bf16[1,4,4,128]{3,2,1,0:T(4,128)(2,1)S(1)}, bf16[1,4,4,128]{3,2,1,0:T(4,128)(2,1)S(1)}, u32[]{:S(2)}, u32[]{:S(2)}) collective-permute-start(bf16[1,4,4,128]{3,2,1,0:T(4,128)(2,1)S(1)} %get-tuple-element.42), channel_id=1, source_target_pairs={{16,0},{32,16},{48,32},{64,48},{80,64},{96,80},{112,96},{128,112},... | collective-permute-start | bytes 12296 | tf_op jit(solution)/shard_map/ppermute | solution.py:17
  162.4 7.8 %collective-permute-start.14 = (bf16[6,1,4,128]{3,2,1,0:T(4,128)(2,1)S(1)}, bf16[6,1,4,128]{3,2,1,0:T(4,128)(2,1)S(1)}, u32[]{:S(2)}, u32[]{:S(2)}) collective-permute-start(bf16[6,1,4,128]{3,2,1,0:T(4,128)(2,1)S(1)} %get-tuple-element.29), channel_id=1, source_target_pairs={{0,1},{1,2},{2,3},{3,4},{4,5},{5,6},{6,7},{7,8},{8,9},{9,10},{10,1... | collective-permute-start | bytes 18440 | tf_op jit(solution)/shard_map/ppermute | solution.py:16
  166.4 6.2 %collective-permute-start.15 = (bf16[6,1,4,128]{3,2,1,0:T(4,128)(2,1)S(1)}, bf16[6,1,4,128]{3,2,1,0:T(4,128)(2,1)S(1)}, u32[]{:S(2)}, u32[]{:S(2)}) collective-permute-start(bf16[6,1,4,128]{3,2,1,0:T(4,128)(2,1)S(1)} %get-tuple-element.30), channel_id=1, source_target_pairs={{1,0},{2,1},{3,2},{4,3},{5,4},{6,5},{7,6},{8,7},{9,8},{10,9},{11,1... | collective-permute-start | bytes 18440 | tf_op jit(solution)/shard_map/ppermute | solution.py:17
  174.8 5.3 %collective-permute-start.16 = (bf16[1,4,4,128]{3,2,1,0:T(4,128)(2,1)S(1)}, bf16[1,4,4,128]{3,2,1,0:T(4,128)(2,1)S(1)}, u32[]{:S(2)}, u32[]{:S(2)}) collective-permute-start(bf16[1,4,4,128]{3,2,1,0:T(4,128)(2,1)S(1)} %get-tuple-element.39), channel_id=1, source_target_pairs={{0,16},{16,32},{32,48},{48,64},{64,80},{80,96},{96,112},{112,128},... | collective-permute-start | bytes 12296 | tf_op jit(solution)/shard_map/ppermute | solution.py:16
  176.8 17.3 %collective-permute-start.17 = (bf16[1,4,4,128]{3,2,1,0:T(4,128)(2,1)S(1)}, bf16[1,4,4,128]{3,2,1,0:T(4,128)(2,1)S(1)}, u32[]{:S(2)}, u32[]{:S(2)}) collective-permute-start(bf16[1,4,4,128]{3,2,1,0:T(4,128)(2,1)S(1)} %get-tuple-element.40), channel_id=1, source_target_pairs={{16,0},{32,16},{48,32},{64,48},{80,64},{96,80},{112,96},{128,112},... | collective-permute-start | bytes 12296 | tf_op jit(solution)/shard_map/ppermute | solution.py:17
  194.1 6.9 %collective-permute-start.18 = (bf16[6,1,4,128]{3,2,1,0:T(4,128)(2,1)S(1)}, bf16[6,1,4,128]{3,2,1,0:T(4,128)(2,1)S(1)}, u32[]{:S(2)}, u32[]{:S(2)}) collective-permute-start(bf16[6,1,4,128]{3,2,1,0:T(4,128)(2,1)S(1)} %get-tuple-element.25), channel_id=1, source_target_pairs={{0,1},{1,2},{2,3},{3,4},{4,5},{5,6},{6,7},{7,8},{8,9},{9,10},{10,1... | collective-permute-start | bytes 18440 | tf_op jit(solution)/shard_map/ppermute | solution.py:16
  197.7 6.2 %collective-permute-start.19 = (bf16[6,1,4,128]{3,2,1,0:T(4,128)(2,1)S(1)}, bf16[6,1,4,128]{3,2,1,0:T(4,128)(2,1)S(1)}, u32[]{:S(2)}, u32[]{:S(2)}) collective-permute-start(bf16[6,1,4,128]{3,2,1,0:T(4,128)(2,1)S(1)} %get-tuple-element.26), channel_id=1, source_target_pairs={{1,0},{2,1},{3,2},{4,3},{5,4},{6,5},{7,6},{8,7},{9,8},{10,9},{11,1... | collective-permute-start | bytes 18440 | tf_op jit(solution)/shard_map/ppermute | solution.py:17
  237.2 26.7 %copy-start.2 = (bf16[27,32,64]{2,1,0:T(8,128)(2,1)S(1)}, bf16[27,32,64]{2,1,0:T(8,128)(2,1)}, u32[]{:S(2)}) copy-start(bf16[27,32,64]{2,1,0:T(8,128)(2,1)} %param.11) | copy-start | bytes 331780
  237.2 5.4 %collective-permute-start.20 = (bf16[64,1,16,16]{0,3,2,1:T(8,128)(2,1)S(1)}, bf16[64,1,16,16]{0,3,2,1:T(8,128)(2,1)S(1)}, u32[]{:S(2)}, u32[]{:S(2)}) collective-permute-start(bf16[64,1,16,16]{0,3,2,1:T(8,128)(2,1)S(1)} %get-tuple-element.11), channel_id=1, source_target_pairs={{0,16},{16,32},{32,48},{48,64},{64,80},{80,96},{96,112},{112,128},... | collective-permute-start | bytes 98312 | tf_op jit(solution)/shard_map/ppermute | solution.py:16
  239.3 17.9 %collective-permute-start.21 = (bf16[64,1,16,16]{0,3,2,1:T(8,128)(2,1)S(1)}, bf16[64,1,16,16]{0,3,2,1:T(8,128)(2,1)S(1)}, u32[]{:S(2)}, u32[]{:S(2)}) collective-permute-start(bf16[64,1,16,16]{0,3,2,1:T(8,128)(2,1)S(1)} %get-tuple-element.12), channel_id=1, source_target_pairs={{16,0},{32,16},{48,32},{64,48},{80,64},{96,80},{112,96},{128,112},... | collective-permute-start | bytes 98312 | tf_op jit(solution)/shard_map/ppermute | solution.py:17
  257.4 7.0 %collective-permute-start.22 = (bf16[64,18,1,16]{0,3,2,1:T(8,128)(2,1)S(1)}, bf16[64,18,1,16]{0,3,2,1:T(8,128)(2,1)S(1)}, u32[]{:S(2)}, u32[]{:S(2)}) collective-permute-start(bf16[64,18,1,16]{0,3,2,1:T(8,128)(2,1)S(1)} %get-tuple-element.9), channel_id=1, source_target_pairs={{0,1},{1,2},{2,3},{3,4},{4,5},{5,6},{6,7},{7,8},{8,9},{9,10},{10,1... | collective-permute-start | bytes 110600 | tf_op jit(solution)/shard_map/ppermute | solution.py:16
  262.0 6.9 %collective-permute-start.23 = (bf16[64,18,1,16]{0,3,2,1:T(8,128)(2,1)S(1)}, bf16[64,18,1,16]{0,3,2,1:T(8,128)(2,1)S(1)}, u32[]{:S(2)}, u32[]{:S(2)}) collective-permute-start(bf16[64,18,1,16]{0,3,2,1:T(8,128)(2,1)S(1)} %get-tuple-element.10), channel_id=1, source_target_pairs={{1,0},{2,1},{3,2},{4,3},{5,4},{6,5},{7,6},{8,7},{9,8},{10,9},{11,1... | collective-permute-start | bytes 110600 | tf_op jit(solution)/shard_map/ppermute | solution.py:17
where the time goes:
time: 281 us; the launch traced here: 280 us
  waiting for transfers between devices  101 us (36%)
  starting transfers between devices  80 us (28%)
  local copies, waits for them, and re-layouts  78.9 us (28%)
  matrix products  13.6 us (5%)
  other arithmetic  5 us (2%)
    ppermute x12, waiting for transfers between devices, padded_2(): after = lax.ppermute(leading, axis, down)  101 us
    ppermute x12, starting transfers between devices, padded_2(): before = lax.ppermute(last, axis, up)  47.5 us
    ppermute x12, starting transfers between devices, padded_2(): after = lax.ppermute(leading, axis, down)  32.6 us
    reshape x1, local copies, waits for them, and re-layouts, expand(): summed.reshape(span_x, span_y, span_z, width, 4, 4, 4)  19.1 us
    dot_general x1, local copies, waits for them, and re-layouts, strided_reduction(): summed = jnp.dot(blocks, down_weight, preferred_element_type=jnp.float32)  16.7 us
    transpose x1, local copies, waits for them, and re-layouts, expand(): summed.reshape(span_x, span_y, span_z, width, 4, 4, 4)  12.8 us
    transpose x1, local copies, waits for them, and re-layouts, strided_reduction(): blocks = skip_features.reshape(width, voxel_count_x // 4, 4, voxel_count_...  11.3 us
    transpose x5, local copies, waits for them, and re-layouts, coarse_conv(): kernel = weight.transpose(0, 2, 1).reshape(27 * in_width, out_width)  11 us
  transfers between devices with their start and end apart: 24, of which 11 were waited for; matrix products, arithmetic and copies ran while one was open for 4% of the time, Pallas kernels for 0%

commit v1 on v0

v1 whole, which is shorter than its diff:
```python
import jax
import jax.numpy as jnp
from jax import lax
from jax.experimental import pallas as pl
from jax.experimental.pallas import tpu as pltpu
from jax.sharding import PartitionSpec as P

NZ = 16
BF = jnp.bfloat16
F32 = jnp.float32
NT = (((1,), (1,)), ((), ()))
NN = (((1,), (0,)), ((), ()))
TN = (((0,), (0,)), ((), ()))


def iota(shape, dim):
    return lax.broadcasted_iota(jnp.int32, shape, dim)


def dot(a, b, dims):
    return lax.dot_general(a, b, dims, preferred_element_type=F32)


def z_shifts(value, rows):
    z = iota(value.shape, 0) & (NZ - 1)
    before = jnp.where(z == 0, 0.0, pltpu.roll(value, 1, 0))
    after = jnp.where(z == NZ - 1, 0.0, pltpu.roll(value, rows - 1, 0))
    return before, value, after


def regroup(rows, columns, row_dim, first):
    coarse = iota((rows, columns), row_dim)
    fine = iota((rows, columns), 1 - row_dim)
    offset = coarse >> 5
    y = 4 * (coarse & 7) + (offset >> 2)
    z = 4 * ((coarse >> 3) & 3) + (offset & 3)
    return jnp.where(fine == (y - first) * NZ + z, 1.0, 0.0).astype(BF)


def first_kernel(bounds, below, middle, above, w1, dwr, skip_ref, c0_ref, vz, grouped):
    for tile in range(7):
        lanes = slice(128 * tile, 128 * tile + 128)
        value = jnp.concatenate(
            [below[:, lanes].astype(F32), middle[:, lanes].astype(F32), above[:, lanes].astype(F32)], axis=0
        )
        for k, shifted in enumerate(z_shifts(value, 416)):
            vz[k, :, lanes] = shifted.astype(BF)
    to_groups = regroup(512, 384, 0, 0)
    y = (iota((384, 256), 0) >> 4) - 4
    lane = iota((384, 256), 1)
    y_inside = (y >= bounds[2]) & (y <= bounds[3])
    for g in range(3):
        summed = jnp.zeros((384, 256), F32)
        for oy in range(3):
            for oz in range(3):
                weight = jnp.concatenate([w1[0, 3 * oy + oz], w1[1, 3 * oy + oz]], axis=0)
                summed += dot(vz[oz, 16 * oy : 16 * oy + 384, 256 * g : 256 * g + 384], weight, NT)
        x = 8 * g - 4 + 4 * (lane >> 7) + (lane & 3)
        inside = y_inside & (x >= bounds[0]) & (x <= bounds[1])
        skip = jnp.where(inside, jnp.maximum(summed, 0.0), 0.0).astype(BF)
        skip_ref[:, 256 * g : 256 * g + 256] = skip
        grouped[:, 256 * g : 256 * g + 256] = dot(to_groups, skip, NN).astype(BF)
    coarse = jnp.zeros((192, 128), F32)
    for i in range(0, 16, 2):
        pieces = []
        for a in range(6):
            lanes = slice(128 * a, 128 * a + 128)
            pieces.append(
                jnp.concatenate([grouped[32 * i : 32 * i + 32, lanes], grouped[32 * i + 32 : 32 * i + 64, lanes]], axis=1)
            )
        coarse += dot(
            jnp.concatenate(pieces, axis=0), jnp.concatenate([dwr[i], dwr[i + 1]], axis=0), NN
        )
    for a in range(6):
        for z in range(4):
            c0_ref[a, :, 128 * z : 128 * z + 128] = coarse[32 * a + 8 * z : 32 * a + 8 * z + 8].astype(BF)


def closing_sum(values, weight, scratch, g):
    summed = jnp.zeros((256, 256), F32)
    for oy in range(3):
        for oz in range(3):
            summed += dot(
                weight[3 * oy + oz], scratch[oz, 16 * oy : 16 * oy + 256, 256 * g : 256 * g + 512], NT
            )
    return summed


def fill_shifts(value_of, scratch):
    for tile in range(6):
        lanes = slice(128 * tile, 128 * tile + 128)
        for k, shifted in enumerate(z_shifts(value_of(lanes), 288)):
            scratch[k, :, lanes] = shifted.astype(BF)


def skip_kernel(skip_ref, weight, out_ref, scratch):
    fill_shifts(lambda lanes: skip_ref[48:336, lanes].astype(F32), scratch)
    for g in range(2):
        out_ref[g] = closing_sum(None, weight, scratch, g)


def last_kernel(bounds, coarse_ref, w_coarse, wupr, weight, part_ref, out_ref, state, raw, up, scratch):
    value = coarse_ref[...].reshape(224, 512).astype(F32)
    for layer in range(4):
        rows_in = (14 - 2 * layer) * 16
        rows = rows_in - 32
        state[0, :rows_in] = value.astype(BF)
        state[1, :rows_in] = pltpu.roll(value, rows_in - 1, 0).astype(BF)
        state[2, :rows_in] = pltpu.roll(value, rows_in - 2, 0).astype(BF)
        low = jnp.zeros((rows, 256), F32)
        high = jnp.zeros((rows, 256), F32)
        zero = jnp.zeros((128, 128), BF)
        for oa in range(3):
            for ob in range(3):
                w = [w_coarse[layer, 9 * oa + 3 * ob + oz] for oz in range(3)]
                middle = jnp.concatenate(w, axis=1)
                w_low = jnp.concatenate([jnp.concatenate([w[1], w[2], zero], axis=1), middle], axis=0)
                w_high = jnp.concatenate([middle, jnp.concatenate([zero, w[0], w[1]], axis=1)], axis=0)
                low += dot(state[ob, 16 * oa : 16 * oa + rows, 0:384], w_low, NT)
                high += dot(state[ob, 16 * oa : 16 * oa + rows, 128:512], w_high, NT)
        index = iota((rows, 512), 0)
        a = (index >> 4) - 4 + layer
        b = index & 15
        kept = (a >= bounds[4]) & (a <= bounds[5]) & (b < 12 - 2 * layer)
        kept = kept & (b - 4 + layer >= bounds[6]) & (b - 4 + layer <= bounds[7])
        value = jnp.where(kept, jnp.maximum(jnp.concatenate([low, high], axis=1), 0.0), 0.0)
        value = value.astype(BF).astype(F32)
    cells = jnp.concatenate(
        [value[16 * a : 16 * a + 8, 128 * z : 128 * z + 128] for z in range(4) for a in range(6)], axis=0
    ).astype(BF)
    for i in range(0, 16, 2):
        pair = dot(cells, jnp.concatenate([wupr[i], wupr[i + 1]], axis=0), NT)
        for half in range(2):
            for z in range(4):
                for a in range(6):
                    raw[32 * (i + half) + 8 * z : 32 * (i + half) + 8 * z + 8, 128 * a : 128 * a + 128] = pair[
                        48 * z + 8 * a : 48 * z + 8 * a + 8, 128 * half : 128 * half + 128
                    ]
    from_groups = regroup(288, 512, 1, 3)
    for g in range(3):
        up[:, 256 * g : 256 * g + 256] = dot(from_groups, raw[:, 256 * g : 256 * g + 256].astype(BF), NN)
    fill_shifts(lambda lanes: up[:, lanes], scratch)
    for g in range(2):
        total = closing_sum(None, weight, scratch, g) + part_ref[g]
        out_ref[:, 8 * g : 8 * g + 8, :] = total.reshape(32, 8, 256).astype(BF)


VMEM = pl.BlockSpec(memory_space=pltpu.VMEM)
SMEM = pl.BlockSpec(memory_space=pltpu.SMEM)


def call(body, shapes, scratch, n_in, scalars, flops, limit):
    return pl.pallas_call(
        body,
        out_shape=[jax.ShapeDtypeStruct(s, t) for s, t in shapes],
        in_specs=([SMEM] if scalars else []) + [VMEM] * n_in,
        out_specs=[VMEM] * len(shapes),
        scratch_shapes=[pltpu.VMEM(s, t) for s, t in scratch],
        compiler_params=pltpu.CompilerParams(vmem_limit_bytes=limit << 20),
        cost_estimate=pl.CostEstimate(flops=flops, bytes_accessed=4 << 20, transcendentals=0),
        name=body.__name__,
    )


def ones_where(condition):
    return jnp.where(condition, 1.0, 0.0).astype(BF)


def place(rows, planes, shift):
    r, lane = iota((rows, 896), 0), iota((rows, 896), 1)
    return ones_where((lane & 31 == r // planes) & (lane >> 5 == r % planes + shift))


def taps(weight):
    out, width = weight.shape[1:]
    return weight.reshape(3, 9, out, width).transpose(1, 2, 0, 3).reshape(9, out, 3 * width)


def first_banded(weight):
    shape = (2, 4, 96, 384)
    xo = 4 * iota(shape, 0) + iota(shape, 1)
    d, k = iota(shape, 2), iota(shape, 3)
    select = ones_where((d & 31 == k & 31) & (k >> 5 == xo + (d >> 5)))
    banded = jnp.einsum("tod,axdk->atoxk", taps(weight), select, preferred_element_type=F32)
    return banded.astype(BF).reshape(2, 9, 128, 384)


def closing_banded(weight):
    shape = (8, 96, 512)
    xo, d, k = iota(shape, 0), iota(shape, 1), iota(shape, 2)
    select = ones_where((d & 31 == (k >> 2) & 31) & (4 * (k >> 7) + (k & 3) == xo + (d >> 5) + 3))
    banded = jnp.einsum("tod,xdk->toxk", taps(weight), select, preferred_element_type=F32)
    return banded.astype(BF).reshape(9, 256, 512)


def both_ways(array_up, array_down, axis):
    size = lax.axis_size(axis)
    up = [(i, i + 1) for i in range(size - 1)]
    down = [(j, i) for i, j in up]
    return lax.ppermute(array_up, axis, up), lax.ppermute(array_down, axis, down)


def local(volume, w_first, down_weight, w_coarse, w_up, closing_weight):
    ix, iy = lax.axis_index("sx"), lax.axis_index("sy")
    first_x, last_x = ix == 0, ix == lax.axis_size("sx") - 1
    first_y, last_y = iy == 0, iy == lax.axis_size("sy") - 1
    bounds = jnp.stack(
        [
            jnp.where(first_x, 0, -99),
            jnp.where(last_x, 15, 99),
            jnp.where(first_y, 0, -99),
            jnp.where(last_y, 15, 99),
            jnp.where(first_x, 0, -99),
            jnp.where(last_x, 3, 99),
            jnp.where(first_y, 0, -99),
            jnp.where(last_y, 3, 99),
        ]
    ).astype(jnp.int32)
    left, right = both_ways(volume[:, 8:16], volume[:, 0:8], "sx")
    rows = dot(volume.reshape(512, 256), place(512, 16, 5), TN)
    rows = rows + dot(left.reshape(256, 256), place(256, 8, -3), TN)
    rows = (rows + dot(right.reshape(256, 256), place(256, 8, 21), TN)).astype(BF)
    below, above = both_ways(rows[176:256], rows[0:80], "sy")
    skip, coarse = call(
        first_kernel,
        [((384, 768), BF), ((6, 8, 512), BF)],
        [((3, 416, 896), BF), ((512, 768), BF)],
        5,
        True,
        2 << 30,
        24,
    )(
        bounds,
        below,
        rows,
        above,
        first_banded(w_first),
        down_weight.reshape(128, 16, 128).transpose(1, 0, 2),
    )
    (part,) = call(skip_kernel, [((2, 256, 256), F32)], [((3, 288, 768), BF)], 2, False, 2 << 30, 16)(
        skip, closing_banded(closing_weight[:, :, :32])
    )
    before, after = both_ways(coarse[:, 0:4], coarse[:, 2:6], "sy")
    coarse = jnp.concatenate([before, coarse[:, 0:6], after, jnp.zeros((6, 2, 512), BF)], axis=1)
    before, after = both_ways(coarse[0:4], coarse[2:6], "sx")
    coarse = jnp.concatenate([before, coarse, after], axis=0)
    w_up_rows = lax.optimization_barrier(w_up.T).reshape(128, 16, 128).transpose(1, 0, 2)
    (result,) = call(
        last_kernel,
        [((32, 16, 256), BF)],
        [((3, 224, 512), BF), ((512, 768), F32), ((288, 768), F32), ((3, 288, 768), BF)],
        5,
        True,
        3 << 30,
        32,
    )(bounds, coarse, w_coarse, w_up_rows, closing_banded(closing_weight[:, :, 32:]), part)
    return result


def solution(mesh):
    return jax.shard_map(
        local,
        mesh=mesh,
        in_specs=(P(None, "sx", "sy"), P(), P(), P(), P(), P()),
        out_specs=P(None, "sx", "sy"),
        check_vma=False,
    )
```

time: 281 us -> 109 us (0.39)
  the two profiles are of different devices: /device:TPU:127 before, /device:TPU:62 now
where the time goes in v1:
time: 109 us; the launch traced here: 108 us
  starting transfers between devices  33.6 us (31%)
  waiting for transfers between devices  32.9 us (30%)
  local copies, waits for them, and re-layouts  16.2 us (15%)
  Pallas kernels  14.5 us (13%)
  matrix products  7.54 us (7%)
  other arithmetic  2.79 us (3%)
    ppermute x4, waiting for transfers between devices, both_ways(): lax.ppermute(array_down, axis, down)  32.8 us
    ppermute x4, starting transfers between devices, both_ways(): lax.ppermute(array_up, axis, up)  20.6 us
    ppermute x4, starting transfers between devices, both_ways(): lax.ppermute(array_down, axis, down)  13 us
    pallas_call x1, Pallas kernels, local(): call(last_kernel, [((32, 16, 256), BF)], [((3, 224, 512), BF), ((512, 768...  7.91 us
    dot_general x3, matrix products, dot(): return lax.dot_general(a, b, dims, preferred_element_type=F32)  5.09 us
    pallas_call x1, Pallas kernels, local(): call(first_kernel, [((384, 768), BF), ((6, 8, 512), BF)], [((3, 416, 896)...  5.07 us
    convert_element_type x2, local copies, waits for them, and re-layouts, closing_banded(): return banded.astype(BF).reshape(9, 256, 512)  4.26 us
    unnamed x27, local copies, waits for them, and re-layouts  3.06 us
  transfers between devices with their start and end apart: 8, of which 3 were waited for; matrix products, arithmetic and copies ran while one was open for 18% of the time, Pallas kernels for 1%

profile of v1, /device:TPU:62, one launch (start us, length us, event | category | flops | bytes accessed | tf_op | source)
XLA Modules:
  0.0 108.0 jit_solution(17211071522641201734)
XLA Ops:
  0.0 1.8 %fusion.87 = (bf16[32,8,256]{2,1,0:T(8,128)(2,1)}, bf16[32,8,256]{2,1,0:T(8,128)(2,1)}) fusion(bf16[32,16,256]{2,1,0:T(8,128)(2,1)} %param.6), kind=kLoop, calls=%fused_computation.130 | loop fusion | bytes 524288 | tf_op jit(solution)/shard_map/slice | solution.py:219
  1.8 14.4 %collective-permute-start = (bf16[32,8,256]{2,1,0:T(8,128)(2,1)}, bf16[32,8,256]{2,1,0:T(8,128)(2,1)}, u32[]{:S(2)}, u32[]{:S(2)}) collective-permute-start(bf16[32,8,256]{2,1,0:T(8,128)(2,1)} %get-tuple-element.12), channel_id=1, source_target_pairs={{0,16},{16,32},{32,48},{48,64},{64,80},{80,96},{96,112},{112,128},... | collective-permute-start | bytes 393224 | tf_op jit(solution)/shard_map/ppermute | solution.py:200
  16.2 1.9 %collective-permute-start.1 = (bf16[32,8,256]{2,1,0:T(8,128)(2,1)}, bf16[32,8,256]{2,1,0:T(8,128)(2,1)}, u32[]{:S(2)}, u32[]{:S(2)}) collective-permute-start(bf16[32,8,256]{2,1,0:T(8,128)(2,1)} %get-tuple-element.11), channel_id=1, source_target_pairs={{16,0},{32,16},{48,32},{64,48},{80,64},{96,80},{112,96},{128,112},... | collective-permute-start | bytes 393224 | tf_op jit(solution)/shard_map/ppermute | solution.py:200
  18.2 0.6 fusion.67
  18.8 1.1 %copy.38 = bf16[3,9,32,32]{3,0,2,1:T(4,128)(2,1)S(1)} copy(bf16[3,9,32,32]{3,2,1,0:T(8,128)(2,1)} %bitcast.80) | data formatting | bytes 110592 | tf_op jit(solution)/shard_map/reshape | solution.py:176
  19.9 0.2 reshape.57
  20.0 0.0 copy-done.3
  20.0 0.0 copy-start.4
  20.1 0.8 fusion.88
  20.9 0.7 convert_bitcast_fusion.2
  21.6 0.0 copy-done.7
  21.6 0.0 copy-done.9
  21.6 0.0 copy-done.4
  21.6 1.8 %fusion.5 = f32[896,256]{0,1:T(8,128)} fusion(bf16[512,256]{1,0:T(8,128)(2,1)S(1)} %bitcast.79, s32[512]{0:T(512)S(1)} %get-tuple-element.22, s32[512]{0:T(512)S(1)} %get-tuple-element.23, s32[896]{0:T(1024)S(1)} %get-tuple-element.19, s32[512]{0:T(512)S(1)} %get-tuple-element.21, s32[512]{0:T(512)S(1)} %get-tuple-element.24, ...), kind=kOutput, calls=%fused_computation.21 | convolution fusion | flops 238551040 | bytes 1196032 | tf_op jit(solution)/shard_map/dot_general | solution.py:21
  23.4 0.5 compare_and_fusion
  24.0 0.9 copy.14
  24.9 0.5 reshape.47.w1
  25.3 0.0 copy-start.2
  25.4 0.0 copy-start.5
  25.4 0.0 copy-start.6
  25.4 0.0 copy-start.11
  25.4 0.0 copy-start.12
  25.4 1.2 %copy.35 = bf16[128,16,128]{2,0,1:T(8,128)(2,1)S(1)} copy(bf16[128,16,128]{2,1,0:T(8,128)(2,1)} %bitcast.78) | data formatting | bytes 1048576 | tf_op jit(solution)/shard_map/reshape | solution.py:238
  26.7 1.1 %copy.36 = bf16[3,9,32,32]{3,0,2,1:T(4,128)(2,1)S(1)} copy(bf16[3,9,32,32]{3,2,1,0:T(8,128)(2,1)} %bitcast.77) | data formatting | bytes 110592 | tf_op jit(solution)/shard_map/reshape | solution.py:176
  27.7 0.2 reshape.60
  27.9 0.0 copy-done.2
  27.9 0.2 copy.37
  28.1 0.2 reshape.59
  28.3 0.1 stack.29.bounds
  28.4 0.0 collective-permute-done
  28.4 0.0 copy-done.5
  28.4 0.0 copy-done.6
  28.4 0.0 copy-done.11
  28.4 1.8 %convolution_add_fusion.1 = f32[896,256]{0,1:T(8,128)S(1)} fusion(f32[896,256]{0,1:T(8,128)} %fusion.5, s32[256]{0:T(256)S(1)} %get-tuple-element.28, s32[256]{0:T(256)S(1)} %copy-done.5, s32[896]{0:T(1024)S(1)} %get-tuple-element.19, s32[256]{0:T(256)S(1)} %get-tuple-element.27, s32[256]{0:T(256)S(1)} %copy-done.6, s32[896]{0:T(1024)S(1)} %get-tuple-element.20, ...), kind=kOutput, calls=%fused_computation.13 | convolution fusion | flops 119504896 | bytes 1977856 | tf_op jit(solution)/shard_map/dot_general | solution.py:21
  30.2 0.0 copy-start.8
  30.2 0.0 copy-start.10
  30.2 14.5 %collective-permute-done.1 = bf16[32,8,256]{2,1,0:T(8,128)(2,1)} collective-permute-done((bf16[32,8,256]{2,1,0:T(8,128)(2,1)}, bf16[32,8,256]{2,1,0:T(8,128)(2,1)}, u32[]{:S(2)}, u32[]{:S(2)}) %collective-permute-start.1) | collective-permute-done | bytes 131104 | tf_op jit(solution)/shard_map/ppermute | solution.py:200
  44.8 1.5 %fusion.3.middle = bf16[256,896]{1,0:T(8,128)(2,1)S(1)} fusion(f32[896,256]{0,1:T(8,128)S(1)} %convolution_add_fusion.1, s32[256]{0:T(256)S(1)} %get-tuple-element.28, s32[256]{0:T(256)S(1)} %copy-done.5, s32[896]{0:T(1024)S(1)} %get-tuple-element.19, s32[256]{0:T(256)S(1)} %get-tuple-element.27, s32[256]{0:T(256)S(1)} %copy-done.6, ...), kind=kOutput, calls=%fused_computation.17 | convolution fusion | flops 119734272 | bytes 1519104 | tf_op jit(solution)/shard_map/dot_general | solution.py:21
  46.3 1.9 %collective-permute-start.2 = (bf16[80,896]{1,0:T(8,128)(2,1)S(1)}, bf16[80,896]{1,0:T(8,128)(2,1)S(1)}, u32[]{:S(2)}, u32[]{:S(2)}) collective-permute-start(bf16[80,896]{1,0:T(8,128)(2,1)S(1)} %get-tuple-element.10), channel_id=1, source_target_pairs={{0,1},{1,2},{2,3},{3,4},{4,5},{5,6},{6,7},{7,8},{8,9},{9,10},{10,1... | collective-permute-start | bytes 430088 | tf_op jit(solution)/shard_map/ppermute | solution.py:200
  48.2 3.6 %collective-permute-start.3 = (bf16[80,896]{1,0:T(8,128)(2,1)S(1)}, bf16[80,896]{1,0:T(8,128)(2,1)S(1)}, u32[]{:S(2)}, u32[]{:S(2)}) collective-permute-start(bf16[80,896]{1,0:T(8,128)(2,1)S(1)} %get-tuple-element.9), channel_id=1, source_target_pairs={{1,0},{2,1},{3,2},{4,3},{5,4},{6,5},{7,6},{8,7},{9,8},{10,9},{11,1... | collective-permute-start | bytes 430088 | tf_op jit(solution)/shard_map/ppermute | solution.py:200
  51.9 0.9 convert_bitcast_fusion
  52.7 0.0 collective-permute-done.2.below
  52.7 1.7 %collective-permute-done.3.above = bf16[80,896]{1,0:T(8,128)(2,1)S(1)} collective-permute-done((bf16[80,896]{1,0:T(8,128)(2,1)S(1)}, bf16[80,896]{1,0:T(8,128)(2,1)S(1)}, u32[]{:S(2)}, u32[]{:S(2)}) %collective-permute-start.3) | collective-permute-done | bytes 143392 | tf_op jit(solution)/shard_map/ppermute | solution.py:200
  54.4 5.1 %first_kernel.1 = (bf16[384,768]{1,0:T(8,128)(2,1)S(1)}, bf16[6,8,512]{2,1,0:T(8,128)(2,1)S(1)}) custom-call(s32[8]{0:T(128)S(1)} %stack.29.bounds, bf16[80,896]{1,0:T(8,128)(2,1)S(1)} %collective-permute-done.2.below, bf16[256,896]{1,0:T(8,128)(2,1)S(1)} %fusion.3.middle, bf16[80,896]{1,0:T(8,128)(2,1)S(1)} %collective-permute-done.3.above, ...), custom_call_target="tpu_custom_call" | custom-call | flops 2147483648 | bytes 4194304 | tf_op jit(solution)/shard_map/first_kernel/pallas_call | solution.py:224
  59.5 0.6 fusion.90
  60.1 1.9 %collective-permute-start.4 = (bf16[6,4,512]{2,1,0:T(4,128)(2,1)}, bf16[6,4,512]{2,1,0:T(4,128)(2,1)S(1)}, u32[]{:S(2)}, u32[]{:S(2)}) collective-permute-start(bf16[6,4,512]{2,1,0:T(4,128)(2,1)} %get-tuple-element.17), channel_id=1, source_target_pairs={{0,1},{1,2},{2,3},{3,4},{4,5},{5,6},{6,7},{7,8},{8,9},{9,10},{10,1... | collective-permute-start | bytes 73736 | tf_op jit(solution)/shard_map/ppermute | solution.py:200
  62.1 4.0 %collective-permute-start.5 = (bf16[6,4,512]{2,1,0:T(4,128)(2,1)}, bf16[6,4,512]{2,1,0:T(4,128)(2,1)}, u32[]{:S(2)}, u32[]{:S(2)}) collective-permute-start(bf16[6,4,512]{2,1,0:T(4,128)(2,1)} %get-tuple-element.18), channel_id=1, source_target_pairs={{1,0},{2,1},{3,2},{4,3},{5,4},{6,5},{7,6},{8,7},{9,8},{10,9},{11,1... | collective-permute-start | bytes 73736 | tf_op jit(solution)/shard_map/ppermute | solution.py:200
  66.0 0.9 convert_bitcast_fusion.1
  66.9 2.8 %copy.32 = bf16[9,32,8,512]{3,2,1,0:T(8,128)(2,1)} copy(bf16[9,32,8,512]{3,1,0,2:T(8,128)(2,1)S(1)} %convert_bitcast_fusion) | data formatting | bytes 4718592 | tf_op jit(solution)/shard_map/convert_element_type | solution.py:193
  69.8 1.4 %copy.33 = bf16[9,32,8,512]{3,2,1,0:T(8,128)(2,1)S(1)} copy(bf16[9,32,8,512]{3,1,0,2:T(8,128)(2,1)S(1)} %convert_bitcast_fusion.1) | data formatting | bytes 4718592 | tf_op jit(solution)/shard_map/convert_element_type | solution.py:193
  71.2 1.4 %copy.16 = bf16[128,2048]{0,1:T(8,128)(2,1)S(1)} copy(bf16[128,2048]{1,0:T(8,128)(2,1)} %param.10) | data formatting | bytes 1048576 | tf_op args[4]
  72.6 0.1 copy.34
  72.7 0.0 collective-permute-done.4
  72.7 0.0 collective-permute-done.5
  72.7 0.8 pad_maximum_fusion.1
  73.6 2.4 %collective-permute-start.6 = (bf16[4,16,512]{2,1,0:T(8,128)(2,1)S(1)}, bf16[4,16,512]{2,1,0:T(8,128)(2,1)S(1)}, u32[]{:S(2)}, u32[]{:S(2)}) collective-permute-start(bf16[4,16,512]{2,1,0:T(8,128)(2,1)S(1)} %get-tuple-element.15), channel_id=1, source_target_pairs={{0,16},{16,32},{32,48},{48,64},{64,80},{80,96},{96,112},{112,128},... | collective-permute-start | bytes 196616 | tf_op jit(solution)/shard_map/ppermute | solution.py:200
  75.9 3.5 %collective-permute-start.7 = (bf16[4,16,512]{2,1,0:T(8,128)(2,1)S(1)}, bf16[4,16,512]{2,1,0:T(8,128)(2,1)S(1)}, u32[]{:S(2)}, u32[]{:S(2)}) collective-permute-start(bf16[4,16,512]{2,1,0:T(8,128)(2,1)S(1)} %get-tuple-element.16), channel_id=1, source_target_pairs={{16,0},{32,16},{48,32},{64,48},{80,64},{96,80},{112,96},{128,112},... | collective-permute-start | bytes 196616 | tf_op jit(solution)/shard_map/ppermute | solution.py:200
  79.4 0.0 copy-start
  79.4 1.7 %copy-done = bf16[9,32,8,512]{3,2,1,0:T(8,128)(2,1)S(1)} copy-done((bf16[9,32,8,512]{3,2,1,0:T(8,128)(2,1)S(1)}, bf16[9,32,8,512]{3,2,1,0:T(8,128)(2,1)}, u32[]{:S(2)}) %copy-start) | copy-done | bytes 2359320
  81.1 1.5 %skip_kernel.1.part_ref = f32[2,256,256]{2,1,0:T(8,128)S(1)} custom-call(bf16[384,768]{1,0:T(8,128)(2,1)S(1)} %get-tuple-element.8.skip_ref, bf16[9,256,512]{2,1,0:T(8,128)(2,1)S(1)} %bitcast.67), custom_call_target="tpu_custom_call" | custom-call | flops 2147483648 | bytes 4194304 | tf_op jit(solution)/shard_map/skip_kernel/pallas_call | solution.py:240
  82.6 0.0 collective-permute-done.6
  82.6 16.6 %collective-permute-done.7 = bf16[4,16,512]{2,1,0:T(8,128)(2,1)S(1)} collective-permute-done((bf16[4,16,512]{2,1,0:T(8,128)(2,1)S(1)}, bf16[4,16,512]{2,1,0:T(8,128)(2,1)S(1)}, u32[]{:S(2)}, u32[]{:S(2)}) %collective-permute-start.7) | collective-permute-done | bytes 65568 | tf_op jit(solution)/shard_map/ppermute | solution.py:200
  99.3 0.8 pad_maximum_fusion.coarse_ref
  100.1 7.9 %last_kernel.1 = bf16[32,16,256]{2,1,0:T(8,128)(2,1)} custom-call(s32[8]{0:T(128)S(1)} %stack.29.bounds, bf16[14,16,512]{2,1,0:T(8,128)(2,1)S(1)} %pad_maximum_fusion.coarse_ref, bf16[4,27,128,128]{3,2,1,0:T(8,128)(2,1)S(1)} %copy-done.1, bf16[16,128,128]{2,1,0:T(8,128)(2,1)S(1)} %bitcast.69, bf16[9,256,512]{2,1,0:T(8,128)(2,1)S(1)} %bitcast.66, ...), custom_call_target="tpu_custom_call" | custom-call | flops 3221225472 | bytes 4194304 | tf_op jit(solution)/shard_map/last_kernel/pallas_call | solution.py:248
  (20 shorter events, 0.1 us)
Async XLA Ops:
  0.0 20.0 %copy-start.3 = (bf16[27,32,64]{2,1,0:T(8,128)(2,1)S(1)}, bf16[27,32,64]{2,1,0:T(8,128)(2,1)}, u32[]{:S(2)}) copy-start(bf16[27,32,64]{2,1,0:T(8,128)(2,1)} %param.11) | copy-start | bytes 331780
  1.8 26.6 %collective-permute-start = (bf16[32,8,256]{2,1,0:T(8,128)(2,1)}, bf16[32,8,256]{2,1,0:T(8,128)(2,1)}, u32[]{:S(2)}, u32[]{:S(2)}) collective-permute-start(bf16[32,8,256]{2,1,0:T(8,128)(2,1)} %get-tuple-element.12), channel_id=1, source_target_pairs={{0,16},{16,32},{32,48},{48,64},{64,80},{80,96},{96,112},{112,128},... | collective-permute-start | bytes 393224 | tf_op jit(solution)/shard_map/ppermute | solution.py:200
  16.2 28.6 %collective-permute-start.1 = (bf16[32,8,256]{2,1,0:T(8,128)(2,1)}, bf16[32,8,256]{2,1,0:T(8,128)(2,1)}, u32[]{:S(2)}, u32[]{:S(2)}) collective-permute-start(bf16[32,8,256]{2,1,0:T(8,128)(2,1)} %get-tuple-element.11), channel_id=1, source_target_pairs={{16,0},{32,16},{48,32},{64,48},{80,64},{96,80},{112,96},{128,112},... | collective-permute-start | bytes 393224 | tf_op jit(solution)/shard_map/ppermute | solution.py:200
  18.7 2.8 %copy-start.7 = (s32[96]{0:T(128)}, s32[96]{0:T(128)S(1)}, u32[]{:S(2)}) copy-start(s32[96]{0:T(128)S(1)} %get-tuple-element.35) | copy-start | bytes 1156
  18.8 2.8 %copy-start.9 = (s32[96]{0:T(128)}, s32[96]{0:T(128)S(1)}, u32[]{:S(2)}) copy-start(s32[96]{0:T(128)S(1)} %get-tuple-element.36) | copy-start | bytes 1156
  20.0 1.5 %copy-start.4 = (bf16[32,16,256]{2,1,0:T(8,128)(2,1)S(1)}, bf16[32,16,256]{2,1,0:T(8,128)(2,1)}, u32[]{:S(2)}) copy-start(bf16[32,16,256]{2,1,0:T(8,128)(2,1)} %param.6) | copy-start | bytes 786436
  25.3 2.6 %copy-start.2 = (bf16[27,32,32]{2,1,0:T(8,128)(2,1)S(1)}, bf16[27,32,32]{2,1,0:T(8,128)(2,1)}, u32[]{:S(2)}) copy-start(bf16[27,32,32]{2,1,0:T(8,128)(2,1)} %get-tuple-element.14) | copy-start | bytes 165892
  25.4 3.0 %copy-start.5 = (s32[256]{0:T(256)S(1)}, s32[256]{0:T(256)}, u32[]{:S(2)}) copy-start(s32[256]{0:T(256)} %get-tuple-element.31) | copy-start | bytes 3076
  25.4 3.0 %copy-start.6 = (s32[256]{0:T(256)S(1)}, s32[256]{0:T(256)}, u32[]{:S(2)}) copy-start(s32[256]{0:T(256)} %get-tuple-element.32) | copy-start | bytes 3076
  25.4 3.0 %copy-start.11 = (pred[256]{0:T(512)(128)(4,1)S(1)}, pred[256]{0:T(512)(128)(4,1)}, u32[]{:S(2)}) copy-start(pred[256]{0:T(512)(128)(4,1)} %get-tuple-element.29) | copy-start | bytes 772
  25.4 3.0 %copy-start.12 = (pred[256]{0:T(512)(128)(4,1)S(1)}, pred[256]{0:T(512)(128)(4,1)}, u32[]{:S(2)}) copy-start(pred[256]{0:T(512)(128)(4,1)} %get-tuple-element.30) | copy-start | bytes 772
  30.2 21.6 %copy-start.8 = (s32[96]{0:T(128)S(1)}, s32[96]{0:T(128)}, u32[]{:S(2)}) copy-start(s32[96]{0:T(128)} %copy-done.7) | copy-start | bytes 1156
  30.2 21.6 %copy-start.10 = (s32[96]{0:T(128)S(1)}, s32[96]{0:T(128)}, u32[]{:S(2)}) copy-start(s32[96]{0:T(128)} %copy-done.9) | copy-start | bytes 1156
  46.3 6.5 %collective-permute-start.2 = (bf16[80,896]{1,0:T(8,128)(2,1)S(1)}, bf16[80,896]{1,0:T(8,128)(2,1)S(1)}, u32[]{:S(2)}, u32[]{:S(2)}) collective-permute-start(bf16[80,896]{1,0:T(8,128)(2,1)S(1)} %get-tuple-element.10), channel_id=1, source_target_pairs={{0,1},{1,2},{2,3},{3,4},{4,5},{5,6},{6,7},{7,8},{8,9},{9,10},{10,1... | collective-permute-start | bytes 430088 | tf_op jit(solution)/shard_map/ppermute | solution.py:200
  48.2 6.3 %collective-permute-start.3 = (bf16[80,896]{1,0:T(8,128)(2,1)S(1)}, bf16[80,896]{1,0:T(8,128)(2,1)S(1)}, u32[]{:S(2)}, u32[]{:S(2)}) collective-permute-start(bf16[80,896]{1,0:T(8,128)(2,1)S(1)} %get-tuple-element.9), channel_id=1, source_target_pairs={{1,0},{2,1},{3,2},{4,3},{5,4},{6,5},{7,6},{8,7},{9,8},{10,9},{11,1... | collective-permute-start | bytes 430088 | tf_op jit(solution)/shard_map/ppermute | solution.py:200
  60.1 12.6 %collective-permute-start.4 = (bf16[6,4,512]{2,1,0:T(4,128)(2,1)}, bf16[6,4,512]{2,1,0:T(4,128)(2,1)S(1)}, u32[]{:S(2)}, u32[]{:S(2)}) collective-permute-start(bf16[6,4,512]{2,1,0:T(4,128)(2,1)} %get-tuple-element.17), channel_id=1, source_target_pairs={{0,1},{1,2},{2,3},{3,4},{4,5},{5,6},{6,7},{7,8},{8,9},{9,10},{10,1... | collective-permute-start | bytes 73736 | tf_op jit(solution)/shard_map/ppermute | solution.py:200
  62.1 10.7 %collective-permute-start.5 = (bf16[6,4,512]{2,1,0:T(4,128)(2,1)}, bf16[6,4,512]{2,1,0:T(4,128)(2,1)}, u32[]{:S(2)}, u32[]{:S(2)}) collective-permute-start(bf16[6,4,512]{2,1,0:T(4,128)(2,1)} %get-tuple-element.18), channel_id=1, source_target_pairs={{1,0},{2,1},{3,2},{4,3},{5,4},{6,5},{7,6},{8,7},{9,8},{10,9},{11,1... | collective-permute-start | bytes 73736 | tf_op jit(solution)/shard_map/ppermute | solution.py:200
  73.6 9.1 %collective-permute-start.6 = (bf16[4,16,512]{2,1,0:T(8,128)(2,1)S(1)}, bf16[4,16,512]{2,1,0:T(8,128)(2,1)S(1)}, u32[]{:S(2)}, u32[]{:S(2)}) collective-permute-start(bf16[4,16,512]{2,1,0:T(8,128)(2,1)S(1)} %get-tuple-element.15), channel_id=1, source_target_pairs={{0,16},{16,32},{32,48},{48,64},{64,80},{80,96},{96,112},{112,128},... | collective-permute-start | bytes 196616 | tf_op jit(solution)/shard_map/ppermute | solution.py:200
  75.9 23.3 %collective-permute-start.7 = (bf16[4,16,512]{2,1,0:T(8,128)(2,1)S(1)}, bf16[4,16,512]{2,1,0:T(8,128)(2,1)S(1)}, u32[]{:S(2)}, u32[]{:S(2)}) collective-permute-start(bf16[4,16,512]{2,1,0:T(8,128)(2,1)S(1)} %get-tuple-element.16), channel_id=1, source_target_pairs={{16,0},{32,16},{48,32},{64,48},{80,64},{96,80},{112,96},{128,112},... | collective-permute-start | bytes 196616 | tf_op jit(solution)/shard_map/ppermute | solution.py:200
  79.4 1.7 %copy-start = (bf16[9,32,8,512]{3,2,1,0:T(8,128)(2,1)S(1)}, bf16[9,32,8,512]{3,2,1,0:T(8,128)(2,1)}, u32[]{:S(2)}) copy-start(bf16[9,32,8,512]{3,2,1,0:T(8,128)(2,1)} %copy.32) | copy-start | bytes 7077892
  81.1 19.0 %copy-start.1 = (bf16[4,27,128,128]{3,2,1,0:T(8,128)(2,1)S(1)}, bf16[4,27,128,128]{3,2,1,0:T(8,128)(2,1)}, u32[]{:S(2)}) copy-start(bf16[4,27,128,128]{3,2,1,0:T(8,128)(2,1)} %w_coarse.1) | copy-start | bytes 10616836

commit v2 on v1

--- a/solution.py
+++ b/solution.py
@@ -76,7 +76,7 @@
             c0_ref[a, :, 128 * z : 128 * z + 128] = coarse[32 * a + 8 * z : 32 * a + 8 * z + 8].astype(BF)
 
 
-def closing_sum(values, weight, scratch, g):
+def closing_sum(weight, scratch, g):
     summed = jnp.zeros((256, 256), F32)
     for oy in range(3):
         for oz in range(3):
@@ -96,10 +96,13 @@
 def skip_kernel(skip_ref, weight, out_ref, scratch):
     fill_shifts(lambda lanes: skip_ref[48:336, lanes].astype(F32), scratch)
     for g in range(2):
-        out_ref[g] = closing_sum(None, weight, scratch, g)
-
-
-def last_kernel(bounds, coarse_ref, w_coarse, wupr, weight, part_ref, out_ref, state, raw, up, scratch):
+        out_ref[g] = closing_sum(weight, scratch, g)
+
+
+def last_kernel(bounds, coarse_ref, w_hbm, wupr, weight, part_ref, out_ref, state, raw, up, scratch, w_coarse, arrived):
+    copies = [pltpu.make_async_copy(w_hbm.at[k], w_coarse.at[k], arrived.at[k]) for k in range(4)]
+    for copy in copies:
+        copy.start()
     value = coarse_ref[...].reshape(224, 512).astype(F32)
     for layer in range(4):
         rows_in = (14 - 2 * layer) * 16
@@ -110,6 +113,7 @@
         low = jnp.zeros((rows, 256), F32)
         high = jnp.zeros((rows, 256), F32)
         zero = jnp.zeros((128, 128), BF)
+        copies[layer].wait()
         for oa in range(3):
             for ob in range(3):
                 w = [w_coarse[layer, 9 * oa + 3 * ob + oz] for oz in range(3)]
@@ -140,25 +144,26 @@
     for g in range(3):
         up[:, 256 * g : 256 * g + 256] = dot(from_groups, raw[:, 256 * g : 256 * g + 256].astype(BF), NN)
     fill_shifts(lambda lanes: up[:, lanes], scratch)
+    row, column = iota((256, 256), 0), iota((256, 256), 1)
+    to_channels = jnp.where(column == ((row & 7) << 5) + (row >> 3), 1.0, 0.0).astype(BF)
     for g in range(2):
-        total = closing_sum(None, weight, scratch, g) + part_ref[g]
-        out_ref[:, 8 * g : 8 * g + 8, :] = total.reshape(32, 8, 256).astype(BF)
+        total = (closing_sum(weight, scratch, g) + part_ref[g]).astype(BF)
+        out_ref[:, 8 * g : 8 * g + 8, :] = dot(to_channels, total, NN).reshape(32, 8, 256).astype(BF)
 
 
 VMEM = pl.BlockSpec(memory_space=pltpu.VMEM)
 SMEM = pl.BlockSpec(memory_space=pltpu.SMEM)
 
 
-def call(body, shapes, scratch, n_in, scalars, flops, limit):
+def call(body, shapes, scratch, n_in, scalars, flops, limit, in_hbm=(), semaphores=()):
     return pl.pallas_call(
         body,
         out_shape=[jax.ShapeDtypeStruct(s, t) for s, t in shapes],
-        in_specs=([SMEM] if scalars else []) + [VMEM] * n_in,
+        in_specs=([SMEM] if scalars else []) + [pl.BlockSpec(memory_space=pl.ANY) if k in in_hbm else VMEM for k in range(n_in)],
         out_specs=[VMEM] * len(shapes),
-        scratch_shapes=[pltpu.VMEM(s, t) for s, t in scratch],
+        scratch_shapes=[pltpu.VMEM(s, t) for s, t in scratch] + list(semaphores),
         compiler_params=pltpu.CompilerParams(vmem_limit_bytes=limit << 20),
         cost_estimate=pl.CostEstimate(flops=flops, bytes_accessed=4 << 20, transcendentals=0),
-        name=body.__name__,
     )
 
 
@@ -166,9 +171,22 @@
     return jnp.where(condition, 1.0, 0.0).astype(BF)
 
 
-def place(rows, planes, shift):
-    r, lane = iota((rows, 896), 0), iota((rows, 896), 1)
-    return ones_where((lane & 31 == r // planes) & (lane >> 5 == r % planes + shift))
+def chosen_planes(odd):
+    row, column = iota((320, 512), 0), iota((320, 512), 1)
+    second = row >= 160
+    inner = jnp.where(second, row - 160, row)
+    plane = (inner >> 5) + jnp.where(second != odd, 11, 0)
+    return ones_where((column >> 4 == inner & 31) & (column & 15 == plane))
+
+
+def place_own():
+    r, lane = iota((512, 896), 0), iota((512, 896), 1)
+    return ones_where((lane & 31 == r >> 4) & (lane >> 5 == (r & 15) + 5))
+
+
+def place_halo(at_right):
+    r, lane = iota((160, 896), 0), iota((160, 896), 1)
+    return ones_where(lane == r + jnp.where(at_right, 672, 0))
 
 
 def taps(weight):
@@ -189,7 +207,7 @@
     shape = (8, 96, 512)
     xo, d, k = iota(shape, 0), iota(shape, 1), iota(shape, 2)
     select = ones_where((d & 31 == (k >> 2) & 31) & (4 * (k >> 7) + (k & 3) == xo + (d >> 5) + 3))
-    banded = jnp.einsum("tod,xdk->toxk", taps(weight), select, preferred_element_type=F32)
+    banded = jnp.einsum("tod,xdk->txok", taps(weight), select, preferred_element_type=F32)
     return banded.astype(BF).reshape(9, 256, 512)
 
 
@@ -198,6 +216,15 @@
     up = [(i, i + 1) for i in range(size - 1)]
     down = [(j, i) for i, j in up]
     return lax.ppermute(array_up, axis, up), lax.ppermute(array_down, axis, down)
+
+
+def swaps(first, second, axis):
+    size = lax.axis_size(axis)
+    received = []
+    for array, start in ((first, 1), (second, 0)):
+        pairs = [(i, i + 1) for i in range(start, size - 1, 2)]
+        received.append(lax.ppermute(array, axis, pairs + [(j, i) for i, j in pairs]))
+    return received
 
 
 def local(volume, w_first, down_weight, w_coarse, w_up, closing_weight):
@@ -216,10 +243,23 @@
             jnp.where(last_y, 3, 99),
         ]
     ).astype(jnp.int32)
-    left, right = both_ways(volume[:, 8:16], volume[:, 0:8], "sx")
-    rows = dot(volume.reshape(512, 256), place(512, 16, 5), TN)
-    rows = rows + dot(left.reshape(256, 256), place(256, 8, -3), TN)
-    rows = (rows + dot(right.reshape(256, 256), place(256, 8, 21), TN)).astype(BF)
+    odd = (ix & 1) == 1
+    flat = volume.reshape(512, 256)
+    payload = dot(chosen_planes(odd), flat, NN).astype(BF)
+    far, near = swaps(payload[:160], payload[160:], "sx")
+    rows = dot(flat, place_own(), TN) + dot(near, place_halo(~odd), TN)
+    prepared = (
+        rows,
+        place_halo(odd),
+        first_banded(w_first),
+        down_weight.reshape(128, 16, 128).transpose(1, 0, 2),
+        closing_banded(closing_weight[:, :, :32]),
+        closing_banded(closing_weight[:, :, 32:]),
+        lax.optimization_barrier(w_up.T).reshape(128, 16, 128).transpose(1, 0, 2),
+    )
+    far, prepared = lax.optimization_barrier((far, prepared))
+    rows, far_place, w1, dwr, skip_weight, up_weight, wupr = prepared
+    rows = (rows + dot(far, far_place, TN)).astype(BF)
     below, above = both_ways(rows[176:256], rows[0:80], "sy")
     skip, coarse = call(
         first_kernel,
@@ -229,31 +269,30 @@
         True,
         2 << 30,
         24,
-    )(
-        bounds,
-        below,
-        rows,
-        above,
-        first_banded(w_first),
-        down_weight.reshape(128, 16, 128).transpose(1, 0, 2),
-    )
-    (part,) = call(skip_kernel, [((2, 256, 256), F32)], [((3, 288, 768), BF)], 2, False, 2 << 30, 16)(
-        skip, closing_banded(closing_weight[:, :, :32])
-    )
+    )(bounds, below, rows, above, w1, dwr)
+    lower, upper = coarse[0:4], coarse[2:6]
+    far, near = swaps(jnp.where(odd, lower, upper), jnp.where(odd, upper, lower), "sx")
+    (part,) = call(skip_kernel, [((2, 256, 256), F32)], [((3, 288, 768), BF)], 2, False, 2 << 30, 16)(skip, skip_weight)
+    coarse = jnp.concatenate([jnp.where(odd, near, far), coarse, jnp.where(odd, far, near)], axis=0)
     before, after = both_ways(coarse[:, 0:4], coarse[:, 2:6], "sy")
-    coarse = jnp.concatenate([before, coarse[:, 0:6], after, jnp.zeros((6, 2, 512), BF)], axis=1)
-    before, after = both_ways(coarse[0:4], coarse[2:6], "sx")
-    coarse = jnp.concatenate([before, coarse, after], axis=0)
-    w_up_rows = lax.optimization_barrier(w_up.T).reshape(128, 16, 128).transpose(1, 0, 2)
+    coarse = jnp.concatenate([before, coarse[:, 0:6], after, jnp.zeros((14, 2, 512), BF)], axis=1)
     (result,) = call(
         last_kernel,
         [((32, 16, 256), BF)],
-        [((3, 224, 512), BF), ((512, 768), F32), ((288, 768), F32), ((3, 288, 768), BF)],
+        [
+            ((3, 224, 512), BF),
+            ((512, 768), F32),
+            ((288, 768), F32),
+            ((3, 288, 768), BF),
+            ((4, 27, 128, 128), BF),
+        ],
         5,
         True,
         3 << 30,
         32,
-    )(bounds, coarse, w_coarse, w_up_rows, closing_banded(closing_weight[:, :, 32:]), part)
+        in_hbm=(1,),
+        semaphores=(pltpu.SemaphoreType.DMA((4,)),),
+    )(bounds, coarse, w_coarse, wupr, up_weight, part)
     return result
 
 

time: 109 us -> 97 us (0.89)
  the two profiles are of different devices: /device:TPU:62 before, /device:TPU:31 now
where the time goes in v2:
time: 97 us; the launch traced here: 96.3 us
  starting transfers between devices  36.9 us (38%)
  local copies, waits for them, and re-layouts  18.3 us (19%)
  waiting for transfers between devices  17.7 us (18%)
  Pallas kernels  17.5 us (18%)
  matrix products  4.92 us (5%)
    ppermute x4, starting transfers between devices, swaps(): lax.ppermute(array, axis, pairs + [(j, i) for i, j in pairs])  26.2 us
    ppermute x4, waiting for transfers between devices, swaps(): lax.ppermute(array, axis, pairs + [(j, i) for i, j in pairs])  11.5 us
    pallas_call x1, Pallas kernels, local(): call(last_kernel, [((32, 16, 256), BF)], [((3, 224, 512), BF), ((512, 768...  10.9 us
    ppermute x2, starting transfers between devices, both_ways(): lax.ppermute(array_up, axis, up)  6.71 us
    ppermute x2, waiting for transfers between devices, both_ways(): lax.ppermute(array_down, axis, down)  5.89 us
    unnamed x17, local copies, waits for them, and re-layouts  5.52 us
    pallas_call x1, Pallas kernels, local(): call(first_kernel, [((384, 768), BF), ((6, 8, 512), BF)], [((3, 416, 896)...  5.07 us
    ppermute x2, starting transfers between devices, both_ways(): lax.ppermute(array_down, axis, down)  4.02 us
  transfers between devices with their start and end apart: 8, of which 4 were waited for; matrix products, arithmetic and copies ran while one was open for 18% of the time, Pallas kernels for 2%

profile of v2, /device:TPU:31, one launch (start us, length us, event | category | flops | bytes accessed | tf_op | source)
XLA Modules:
  0.0 96.3 jit_solution(3439060444985616710)
XLA Ops:
  0.0 0.0 copy-start
  0.0 0.0 copy-start.6
  0.0 0.9 copy-done
  1.0 0.3 convolution_convert_fusion
  1.3 0.7 fusion.55
  2.0 2.4 %collective-permute-start.1 = (bf16[160,256]{1,0:T(8,128)(2,1)}, bf16[160,256]{1,0:T(8,128)(2,1)}, u32[]{:S(2)}, u32[]{:S(2)}) collective-permute-start(bf16[160,256]{1,0:T(8,128)(2,1)} %get-tuple-element.29), channel_id=1, source_target_pairs={{0,16},{32,48},{64,80},{96,112},{128,144},{160,176},{192,208},{224... | collective-permute-start | bytes 245768 | tf_op jit(solution)/shard_map/ppermute | solution.py:226
  4.3 15.8 %collective-permute-start = (bf16[160,256]{1,0:T(8,128)(2,1)}, bf16[160,256]{1,0:T(8,128)(2,1)S(1)}, u32[]{:S(2)}, u32[]{:S(2)}) collective-permute-start(bf16[160,256]{1,0:T(8,128)(2,1)} %get-tuple-element.30), channel_id=1, source_target_pairs={{16,32},{48,64},{80,96},{112,128},{144,160},{176,192},{208,224},{2... | collective-permute-start | bytes 245768 | tf_op jit(solution)/shard_map/ppermute | solution.py:226
  20.3 0.0 copy-done.6
  20.3 0.1 fusion.54
  20.4 0.2 copy.34
  20.6 0.2 reshape.51
  20.7 0.9 convert_bitcast_fusion.1
  21.6 1.6 %copy.19 = bf16[9,8,32,512]{3,2,1,0:T(8,128)(2,1)} copy(bf16[9,8,32,512]{3,2,0,1:T(8,128)(2,1)S(1)} %convert_bitcast_fusion.1) | data formatting | bytes 4718592 | tf_op jit(solution)/shard_map/convert_element_type | solution.py:211
  23.2 0.2 copy.33
  23.4 0.2 reshape.52
  23.5 0.9 convert_bitcast_fusion
  24.4 0.0 copy-start.7
  24.4 0.2 copy.21
  24.6 0.8 copy-done.7
  25.4 0.2 copy.35
  25.5 0.2 reshape.49
  25.7 0.7 convert_bitcast_fusion.2
  26.4 2.1 %copy.16 = bf16[2,9,32,4,384]{4,3,2,1,0:T(4,128)(2,1)} copy(bf16[2,9,32,4,384]{4,2,1,3,0:T(8,128)(2,1)S(1)} %convert_bitcast_fusion.2) | data formatting | bytes 3538944 | tf_op jit(solution)/shard_map/convert_element_type | solution.py:203
  28.5 3.9 %reshape.39.w1 = bf16[2,9,128,384]{3,2,1,0:T(8,128)(2,1)} reshape(bf16[2,9,32,4,384]{4,3,2,1,0:T(4,128)(2,1)} %copy.16) | data formatting | bytes 3538944 | tf_op jit(solution)/shard_map/reshape | solution.py:203
  32.5 0.1 select_convert_fusion.5
  32.6 1.3 %copy.22 = bf16[128,2048]{0,1:T(8,128)(2,1)S(1)} copy(bf16[128,2048]{1,0:T(8,128)(2,1)} %param.10) | data formatting | bytes 1048576 | tf_op args[4]
  33.9 2.3 %copy_bitcast_fusion = (bf16[16,128,128]{2,1,0:T(8,128)(2,1)}, bf16[16,128,128]{2,1,0:T(8,128)(2,1)}) fusion(bf16[128,16,128]{2,1,0:T(8,128)(2,1)S(1)} %bitcast.62, bf16[128,16,128]{2,1,0:T(8,128)(2,1)} %bitcast.69), kind=kLoop, calls=%fused_computation.38 | loop fusion | bytes 2097152 | tf_op jit(solution)/shard_map/transpose | solution.py:258
  36.2 0.6 convolution_bitcast_fusion
  36.8 0.0 collective-permute-done.1
  36.8 1.2 %convolution_add_fusion = f32[256,896]{1,0:T(8,128)S(1)} fusion(f32[256,896]{1,0:T(8,128)S(1)} %convolution_bitcast_fusion, bf16[160,256]{1,0:T(8,128)(2,1)} %collective-permute-done.1, s32[160]{0:T(256)S(1)} %iota_add_fusion.2), kind=kOutput, calls=%fused_computation.7 | convolution fusion | flops 74059776 | bytes 1917568 | tf_op jit(solution)/shard_map/dot_general | solution.py:21
  38.1 0.0 collective-permute-done
  38.1 0.3 fusion.57
  38.4 0.1 add_convert_fusion.middle
  38.5 0.7 fusion.53
  39.2 3.7 %collective-permute-start.2 = (bf16[80,896]{1,0:T(8,128)(2,1)}, bf16[80,896]{1,0:T(8,128)(2,1)S(1)}, u32[]{:S(2)}, u32[]{:S(2)}) collective-permute-start(bf16[80,896]{1,0:T(8,128)(2,1)} %get-tuple-element.26), channel_id=1, source_target_pairs={{0,1},{1,2},{2,3},{3,4},{4,5},{5,6},{6,7},{7,8},{8,9},{9,10},{10,1... | collective-permute-start | bytes 430088 | tf_op jit(solution)/shard_map/ppermute | solution.py:218
  43.0 1.9 %collective-permute-start.3 = (bf16[80,896]{1,0:T(8,128)(2,1)S(1)}, bf16[80,896]{1,0:T(8,128)(2,1)S(1)}, u32[]{:S(2)}, u32[]{:S(2)}) collective-permute-start(bf16[80,896]{1,0:T(8,128)(2,1)S(1)} %get-tuple-element.25), channel_id=1, source_target_pairs={{1,0},{2,1},{3,2},{4,3},{5,4},{6,5},{7,6},{8,7},{9,8},{10,9},{11,1... | collective-permute-start | bytes 430088 | tf_op jit(solution)/shard_map/ppermute | solution.py:218
  44.9 0.1 stack.29.bounds
  45.0 0.0 copy-start.1
  45.0 0.3 collective-permute-done.2.below
  45.3 4.1 %collective-permute-done.3.above = bf16[80,896]{1,0:T(8,128)(2,1)S(1)} collective-permute-done((bf16[80,896]{1,0:T(8,128)(2,1)S(1)}, bf16[80,896]{1,0:T(8,128)(2,1)S(1)}, u32[]{:S(2)}, u32[]{:S(2)}) %collective-permute-start.3) | collective-permute-done | bytes 143392 | tf_op jit(solution)/shard_map/ppermute | solution.py:218
  49.4 0.0 copy-start.2
  49.4 1.5 %copy-done.2 = bf16[2,9,128,384]{3,2,1,0:T(8,128)(2,1)S(1)} copy-done((bf16[2,9,128,384]{3,2,1,0:T(8,128)(2,1)S(1)}, bf16[2,9,128,384]{3,2,1,0:T(8,128)(2,1)}, u32[]{:S(2)}) %copy-start.2) | copy-done | bytes 1769496
  50.9 0.0 copy-start.4
  50.9 1.0 %copy-done.4 = bf16[16,128,128]{2,1,0:T(8,128)(2,1)S(1)} copy-done((bf16[16,128,128]{2,1,0:T(8,128)(2,1)S(1)}, bf16[16,128,128]{2,1,0:T(8,128)(2,1)}, u32[]{:S(2)}) %copy-start.4) | copy-done | bytes 524312
  51.9 5.1 %shard_map.64 = (bf16[384,768]{1,0:T(8,128)(2,1)S(1)}, bf16[6,8,512]{2,1,0:T(8,128)(2,1)S(1)}) custom-call(s32[8]{0:T(128)S(1)} %stack.29.bounds, bf16[80,896]{1,0:T(8,128)(2,1)S(1)} %collective-permute-done.2.below, bf16[256,896]{1,0:T(8,128)(2,1)S(1)} %add_convert_fusion.middle, bf16[80,896]{1,0:T(8,128)(2,1)S(1)} %collective-permute-done.3.above, ...), custom_call_target="tpu_custom_call" | custom-call | flops 2147483648 | bytes 4194304 | tf_op jit(solution)/shard_map/pallas_call | solution.py:264
  57.0 1.9 %collective-permute-start.4 = (bf16[4,8,512]{2,1,0:T(8,128)(2,1)S(1)}, bf16[4,8,512]{2,1,0:T(8,128)(2,1)S(1)}, u32[]{:S(2)}, u32[]{:S(2)}) collective-permute-start(bf16[4,8,512]{2,1,0:T(8,128)(2,1)S(1)} %get-tuple-element.35), channel_id=1, source_target_pairs={{0,16},{32,48},{64,80},{96,112},{128,144},{160,176},{192,208},{224... | collective-permute-start | bytes 98312 | tf_op jit(solution)/shard_map/ppermute | solution.py:226
  58.9 6.0 %collective-permute-start.5 = (bf16[4,8,512]{2,1,0:T(8,128)(2,1)S(1)}, bf16[4,8,512]{2,1,0:T(8,128)(2,1)S(1)}, u32[]{:S(2)}, u32[]{:S(2)}) collective-permute-start(bf16[4,8,512]{2,1,0:T(8,128)(2,1)S(1)} %get-tuple-element.36), channel_id=1, source_target_pairs={{16,32},{48,64},{80,96},{112,128},{144,160},{176,192},{208,224},{2... | collective-permute-start | bytes 98312 | tf_op jit(solution)/shard_map/ppermute | solution.py:226
  65.0 0.1 pad.3.clone
  65.1 0.0 collective-permute-done.4
  65.1 11.5 %collective-permute-done.5 = bf16[4,8,512]{2,1,0:T(8,128)(2,1)S(1)} collective-permute-done((bf16[4,8,512]{2,1,0:T(8,128)(2,1)S(1)}, bf16[4,8,512]{2,1,0:T(8,128)(2,1)S(1)}, u32[]{:S(2)}, u32[]{:S(2)}) %collective-permute-start.5) | collective-permute-done | bytes 32800 | tf_op jit(solution)/shard_map/ppermute | solution.py:226
  76.6 3.0 %collective-permute-start.6 = (bf16[14,4,512]{2,1,0:T(4,128)(2,1)S(1)}, bf16[14,4,512]{2,1,0:T(4,128)(2,1)S(1)}, u32[]{:S(2)}, u32[]{:S(2)}) collective-permute-start(bf16[14,4,512]{2,1,0:T(4,128)(2,1)S(1)} %get-tuple-element.31), channel_id=1, source_target_pairs={{0,1},{1,2},{2,3},{3,4},{4,5},{5,6},{6,7},{7,8},{8,9},{9,10},{10,1... | collective-permute-start | bytes 172040 | tf_op jit(solution)/shard_map/ppermute | solution.py:218
  79.6 2.1 %collective-permute-start.7 = (bf16[14,4,512]{2,1,0:T(4,128)(2,1)S(1)}, bf16[14,4,512]{2,1,0:T(4,128)(2,1)S(1)}, u32[]{:S(2)}, u32[]{:S(2)}) collective-permute-start(bf16[14,4,512]{2,1,0:T(4,128)(2,1)S(1)} %get-tuple-element.32), channel_id=1, source_target_pairs={{1,0},{2,1},{3,2},{4,3},{5,4},{6,5},{7,6},{8,7},{9,8},{10,9},{11,1... | collective-permute-start | bytes 172040 | tf_op jit(solution)/shard_map/ppermute | solution.py:218
  81.7 0.0 copy-done.1
  81.7 0.0 copy-start.3
  81.7 0.0 copy-start.5
  81.7 1.5 %shard_map.65.part_ref = f32[2,256,256]{2,1,0:T(8,128)S(1)} custom-call(bf16[384,768]{1,0:T(8,128)(2,1)S(1)} %get-tuple-element.23.skip_ref, bf16[9,256,512]{2,1,0:T(8,128)(2,1)S(1)} %bitcast.61), custom_call_target="tpu_custom_call" | custom-call | flops 2147483648 | bytes 4194304 | tf_op jit(solution)/shard_map/pallas_call | solution.py:275
  83.2 0.0 collective-permute-done.6
  83.2 1.8 %collective-permute-done.7 = bf16[14,4,512]{2,1,0:T(4,128)(2,1)S(1)} collective-permute-done((bf16[14,4,512]{2,1,0:T(4,128)(2,1)S(1)}, bf16[14,4,512]{2,1,0:T(4,128)(2,1)S(1)}, u32[]{:S(2)}, u32[]{:S(2)}) %collective-permute-start.7) | collective-permute-done | bytes 57376 | tf_op jit(solution)/shard_map/ppermute | solution.py:218
  85.1 0.1 maximum_maximum_fusion.coarse_ref
  85.2 0.0 copy-done.3
  85.2 0.0 copy-done.5
  85.2 10.9 %shard_map.66 = bf16[32,16,256]{2,1,0:T(8,128)(2,1)} custom-call(s32[8]{0:T(128)S(1)} %stack.29.bounds, bf16[14,16,512]{2,1,0:T(8,128)(2,1)S(1)} %maximum_maximum_fusion.coarse_ref, bf16[4,27,128,128]{3,2,1,0:T(8,128)(2,1)S(1)} %copy-done.5, bf16[16,128,128]{2,1,0:T(8,128)(2,1)S(1)} %copy-done.3, bf16[9,256,512]{2,1,0:T(8,128)(2,1)S(1)} %bitcast.60, ...), custom_call_target="tpu_custom_call" | custom-call | flops 3221225472 | bytes 4194304 | tf_op jit(solution)/shard_map/pallas_call | solution.py:279
  (16 shorter events, 0.1 us)
Async XLA Ops:
  0.0 1.0 copy-start
  0.0 20.3 %copy-start.6 = (bf16[27,32,64]{2,1,0:T(8,128)(2,1)S(1)}, bf16[27,32,64]{2,1,0:T(8,128)(2,1)}, u32[]{:S(2)}) copy-start(bf16[27,32,64]{2,1,0:T(8,128)(2,1)} %param.11) | copy-start | bytes 331780
  2.0 34.9 %collective-permute-start.1 = (bf16[160,256]{1,0:T(8,128)(2,1)}, bf16[160,256]{1,0:T(8,128)(2,1)}, u32[]{:S(2)}, u32[]{:S(2)}) collective-permute-start(bf16[160,256]{1,0:T(8,128)(2,1)} %get-tuple-element.29), channel_id=1, source_target_pairs={{0,16},{32,48},{64,80},{96,112},{128,144},{160,176},{192,208},{224... | collective-permute-start | bytes 245768 | tf_op jit(solution)/shard_map/ppermute | solution.py:226
  4.3 33.8 %collective-permute-start = (bf16[160,256]{1,0:T(8,128)(2,1)}, bf16[160,256]{1,0:T(8,128)(2,1)S(1)}, u32[]{:S(2)}, u32[]{:S(2)}) collective-permute-start(bf16[160,256]{1,0:T(8,128)(2,1)} %get-tuple-element.30), channel_id=1, source_target_pairs={{16,32},{48,64},{80,96},{112,128},{144,160},{176,192},{208,224},{2... | collective-permute-start | bytes 245768 | tf_op jit(solution)/shard_map/ppermute | solution.py:226
  24.4 0.9 copy-start.7
  39.2 6.1 %collective-permute-start.2 = (bf16[80,896]{1,0:T(8,128)(2,1)}, bf16[80,896]{1,0:T(8,128)(2,1)S(1)}, u32[]{:S(2)}, u32[]{:S(2)}) collective-permute-start(bf16[80,896]{1,0:T(8,128)(2,1)} %get-tuple-element.26), channel_id=1, source_target_pairs={{0,1},{1,2},{2,3},{3,4},{4,5},{5,6},{6,7},{7,8},{8,9},{9,10},{10,1... | collective-permute-start | bytes 430088 | tf_op jit(solution)/shard_map/ppermute | solution.py:218
  43.0 6.4 %collective-permute-start.3 = (bf16[80,896]{1,0:T(8,128)(2,1)S(1)}, bf16[80,896]{1,0:T(8,128)(2,1)S(1)}, u32[]{:S(2)}, u32[]{:S(2)}) collective-permute-start(bf16[80,896]{1,0:T(8,128)(2,1)S(1)} %get-tuple-element.25), channel_id=1, source_target_pairs={{1,0},{2,1},{3,2},{4,3},{5,4},{6,5},{7,6},{8,7},{9,8},{10,9},{11,1... | collective-permute-start | bytes 430088 | tf_op jit(solution)/shard_map/ppermute | solution.py:218
  45.0 36.7 %copy-start.1 = (bf16[9,8,32,512]{3,2,1,0:T(8,128)(2,1)S(1)}, bf16[9,8,32,512]{3,2,1,0:T(8,128)(2,1)}, u32[]{:S(2)}) copy-start(bf16[9,8,32,512]{3,2,1,0:T(8,128)(2,1)} %copy.19) | copy-start | bytes 7077892
  49.4 1.5 %copy-start.2 = (bf16[2,9,128,384]{3,2,1,0:T(8,128)(2,1)S(1)}, bf16[2,9,128,384]{3,2,1,0:T(8,128)(2,1)}, u32[]{:S(2)}) copy-start(bf16[2,9,128,384]{3,2,1,0:T(8,128)(2,1)} %reshape.39.w1) | copy-start | bytes 5308420
  50.9 1.0 %copy-start.4 = (bf16[16,128,128]{2,1,0:T(8,128)(2,1)S(1)}, bf16[16,128,128]{2,1,0:T(8,128)(2,1)}, u32[]{:S(2)}) copy-start(bf16[16,128,128]{2,1,0:T(8,128)(2,1)} %get-tuple-element.19.dwr) | copy-start | bytes 1572868
  57.0 8.1 %collective-permute-start.4 = (bf16[4,8,512]{2,1,0:T(8,128)(2,1)S(1)}, bf16[4,8,512]{2,1,0:T(8,128)(2,1)S(1)}, u32[]{:S(2)}, u32[]{:S(2)}) collective-permute-start(bf16[4,8,512]{2,1,0:T(8,128)(2,1)S(1)} %get-tuple-element.35), channel_id=1, source_target_pairs={{0,16},{32,48},{64,80},{96,112},{128,144},{160,176},{192,208},{224... | collective-permute-start | bytes 98312 | tf_op jit(solution)/shard_map/ppermute | solution.py:226
  58.9 17.6 %collective-permute-start.5 = (bf16[4,8,512]{2,1,0:T(8,128)(2,1)S(1)}, bf16[4,8,512]{2,1,0:T(8,128)(2,1)S(1)}, u32[]{:S(2)}, u32[]{:S(2)}) collective-permute-start(bf16[4,8,512]{2,1,0:T(8,128)(2,1)S(1)} %get-tuple-element.36), channel_id=1, source_target_pairs={{16,32},{48,64},{80,96},{112,128},{144,160},{176,192},{208,224},{2... | collective-permute-start | bytes 98312 | tf_op jit(solution)/shard_map/ppermute | solution.py:226
  76.6 6.6 %collective-permute-start.6 = (bf16[14,4,512]{2,1,0:T(4,128)(2,1)S(1)}, bf16[14,4,512]{2,1,0:T(4,128)(2,1)S(1)}, u32[]{:S(2)}, u32[]{:S(2)}) collective-permute-start(bf16[14,4,512]{2,1,0:T(4,128)(2,1)S(1)} %get-tuple-element.31), channel_id=1, source_target_pairs={{0,1},{1,2},{2,3},{3,4},{4,5},{5,6},{6,7},{7,8},{8,9},{9,10},{10,1... | collective-permute-start | bytes 172040 | tf_op jit(solution)/shard_map/ppermute | solution.py:218
  79.6 5.5 %collective-permute-start.7 = (bf16[14,4,512]{2,1,0:T(4,128)(2,1)S(1)}, bf16[14,4,512]{2,1,0:T(4,128)(2,1)S(1)}, u32[]{:S(2)}, u32[]{:S(2)}) collective-permute-start(bf16[14,4,512]{2,1,0:T(4,128)(2,1)S(1)} %get-tuple-element.32), channel_id=1, source_target_pairs={{1,0},{2,1},{3,2},{4,3},{5,4},{6,5},{7,6},{8,7},{9,8},{10,9},{11,1... | collective-permute-start | bytes 172040 | tf_op jit(solution)/shard_map/ppermute | solution.py:218
  81.7 3.5 %copy-start.3 = (bf16[16,128,128]{2,1,0:T(8,128)(2,1)S(1)}, bf16[16,128,128]{2,1,0:T(8,128)(2,1)}, u32[]{:S(2)}) copy-start(bf16[16,128,128]{2,1,0:T(8,128)(2,1)} %get-tuple-element.21.wupr) | copy-start | bytes 1572868
  81.7 3.5 %copy-start.5 = (bf16[4,27,128,128]{3,2,1,0:T(8,128)(2,1)S(1)}, bf16[4,27,128,128]{3,2,1,0:T(8,128)(2,1)}, u32[]{:S(2)}) copy-start(bf16[4,27,128,128]{3,2,1,0:T(8,128)(2,1)} %w_hbm.1) | copy-start | bytes 10616836

commit v3 on v2

--- a/solution.py
+++ b/solution.py
@@ -53,9 +53,10 @@
         summed = jnp.zeros((384, 256), F32)
         for oy in range(3):
             for oz in range(3):
-                weight = jnp.concatenate([w1[0, 3 * oy + oz], w1[1, 3 * oy + oz]], axis=0)
-                summed += dot(vz[oz, 16 * oy : 16 * oy + 384, 256 * g : 256 * g + 384], weight, NT)
-        x = 8 * g - 4 + 4 * (lane >> 7) + (lane & 3)
+                summed += dot(
+                    vz[oz, 16 * oy : 16 * oy + 384, 256 * g : 256 * g + 384], w1[3 * oy + oz], NT
+                )
+        x = 8 * g - 4 + (lane >> 5)
         inside = y_inside & (x >= bounds[0]) & (x <= bounds[1])
         skip = jnp.where(inside, jnp.maximum(summed, 0.0), 0.0).astype(BF)
         skip_ref[:, 256 * g : 256 * g + 256] = skip
@@ -99,10 +100,7 @@
         out_ref[g] = closing_sum(weight, scratch, g)
 
 
-def last_kernel(bounds, coarse_ref, w_hbm, wupr, weight, part_ref, out_ref, state, raw, up, scratch, w_coarse, arrived):
-    copies = [pltpu.make_async_copy(w_hbm.at[k], w_coarse.at[k], arrived.at[k]) for k in range(4)]
-    for copy in copies:
-        copy.start()
+def last_kernel(bounds, coarse_ref, w_coarse, wupr, weight, part_ref, out_ref, state, raw, up, scratch):
     value = coarse_ref[...].reshape(224, 512).astype(F32)
     for layer in range(4):
         rows_in = (14 - 2 * layer) * 16
@@ -113,7 +111,6 @@
         low = jnp.zeros((rows, 256), F32)
         high = jnp.zeros((rows, 256), F32)
         zero = jnp.zeros((128, 128), BF)
-        copies[layer].wait()
         for oa in range(3):
             for ob in range(3):
                 w = [w_coarse[layer, 9 * oa + 3 * ob + oz] for oz in range(3)]
@@ -151,17 +148,45 @@
         out_ref[:, 8 * g : 8 * g + 8, :] = dot(to_channels, total, NN).reshape(32, 8, 256).astype(BF)
 
 
+def prepare_kernel(first, closing, down, up, w1, skip_weight, up_weight, dwr, wupr, tall):
+    for source, target, width, shift, channels in (
+        (first, w1, 384, 0, 0),
+        (closing, skip_weight, 512, 3, 0),
+        (closing, up_weight, 512, 3, 32),
+    ):
+        inputs = source.shape[2]
+        repeat = iota((inputs, width), 0) - channels == iota((inputs, width), 1) & 31
+        repeat = jnp.where(repeat, 1.0, 0.0).astype(BF)
+        plane = (iota((32, width), 1) >> 5) - shift
+        for t in range(9):
+            tiled = dot(jnp.concatenate([source[t], source[t + 9], source[t + 18]], axis=0), repeat, NN)
+            for x in range(8):
+                banded = jnp.where(plane == x + 2, tiled[64:], 0.0)
+                banded = jnp.where(plane == x + 1, tiled[32:64], banded)
+                banded = jnp.where(plane == x, tiled[:32], banded)
+                target[t, 32 * x : 32 * x + 32] = banded.astype(BF)
+    for source, target in ((down, dwr), (up, wupr)):
+        if source is down:
+            tall[...] = down[...].astype(F32)
+        else:
+            for k in range(16):
+                tall[128 * k : 128 * k + 128] = up[:, 128 * k : 128 * k + 128].astype(F32).T
+        for i in range(16):
+            for x in range(4):
+                target[i, 32 * x : 32 * x + 32] = tall[pl.ds(16 * x + i, 32, stride=64), :].astype(BF)
+
+
 VMEM = pl.BlockSpec(memory_space=pltpu.VMEM)
 SMEM = pl.BlockSpec(memory_space=pltpu.SMEM)
 
 
-def call(body, shapes, scratch, n_in, scalars, flops, limit, in_hbm=(), semaphores=()):
+def call(body, shapes, scratch, n_in, scalars, flops, limit):
     return pl.pallas_call(
         body,
         out_shape=[jax.ShapeDtypeStruct(s, t) for s, t in shapes],
-        in_specs=([SMEM] if scalars else []) + [pl.BlockSpec(memory_space=pl.ANY) if k in in_hbm else VMEM for k in range(n_in)],
+        in_specs=([SMEM] if scalars else []) + [VMEM] * n_in,
         out_specs=[VMEM] * len(shapes),
-        scratch_shapes=[pltpu.VMEM(s, t) for s, t in scratch] + list(semaphores),
+        scratch_shapes=[pltpu.VMEM(s, t) for s, t in scratch],
         compiler_params=pltpu.CompilerParams(vmem_limit_bytes=limit << 20),
         cost_estimate=pl.CostEstimate(flops=flops, bytes_accessed=4 << 20, transcendentals=0),
     )
@@ -171,12 +196,10 @@
     return jnp.where(condition, 1.0, 0.0).astype(BF)
 
 
-def chosen_planes(odd):
-    row, column = iota((320, 512), 0), iota((320, 512), 1)
-    second = row >= 160
-    inner = jnp.where(second, row - 160, row)
-    plane = (inner >> 5) + jnp.where(second != odd, 11, 0)
-    return ones_where((column >> 4 == inner & 31) & (column & 15 == plane))
+def chosen_planes(upper):
+    row, column = iota((160, 512), 0), iota((160, 512), 1)
+    plane = (row >> 5) + jnp.where(upper, 11, 0)
+    return ones_where((column >> 4 == row & 31) & (column & 15 == plane))
 
 
 def place_own():
@@ -187,28 +210,6 @@
 def place_halo(at_right):
     r, lane = iota((160, 896), 0), iota((160, 896), 1)
     return ones_where(lane == r + jnp.where(at_right, 672, 0))
-
-
-def taps(weight):
-    out, width = weight.shape[1:]
-    return weight.reshape(3, 9, out, width).transpose(1, 2, 0, 3).reshape(9, out, 3 * width)
-
-
-def first_banded(weight):
-    shape = (2, 4, 96, 384)
-    xo = 4 * iota(shape, 0) + iota(shape, 1)
-    d, k = iota(shape, 2), iota(shape, 3)
-    select = ones_where((d & 31 == k & 31) & (k >> 5 == xo + (d >> 5)))
-    banded = jnp.einsum("tod,axdk->atoxk", taps(weight), select, preferred_element_type=F32)
-    return banded.astype(BF).reshape(2, 9, 128, 384)
-
-
-def closing_banded(weight):
-    shape = (8, 96, 512)
-    xo, d, k = iota(shape, 0), iota(shape, 1), iota(shape, 2)
-    select = ones_where((d & 31 == (k >> 2) & 31) & (4 * (k >> 7) + (k & 3) == xo + (d >> 5) + 3))
-    banded = jnp.einsum("tod,xdk->txok", taps(weight), select, preferred_element_type=F32)
-    return banded.astype(BF).reshape(9, 256, 512)
 
 
 def both_ways(array_up, array_down, axis):
@@ -245,20 +246,20 @@
     ).astype(jnp.int32)
     odd = (ix & 1) == 1
     flat = volume.reshape(512, 256)
-    payload = dot(chosen_planes(odd), flat, NN).astype(BF)
-    far, near = swaps(payload[:160], payload[160:], "sx")
+    payload = [dot(chosen_planes(side), flat, NN).astype(BF) for side in (odd, ~odd)]
+    far, near = swaps(*payload, "sx")
     rows = dot(flat, place_own(), TN) + dot(near, place_halo(~odd), TN)
-    prepared = (
-        rows,
-        place_halo(odd),
-        first_banded(w_first),
-        down_weight.reshape(128, 16, 128).transpose(1, 0, 2),
-        closing_banded(closing_weight[:, :, :32]),
-        closing_banded(closing_weight[:, :, 32:]),
-        lax.optimization_barrier(w_up.T).reshape(128, 16, 128).transpose(1, 0, 2),
-    )
-    far, prepared = lax.optimization_barrier((far, prepared))
-    rows, far_place, w1, dwr, skip_weight, up_weight, wupr = prepared
+    weights = call(
+        prepare_kernel,
+        [((9, 256, 384), BF), ((9, 256, 512), BF), ((9, 256, 512), BF), ((16, 128, 128), BF), ((16, 128, 128), BF)],
+        [((2048, 128), F32)],
+        4,
+        False,
+        1 << 28,
+        24,
+    )(w_first, closing_weight, down_weight, w_up)
+    far, rows, far_place, weights = lax.optimization_barrier((far, rows, place_halo(odd), weights))
+    w1, skip_weight, up_weight, dwr, wupr = weights
     rows = (rows + dot(far, far_place, TN)).astype(BF)
     below, above = both_ways(rows[176:256], rows[0:80], "sy")
     skip, coarse = call(
@@ -284,14 +285,11 @@
             ((512, 768), F32),
             ((288, 768), F32),
             ((3, 288, 768), BF),
-            ((4, 27, 128, 128), BF),
         ],
         5,
         True,
         3 << 30,
         32,
-        in_hbm=(1,),
-        semaphores=(pltpu.SemaphoreType.DMA((4,)),),
     )(bounds, coarse, w_coarse, wupr, up_weight, part)
     return result
 

time: 97 us -> 83.6 us (0.86)
  local copies, waits for them, and re-layouts: 18.3 us -> 3.71 us
  waiting for transfers between devices: 17.7 us -> 9.25 us
  starting transfers between devices: 36.9 us -> 44.5 us
  Pallas kernels: 17.5 us -> 19.9 us
    ppermute x4, starting transfers between devices: 26.2 us -> 33.3 us  [swaps(): lax.ppermute(array, axis, pairs + [(j, i) for i, j in pairs])]
    ppermute x4, waiting for transfers between devices: 11.5 us -> 4.87 us  [swaps(): lax.ppermute(array, axis, pairs + [(j, i) for i, j in pairs])]
    reshape x7 -> x0, local copies, waits for them, and re-layouts: 4.87 us -> none  [the longest x1 3.93 us: first_banded(): return banded.astype(BF).reshape(2, 9, 128, 384)]
    pallas_call x0 -> x1, Pallas kernels: none -> 3.91 us  [local(): call(prepare_kernel, [((9, 256, 384), BF), ((9, 256, 512), BF), ((9, 256,...]
    convert_element_type x3 -> x0, local copies, waits for them, and re-layouts: 3.89 us -> none  [the longest x1 2.13 us: first_banded(): return banded.astype(BF).reshape(2, 9, 128, 384)]
    unnamed x17 -> x28, local copies, waits for them, and re-layouts: 5.52 us -> 2.82 us
    dot_general x4 -> x5, matrix products: 2.47 us -> 5.07 us  [dot(): return lax.dot_general(a, b, dims, preferred_element_type=F32)]
    dot_general x3 -> x0, matrix products: 2.46 us -> none  [the longest x2 1.75 us: closing_banded(): jnp.einsum('tod,xdk->txok', taps(weight), select, preferred_element_type=...]
  transfers between devices with their start and end apart: 8 -> 8, of which waited for: 4 -> 3; matrix products, arithmetic and copies ran while one was open for 18% -> 4% of each run, Pallas kernels for 2% -> 7%
where the time goes in v3:
time: 83.6 us; the launch traced here: 83.2 us
  starting transfers between devices  44.5 us (53%)
  Pallas kernels  19.9 us (24%)
  waiting for transfers between devices  9.25 us (11%)
  matrix products  5.07 us (6%)
  local copies, waits for them, and re-layouts  3.71 us (4%)
    ppermute x4, starting transfers between devices, swaps(): lax.ppermute(array, axis, pairs + [(j, i) for i, j in pairs])  33.3 us
    pallas_call x1, Pallas kernels, local(): call(last_kernel, [((32, 16, 256), BF)], [((3, 224, 512), BF), ((512, 768...  9.41 us
    ppermute x2, starting transfers between devices, both_ways(): lax.ppermute(array_up, axis, up)  7.3 us
    dot_general x5, matrix products, dot(): return lax.dot_general(a, b, dims, preferred_element_type=F32)  5.07 us
    pallas_call x1, Pallas kernels, local(): call(first_kernel, [((384, 768), BF), ((6, 8, 512), BF)], [((3, 416, 896)...  5.07 us
    ppermute x4, waiting for transfers between devices, swaps(): lax.ppermute(array, axis, pairs + [(j, i) for i, j in pairs])  4.87 us
    ppermute x2, waiting for transfers between devices, both_ways(): lax.ppermute(array_down, axis, down)  4.06 us
    pallas_call x1, Pallas kernels, local(): call(prepare_kernel, [((9, 256, 384), BF), ((9, 256, 512), BF), ((9, 256,...  3.91 us
  transfers between devices with their start and end apart: 8, of which 3 were waited for; matrix products, arithmetic and copies ran while one was open for 4% of the time, Pallas kernels for 7%

profile of v3, /device:TPU:31, one launch (start us, length us, event | category | flops | bytes accessed | tf_op | source)
XLA Modules:
  0.0 83.2 jit_solution(6881026564839700724)
XLA Ops:
  0.0 0.0 copy-start
  0.0 0.9 %copy-done = bf16[32,16,256]{2,1,0:T(8,128)(2,1)S(1)} copy-done((bf16[32,16,256]{2,1,0:T(8,128)(2,1)S(1)}, bf16[32,16,256]{2,1,0:T(8,128)(2,1)}, u32[]{:S(2)}) %copy-start) | copy-done | bytes 262168
  1.0 0.9 %convolution_convert_fusion.1 = bf16[160,256]{1,0:T(8,128)(2,1)} fusion(bf16[512,256]{1,0:T(8,128)(2,1)S(1)} %bitcast.16, s32[512]{0:T(512)S(1)} %get-tuple-element.43, s32[512]{0:T(512)S(1)} %get-tuple-element.44, s32[160]{0:T(256)S(1)} %fusion.22, s32[160]{0:T(256)S(1)} %iota_and_fusion.2), kind=kOutput, calls=%fused_computation.4 | convolution fusion | flops 42393600 | bytes 349440 | tf_op jit(solution)/shard_map/dot_general | solution.py:21
  1.8 15.0 %collective-permute-start = (bf16[160,256]{1,0:T(8,128)(2,1)}, bf16[160,256]{1,0:T(8,128)(2,1)}, u32[]{:S(2)}, u32[]{:S(2)}) collective-permute-start(bf16[160,256]{1,0:T(8,128)(2,1)} %convolution_convert_fusion.1), channel_id=1, source_target_pairs={{16,32},{48,64},{80,96},{112,128},{144,160},{176,192},{208,224},{2... | collective-permute-start | bytes 245768 | tf_op jit(solution)/shard_map/ppermute | solution.py:227
  16.9 0.9 %convolution_convert_fusion = bf16[160,256]{1,0:T(8,128)(2,1)} fusion(bf16[512,256]{1,0:T(8,128)(2,1)S(1)} %bitcast.18, s32[512]{0:T(512)S(1)} %get-tuple-element.43, s32[512]{0:T(512)S(1)} %get-tuple-element.44, s32[160]{0:T(256)S(1)} %fusion.21, s32[160]{0:T(256)S(1)} %iota_and_fusion.2), kind=kOutput, calls=%fused_computation.3 | convolution fusion | flops 42393600 | bytes 349440 | tf_op jit(solution)/shard_map/dot_general | solution.py:21
  17.8 0.0 copy-start.1
  17.8 0.0 copy-start.2
  17.8 0.0 copy-start.3
  17.8 0.0 copy-start.4
  17.8 2.1 %collective-permute-start.1 = (bf16[160,256]{1,0:T(8,128)(2,1)}, bf16[160,256]{1,0:T(8,128)(2,1)}, u32[]{:S(2)}, u32[]{:S(2)}) collective-permute-start(bf16[160,256]{1,0:T(8,128)(2,1)} %convolution_convert_fusion), channel_id=1, source_target_pairs={{0,16},{32,48},{64,80},{96,112},{128,144},{160,176},{192,208},{224... | collective-permute-start | bytes 245768 | tf_op jit(solution)/shard_map/ppermute | solution.py:227
  19.9 0.1 select_convert_fusion.2
  20.0 0.6 convolution_bitcast_fusion
  20.6 0.0 copy-done.1
  20.6 0.0 copy-done.2
  20.6 0.0 copy-done.3
  20.6 0.0 copy-done.4
  20.6 3.9 %shard_map.64 = (bf16[9,256,384]{2,1,0:T(8,128)(2,1)S(1)}, bf16[9,256,512]{2,1,0:T(8,128)(2,1)S(1)}, bf16[9,256,512]{2,1,0:T(8,128)(2,1)S(1)}, bf16[16,128,128]{...) custom-call(bf16[27,32,32]{2,1,0:T(8,128)(2,1)S(1)} %copy-done.3, bf16[27,32,64]{2,1,0:T(8,128)(2,1)S(1)} %copy-done.4, ...), custom_call_target="tpu_custom_call" | custom-call | flops 268435456 | bytes 4194304 | tf_op jit(solution)/shard_map/pallas_call | solution.py:252
  24.5 0.0 copy-start.12
  24.5 0.8 copy-done.12
  25.3 0.0 copy-start.6
  25.3 0.0 copy-start.8
  25.3 0.0 copy-start.10
  25.3 0.0 collective-permute-done.1
  25.4 1.4 %convolution_add_fusion = f32[256,896]{1,0:T(8,128)S(1)} fusion(f32[256,896]{1,0:T(8,128)S(1)} %convolution_bitcast_fusion, bf16[160,256]{1,0:T(8,128)(2,1)} %collective-permute-done.1, s32[160]{0:T(256)S(1)} %iota_add_fusion.1), kind=kOutput, calls=%fused_computation.1 | convolution fusion | flops 74059776 | bytes 1917568 | tf_op jit(solution)/shard_map/dot_general | solution.py:21
  26.7 0.0 collective-permute-done
  26.7 0.0 copy-start.13
  26.7 1.4 %fusion.33 = f32[256,896]{1,0:T(8,128)S(1)} fusion(bf16[160,256]{1,0:T(8,128)(2,1)} %collective-permute-done, bf16[160,896]{1,0:T(8,128)(2,1)S(1)} %select_convert_fusion.2), kind=kOutput, calls=%fused_computation.62 | convolution fusion | flops 73400320 | bytes 1286144 | tf_op jit(solution)/shard_map/dot_general | solution.py:21
  28.1 0.1 add_convert_fusion.middle
  28.2 0.0 copy-done.6
  28.2 0.0 copy-done.8
  28.2 0.0 copy-done.10
  28.2 0.7 fusion.31
  28.9 3.5 %collective-permute-start.2 = (bf16[80,896]{1,0:T(8,128)(2,1)}, bf16[80,896]{1,0:T(8,128)(2,1)S(1)}, u32[]{:S(2)}, u32[]{:S(2)}) collective-permute-start(bf16[80,896]{1,0:T(8,128)(2,1)} %get-tuple-element.36), channel_id=1, source_target_pairs={{0,1},{1,2},{2,3},{3,4},{4,5},{5,6},{6,7},{7,8},{8,9},{9,10},{10,1... | collective-permute-start | bytes 430088 | tf_op jit(solution)/shard_map/ppermute | solution.py:219
  32.4 1.9 %collective-permute-start.3 = (bf16[80,896]{1,0:T(8,128)(2,1)S(1)}, bf16[80,896]{1,0:T(8,128)(2,1)S(1)}, u32[]{:S(2)}, u32[]{:S(2)}) collective-permute-start(bf16[80,896]{1,0:T(8,128)(2,1)S(1)} %get-tuple-element.35), channel_id=1, source_target_pairs={{1,0},{2,1},{3,2},{4,3},{5,4},{6,5},{7,6},{8,7},{9,8},{10,9},{11,1... | collective-permute-start | bytes 430088 | tf_op jit(solution)/shard_map/ppermute | solution.py:219
  34.4 0.1 stack.29.bounds
  34.4 0.0 copy-start.9
  34.4 0.3 collective-permute-done.2.below
  34.8 4.1 %collective-permute-done.3.above = bf16[80,896]{1,0:T(8,128)(2,1)S(1)} collective-permute-done((bf16[80,896]{1,0:T(8,128)(2,1)S(1)}, bf16[80,896]{1,0:T(8,128)(2,1)S(1)}, u32[]{:S(2)}, u32[]{:S(2)}) %collective-permute-start.3) | collective-permute-done | bytes 143392 | tf_op jit(solution)/shard_map/ppermute | solution.py:219
  38.8 0.0 copy-done.13
  38.8 5.1 %shard_map.65 = (bf16[384,768]{1,0:T(8,128)(2,1)S(1)}, bf16[6,8,512]{2,1,0:T(8,128)(2,1)S(1)}) custom-call(s32[8]{0:T(128)S(1)} %stack.29.bounds, bf16[80,896]{1,0:T(8,128)(2,1)S(1)} %collective-permute-done.2.below, bf16[256,896]{1,0:T(8,128)(2,1)S(1)} %add_convert_fusion.middle, bf16[80,896]{1,0:T(8,128)(2,1)S(1)} %collective-permute-done.3.above, ...), custom_call_target="tpu_custom_call" | custom-call | flops 2147483648 | bytes 4194304 | tf_op jit(solution)/shard_map/pallas_call | solution.py:265
  43.9 3.6 %collective-permute-start.4 = (bf16[4,8,512]{2,1,0:T(8,128)(2,1)S(1)}, bf16[4,8,512]{2,1,0:T(8,128)(2,1)S(1)}, u32[]{:S(2)}, u32[]{:S(2)}) collective-permute-start(bf16[4,8,512]{2,1,0:T(8,128)(2,1)S(1)} %get-tuple-element.41), channel_id=1, source_target_pairs={{0,16},{32,48},{64,80},{96,112},{128,144},{160,176},{192,208},{224... | collective-permute-start | bytes 98312 | tf_op jit(solution)/shard_map/ppermute | solution.py:227
  47.6 12.6 %collective-permute-start.5 = (bf16[4,8,512]{2,1,0:T(8,128)(2,1)S(1)}, bf16[4,8,512]{2,1,0:T(8,128)(2,1)S(1)}, u32[]{:S(2)}, u32[]{:S(2)}) collective-permute-start(bf16[4,8,512]{2,1,0:T(8,128)(2,1)S(1)} %get-tuple-element.42), channel_id=1, source_target_pairs={{16,32},{48,64},{80,96},{112,128},{144,160},{176,192},{208,224},{2... | collective-permute-start | bytes 98312 | tf_op jit(solution)/shard_map/ppermute | solution.py:227
  60.2 0.1 pad.3.clone
  60.3 0.0 collective-permute-done.4
  60.3 4.9 %collective-permute-done.5 = bf16[4,8,512]{2,1,0:T(8,128)(2,1)S(1)} collective-permute-done((bf16[4,8,512]{2,1,0:T(8,128)(2,1)S(1)}, bf16[4,8,512]{2,1,0:T(8,128)(2,1)S(1)}, u32[]{:S(2)}, u32[]{:S(2)}) %collective-permute-start.5) | collective-permute-done | bytes 32800 | tf_op jit(solution)/shard_map/ppermute | solution.py:227
  65.2 1.9 %collective-permute-start.7 = (bf16[14,4,512]{2,1,0:T(4,128)(2,1)S(1)}, bf16[14,4,512]{2,1,0:T(4,128)(2,1)S(1)}, u32[]{:S(2)}, u32[]{:S(2)}) collective-permute-start(bf16[14,4,512]{2,1,0:T(4,128)(2,1)S(1)} %get-tuple-element.38), channel_id=1, source_target_pairs={{1,0},{2,1},{3,2},{4,3},{5,4},{6,5},{7,6},{8,7},{9,8},{10,9},{11,1... | collective-permute-start | bytes 172040 | tf_op jit(solution)/shard_map/ppermute | solution.py:219
  67.2 3.8 %collective-permute-start.6 = (bf16[14,4,512]{2,1,0:T(4,128)(2,1)S(1)}, bf16[14,4,512]{2,1,0:T(4,128)(2,1)S(1)}, u32[]{:S(2)}, u32[]{:S(2)}) collective-permute-start(bf16[14,4,512]{2,1,0:T(4,128)(2,1)S(1)} %get-tuple-element.37), channel_id=1, source_target_pairs={{0,1},{1,2},{2,3},{3,4},{4,5},{5,6},{6,7},{7,8},{8,9},{9,10},{10,1... | collective-permute-start | bytes 172040 | tf_op jit(solution)/shard_map/ppermute | solution.py:219
  71.0 0.0 copy-done.9
  71.0 0.0 copy-start.5
  71.0 0.0 copy-start.7
  71.0 0.0 copy-start.11
  71.0 1.5 %shard_map.66.part_ref = f32[2,256,256]{2,1,0:T(8,128)S(1)} custom-call(bf16[384,768]{1,0:T(8,128)(2,1)S(1)} %get-tuple-element.33.skip_ref, bf16[9,256,512]{2,1,0:T(8,128)(2,1)S(1)} %copy-done.9), custom_call_target="tpu_custom_call" | custom-call | flops 2147483648 | bytes 4194304 | tf_op jit(solution)/shard_map/pallas_call | solution.py:276
  72.6 0.0 collective-permute-done.7
  72.6 0.0 collective-permute-done.6
  72.6 0.1 maximum_maximum_fusion.coarse_ref
  72.7 0.3 copy-done.5
  73.0 0.7 copy-done.7
  73.8 0.1 copy-done.11
  73.8 9.4 %shard_map.67 = bf16[32,16,256]{2,1,0:T(8,128)(2,1)} custom-call(s32[8]{0:T(128)S(1)} %stack.29.bounds, bf16[14,16,512]{2,1,0:T(8,128)(2,1)S(1)} %maximum_maximum_fusion.coarse_ref, bf16[4,27,128,128]{3,2,1,0:T(8,128)(2,1)S(1)} %copy-done.5, bf16[16,128,128]{2,1,0:T(8,128)(2,1)S(1)} %copy-done.11, bf16[9,256,512]{2,1,0:T(8,128)(2,1)S(1)} %copy-done.7, ...), custom_call_target="tpu_custom_call" | custom-call | flops 3221225472 | bytes 4194304 | tf_op jit(solution)/shard_map/pallas_call | solution.py:280
  (13 shorter events, 0.1 us)
Async XLA Ops:
  0.0 1.0 %copy-start = (bf16[32,16,256]{2,1,0:T(8,128)(2,1)S(1)}, bf16[32,16,256]{2,1,0:T(8,128)(2,1)}, u32[]{:S(2)}) copy-start(bf16[32,16,256]{2,1,0:T(8,128)(2,1)} %param.6) | copy-start | bytes 786436
  1.8 24.9 %collective-permute-start = (bf16[160,256]{1,0:T(8,128)(2,1)}, bf16[160,256]{1,0:T(8,128)(2,1)}, u32[]{:S(2)}, u32[]{:S(2)}) collective-permute-start(bf16[160,256]{1,0:T(8,128)(2,1)} %convolution_convert_fusion.1), channel_id=1, source_target_pairs={{16,32},{48,64},{80,96},{112,128},{144,160},{176,192},{208,224},{2... | collective-permute-start | bytes 245768 | tf_op jit(solution)/shard_map/ppermute | solution.py:227
  17.8 2.8 %copy-start.1 = (bf16[2048,128]{1,0:T(8,128)(2,1)S(1)}, bf16[2048,128]{1,0:T(8,128)(2,1)}, u32[]{:S(2)}) copy-start(bf16[2048,128]{1,0:T(8,128)(2,1)} %down.1) | copy-start | bytes 1572868
  17.8 2.8 %copy-start.2 = (bf16[128,2048]{1,0:T(8,128)(2,1)S(1)}, bf16[128,2048]{1,0:T(8,128)(2,1)}, u32[]{:S(2)}) copy-start(bf16[128,2048]{1,0:T(8,128)(2,1)} %up.1) | copy-start | bytes 1572868
  17.8 2.8 %copy-start.3 = (bf16[27,32,32]{2,1,0:T(8,128)(2,1)S(1)}, bf16[27,32,32]{2,1,0:T(8,128)(2,1)}, u32[]{:S(2)}) copy-start(bf16[27,32,32]{2,1,0:T(8,128)(2,1)} %first.1) | copy-start | bytes 165892
  17.8 2.8 %copy-start.4 = (bf16[27,32,64]{2,1,0:T(8,128)(2,1)S(1)}, bf16[27,32,64]{2,1,0:T(8,128)(2,1)}, u32[]{:S(2)}) copy-start(bf16[27,32,64]{2,1,0:T(8,128)(2,1)} %closing.1) | copy-start | bytes 331780
  17.8 7.6 %collective-permute-start.1 = (bf16[160,256]{1,0:T(8,128)(2,1)}, bf16[160,256]{1,0:T(8,128)(2,1)}, u32[]{:S(2)}, u32[]{:S(2)}) collective-permute-start(bf16[160,256]{1,0:T(8,128)(2,1)} %convolution_convert_fusion), channel_id=1, source_target_pairs={{0,16},{32,48},{64,80},{96,112},{128,144},{160,176},{192,208},{224... | collective-permute-start | bytes 245768 | tf_op jit(solution)/shard_map/ppermute | solution.py:227
  24.5 0.8 copy-start.12
  25.3 2.9 %copy-start.6 = (bf16[9,256,512]{2,1,0:T(8,128)(2,1)}, bf16[9,256,512]{2,1,0:T(8,128)(2,1)S(1)}, u32[]{:S(2)}) copy-start(bf16[9,256,512]{2,1,0:T(8,128)(2,1)S(1)} %get-tuple-element.32.weight) | copy-start | bytes 7077892
  25.3 2.9 %copy-start.8 = (bf16[9,256,512]{2,1,0:T(8,128)(2,1)}, bf16[9,256,512]{2,1,0:T(8,128)(2,1)S(1)}, u32[]{:S(2)}) copy-start(bf16[9,256,512]{2,1,0:T(8,128)(2,1)S(1)} %get-tuple-element.34.weight) | copy-start | bytes 7077892
  25.3 2.9 %copy-start.10 = (bf16[16,128,128]{2,1,0:T(8,128)(2,1)}, bf16[16,128,128]{2,1,0:T(8,128)(2,1)S(1)}, u32[]{:S(2)}) copy-start(bf16[16,128,128]{2,1,0:T(8,128)(2,1)S(1)} %get-tuple-element.31.wupr) | copy-start | bytes 1572868
  26.7 12.1 %copy-start.13 = (bf16[16,128,128]{2,1,0:T(8,128)(2,1)S(1)}, bf16[16,128,128]{2,1,0:T(8,128)(2,1)}, u32[]{:S(2)}) copy-start(bf16[16,128,128]{2,1,0:T(8,128)(2,1)} %copy-done.12) | copy-start | bytes 1572868
  28.9 5.8 %collective-permute-start.2 = (bf16[80,896]{1,0:T(8,128)(2,1)}, bf16[80,896]{1,0:T(8,128)(2,1)S(1)}, u32[]{:S(2)}, u32[]{:S(2)}) collective-permute-start(bf16[80,896]{1,0:T(8,128)(2,1)} %get-tuple-element.36), channel_id=1, source_target_pairs={{0,1},{1,2},{2,3},{3,4},{4,5},{5,6},{6,7},{7,8},{8,9},{9,10},{10,1... | collective-permute-start | bytes 430088 | tf_op jit(solution)/shard_map/ppermute | solution.py:219
  32.4 6.4 %collective-permute-start.3 = (bf16[80,896]{1,0:T(8,128)(2,1)S(1)}, bf16[80,896]{1,0:T(8,128)(2,1)S(1)}, u32[]{:S(2)}, u32[]{:S(2)}) collective-permute-start(bf16[80,896]{1,0:T(8,128)(2,1)S(1)} %get-tuple-element.35), channel_id=1, source_target_pairs={{1,0},{2,1},{3,2},{4,3},{5,4},{6,5},{7,6},{8,7},{9,8},{10,9},{11,1... | collective-permute-start | bytes 430088 | tf_op jit(solution)/shard_map/ppermute | solution.py:219
  34.4 36.6 %copy-start.9 = (bf16[9,256,512]{2,1,0:T(8,128)(2,1)S(1)}, bf16[9,256,512]{2,1,0:T(8,128)(2,1)}, u32[]{:S(2)}) copy-start(bf16[9,256,512]{2,1,0:T(8,128)(2,1)} %copy-done.8) | copy-start | bytes 7077892
  43.9 16.4 %collective-permute-start.4 = (bf16[4,8,512]{2,1,0:T(8,128)(2,1)S(1)}, bf16[4,8,512]{2,1,0:T(8,128)(2,1)S(1)}, u32[]{:S(2)}, u32[]{:S(2)}) collective-permute-start(bf16[4,8,512]{2,1,0:T(8,128)(2,1)S(1)} %get-tuple-element.41), channel_id=1, source_target_pairs={{0,16},{32,48},{64,80},{96,112},{128,144},{160,176},{192,208},{224... | collective-permute-start | bytes 98312 | tf_op jit(solution)/shard_map/ppermute | solution.py:227
  47.6 17.6 %collective-permute-start.5 = (bf16[4,8,512]{2,1,0:T(8,128)(2,1)S(1)}, bf16[4,8,512]{2,1,0:T(8,128)(2,1)S(1)}, u32[]{:S(2)}, u32[]{:S(2)}) collective-permute-start(bf16[4,8,512]{2,1,0:T(8,128)(2,1)S(1)} %get-tuple-element.42), channel_id=1, source_target_pairs={{16,32},{48,64},{80,96},{112,128},{144,160},{176,192},{208,224},{2... | collective-permute-start | bytes 98312 | tf_op jit(solution)/shard_map/ppermute | solution.py:227
  65.2 7.3 %collective-permute-start.7 = (bf16[14,4,512]{2,1,0:T(4,128)(2,1)S(1)}, bf16[14,4,512]{2,1,0:T(4,128)(2,1)S(1)}, u32[]{:S(2)}, u32[]{:S(2)}) collective-permute-start(bf16[14,4,512]{2,1,0:T(4,128)(2,1)S(1)} %get-tuple-element.38), channel_id=1, source_target_pairs={{1,0},{2,1},{3,2},{4,3},{5,4},{6,5},{7,6},{8,7},{9,8},{10,9},{11,1... | collective-permute-start | bytes 172040 | tf_op jit(solution)/shard_map/ppermute | solution.py:219
  67.2 5.4 %collective-permute-start.6 = (bf16[14,4,512]{2,1,0:T(4,128)(2,1)S(1)}, bf16[14,4,512]{2,1,0:T(4,128)(2,1)S(1)}, u32[]{:S(2)}, u32[]{:S(2)}) collective-permute-start(bf16[14,4,512]{2,1,0:T(4,128)(2,1)S(1)} %get-tuple-element.37), channel_id=1, source_target_pairs={{0,1},{1,2},{2,3},{3,4},{4,5},{5,6},{6,7},{7,8},{8,9},{9,10},{10,1... | collective-permute-start | bytes 172040 | tf_op jit(solution)/shard_map/ppermute | solution.py:219
  71.0 2.0 %copy-start.5 = (bf16[4,27,128,128]{3,2,1,0:T(8,128)(2,1)S(1)}, bf16[4,27,128,128]{3,2,1,0:T(8,128)(2,1)}, u32[]{:S(2)}) copy-start(bf16[4,27,128,128]{3,2,1,0:T(8,128)(2,1)} %w_coarse.1) | copy-start | bytes 10616836
  71.0 2.7 %copy-start.7 = (bf16[9,256,512]{2,1,0:T(8,128)(2,1)S(1)}, bf16[9,256,512]{2,1,0:T(8,128)(2,1)}, u32[]{:S(2)}) copy-start(bf16[9,256,512]{2,1,0:T(8,128)(2,1)} %copy-done.6) | copy-start | bytes 7077892
  71.0 2.8 %copy-start.11 = (bf16[16,128,128]{2,1,0:T(8,128)(2,1)S(1)}, bf16[16,128,128]{2,1,0:T(8,128)(2,1)}, u32[]{:S(2)}) copy-start(bf16[16,128,128]{2,1,0:T(8,128)(2,1)} %copy-done.10) | copy-start | bytes 1572868

commit v4 on v1

--- a/solution.py
+++ b/solution.py
@@ -37,33 +37,38 @@
     return jnp.where(fine == (y - first) * NZ + z, 1.0, 0.0).astype(BF)
 
 
-def first_kernel(bounds, below, middle, above, w1, dwr, skip_ref, c0_ref, vz, grouped):
-    for tile in range(7):
-        lanes = slice(128 * tile, 128 * tile + 128)
-        value = jnp.concatenate(
-            [below[:, lanes].astype(F32), middle[:, lanes].astype(F32), above[:, lanes].astype(F32)], axis=0
-        )
-        for k, shifted in enumerate(z_shifts(value, 416)):
-            vz[k, :, lanes] = shifted.astype(BF)
+def side_window(own, halo, halo_at_left, lanes):
+    tile = lanes.start // 128
+    other = slice(128 * (tile ^ 2), 128 * (tile ^ 2) + 128)
+    here = slice(128 * (tile & 1), 128 * (tile & 1) + 128)
+    outer, inner = halo[:, here].astype(F32), own[:, other].astype(F32)
+    return jnp.where(halo_at_left, outer, inner) if tile < 2 else jnp.where(halo_at_left, inner, outer)
+
+
+def fine_groups(windows, bounds, w1, dwr, skip_refs, coarse_refs, vz, grouped):
     to_groups = regroup(512, 384, 0, 0)
     y = (iota((384, 256), 0) >> 4) - 4
-    lane = iota((384, 256), 1)
+    plane = iota((384, 256), 1) >> 5
     y_inside = (y >= bounds[2]) & (y <= bounds[3])
-    for g in range(3):
+    for k, (window, first_x) in enumerate(windows):
+        for tile in range(4):
+            lanes = slice(128 * tile, 128 * tile + 128)
+            for oz, shifted in enumerate(z_shifts(window(lanes), 416)):
+                vz[oz, :, lanes] = shifted.astype(BF)
         summed = jnp.zeros((384, 256), F32)
         for oy in range(3):
             for oz in range(3):
-                weight = jnp.concatenate([w1[0, 3 * oy + oz], w1[1, 3 * oy + oz]], axis=0)
-                summed += dot(vz[oz, 16 * oy : 16 * oy + 384, 256 * g : 256 * g + 384], weight, NT)
-        x = 8 * g - 4 + 4 * (lane >> 7) + (lane & 3)
+                summed += dot(vz[oz, 16 * oy : 16 * oy + 384], w1[3 * oy + oz], NT)
+        x = plane + first_x
         inside = y_inside & (x >= bounds[0]) & (x <= bounds[1])
         skip = jnp.where(inside, jnp.maximum(summed, 0.0), 0.0).astype(BF)
-        skip_ref[:, 256 * g : 256 * g + 256] = skip
-        grouped[:, 256 * g : 256 * g + 256] = dot(to_groups, skip, NN).astype(BF)
-    coarse = jnp.zeros((192, 128), F32)
+        skip_refs[k][...] = skip
+        grouped[:, 256 * k : 256 * k + 256] = dot(to_groups, skip, NN).astype(BF)
+    count = 2 * len(windows)
+    coarse = jnp.zeros((32 * count, 128), F32)
     for i in range(0, 16, 2):
         pieces = []
-        for a in range(6):
+        for a in range(count):
             lanes = slice(128 * a, 128 * a + 128)
             pieces.append(
                 jnp.concatenate([grouped[32 * i : 32 * i + 32, lanes], grouped[32 * i + 32 : 32 * i + 64, lanes]], axis=1)
@@ -71,12 +76,32 @@
         coarse += dot(
             jnp.concatenate(pieces, axis=0), jnp.concatenate([dwr[i], dwr[i + 1]], axis=0), NN
         )
-    for a in range(6):
-        for z in range(4):
-            c0_ref[a, :, 128 * z : 128 * z + 128] = coarse[32 * a + 8 * z : 32 * a + 8 * z + 8].astype(BF)
-
-
-def closing_sum(values, weight, scratch, g):
+    for a in range(count):
+        for target, first_a in coarse_refs[a // 2]:
+            for z in range(4):
+                cell = coarse[32 * a + 8 * z : 32 * a + 8 * z + 8].astype(BF)
+                target[first_a + a % 2, :, 128 * z : 128 * z + 128] = cell
+
+
+def near_kernel(bounds, own, near, w1, dwr, skip_near, skip_own, to_far, coarse_own, vz, grouped):
+    odd = bounds[8] == 1
+    first_near, first_own = 2 - 2 * bounds[8], 2 * bounds[8]
+    windows = (
+        (lambda lanes: side_window(own, near, odd, lanes), jnp.where(odd, -4, 12)),
+        (lambda lanes: own[:, lanes].astype(F32), 4),
+    )
+    coarse = ([(to_far, first_near)], [(to_far, first_own), (coarse_own, 0)])
+    fine_groups(windows, bounds, w1, dwr, (skip_near, skip_own), coarse, vz, grouped)
+
+
+def far_kernel(bounds, own, far, w1, dwr, coarse_own, skip_far, to_near, vz, grouped):
+    to_near[pl.ds(2 - 2 * bounds[8], 2)] = coarse_own[...]
+    even = bounds[8] == 0
+    windows = ((lambda lanes: side_window(own, far, even, lanes), jnp.where(even, -4, 12)),)
+    fine_groups(windows, bounds, w1, dwr, (skip_far,), ([(to_near, 2 * bounds[8])],), vz, grouped)
+
+
+def closing_sum(weight, scratch, g):
     summed = jnp.zeros((256, 256), F32)
     for oy in range(3):
         for oz in range(3):
@@ -93,10 +118,20 @@
             scratch[k, :, lanes] = shifted.astype(BF)
 
 
-def skip_kernel(skip_ref, weight, out_ref, scratch):
-    fill_shifts(lambda lanes: skip_ref[48:336, lanes].astype(F32), scratch)
+def skip_kernel(bounds, near, own, far, weight, out_ref, scratch):
+    odd = bounds[8] == 1
+
+    def value_of(lanes):
+        group, half = divmod(lanes.start // 128, 2)
+        here = slice(128 * half, 128 * half + 128)
+        if group == 1:
+            return own[48:336, here].astype(F32)
+        first, second = near[48:336, here].astype(F32), far[48:336, here].astype(F32)
+        return jnp.where(odd, first, second) if group == 0 else jnp.where(odd, second, first)
+
+    fill_shifts(value_of, scratch)
     for g in range(2):
-        out_ref[g] = closing_sum(None, weight, scratch, g)
+        out_ref[g] = closing_sum(weight, scratch, g)
 
 
 def last_kernel(bounds, coarse_ref, w_coarse, wupr, weight, part_ref, out_ref, state, raw, up, scratch):
@@ -140,9 +175,45 @@
     for g in range(3):
         up[:, 256 * g : 256 * g + 256] = dot(from_groups, raw[:, 256 * g : 256 * g + 256].astype(BF), NN)
     fill_shifts(lambda lanes: up[:, lanes], scratch)
+    row, column = iota((256, 256), 0), iota((256, 256), 1)
+    to_channels = jnp.where(column == ((row & 7) << 5) + (row >> 3), 1.0, 0.0).astype(BF)
     for g in range(2):
-        total = closing_sum(None, weight, scratch, g) + part_ref[g]
-        out_ref[:, 8 * g : 8 * g + 8, :] = total.reshape(32, 8, 256).astype(BF)
+        total = (closing_sum(weight, scratch, g) + part_ref[g]).astype(BF)
+        out_ref[:, 8 * g : 8 * g + 8, :] = dot(to_channels, total, NN).reshape(32, 8, 256).astype(BF)
+
+
+def banded(source, target, channels):
+    inputs = source.shape[2]
+    repeat = iota((inputs, 512), 0) - channels == iota((inputs, 512), 1) & 31
+    repeat = jnp.where(repeat, 1.0, 0.0).astype(BF)
+    plane = (iota((32, 512), 1) >> 5) - 3
+    for t in range(9):
+        tiled = dot(jnp.concatenate([source[t], source[t + 9], source[t + 18]], axis=0), repeat, NN)
+        for x in range(8):
+            rows = jnp.where(plane == x + 2, tiled[64:], 0.0)
+            rows = jnp.where(plane == x + 1, tiled[32:64], rows)
+            rows = jnp.where(plane == x, tiled[:32], rows)
+            target[t, 32 * x : 32 * x + 32] = rows.astype(BF)
+
+
+def by_offset(tall, target):
+    for i in range(16):
+        for x in range(4):
+            target[i, 32 * x : 32 * x + 32] = tall[pl.ds(16 * x + i, 32, stride=64), :].astype(BF)
+
+
+def prepare_first_kernel(first, down, w1, dwr, tall):
+    banded(first, w1, 0)
+    tall[...] = down[...].astype(F32)
+    by_offset(tall, dwr)
+
+
+def prepare_last_kernel(closing, up, skip_weight, up_weight, wupr, tall):
+    banded(closing, skip_weight, 0)
+    banded(closing, up_weight, 32)
+    for k in range(16):
+        tall[128 * k : 128 * k + 128] = up[:, 128 * k : 128 * k + 128].astype(F32).T
+    by_offset(tall, wupr)
 
 
 VMEM = pl.BlockSpec(memory_space=pltpu.VMEM)
@@ -158,7 +229,6 @@
         scratch_shapes=[pltpu.VMEM(s, t) for s, t in scratch],
         compiler_params=pltpu.CompilerParams(vmem_limit_bytes=limit << 20),
         cost_estimate=pl.CostEstimate(flops=flops, bytes_accessed=4 << 20, transcendentals=0),
-        name=body.__name__,
     )
 
 
@@ -166,31 +236,9 @@
     return jnp.where(condition, 1.0, 0.0).astype(BF)
 
 
-def place(rows, planes, shift):
-    r, lane = iota((rows, 896), 0), iota((rows, 896), 1)
-    return ones_where((lane & 31 == r // planes) & (lane >> 5 == r % planes + shift))
-
-
-def taps(weight):
-    out, width = weight.shape[1:]
-    return weight.reshape(3, 9, out, width).transpose(1, 2, 0, 3).reshape(9, out, 3 * width)
-
-
-def first_banded(weight):
-    shape = (2, 4, 96, 384)
-    xo = 4 * iota(shape, 0) + iota(shape, 1)
-    d, k = iota(shape, 2), iota(shape, 3)
-    select = ones_where((d & 31 == k & 31) & (k >> 5 == xo + (d >> 5)))
-    banded = jnp.einsum("tod,axdk->atoxk", taps(weight), select, preferred_element_type=F32)
-    return banded.astype(BF).reshape(2, 9, 128, 384)
-
-
-def closing_banded(weight):
-    shape = (8, 96, 512)
-    xo, d, k = iota(shape, 0), iota(shape, 1), iota(shape, 2)
-    select = ones_where((d & 31 == (k >> 2) & 31) & (4 * (k >> 7) + (k & 3) == xo + (d >> 5) + 3))
-    banded = jnp.einsum("tod,xdk->toxk", taps(weight), select, preferred_element_type=F32)
-    return banded.astype(BF).reshape(9, 256, 512)
+def place_own():
+    r, lane = iota((512, 512), 0), iota((512, 512), 1)
+    return ones_where((lane & 31 == r >> 4) & (lane >> 5 == r & 15))
 
 
 def both_ways(array_up, array_down, axis):
@@ -198,6 +246,15 @@
     up = [(i, i + 1) for i in range(size - 1)]
     down = [(j, i) for i, j in up]
     return lax.ppermute(array_up, axis, up), lax.ppermute(array_down, axis, down)
+
+
+def swap(array, axis, start):
+    pairs = [(i, i + 1) for i in range(start, lax.axis_size(axis) - 1, 2)]
+    return lax.ppermute(array, axis, pairs + [(j, i) for i, j in pairs])
+
+
+def swaps(first, second, axis):
+    return swap(first, axis, 1), swap(second, axis, 0)
 
 
 def local(volume, w_first, down_weight, w_coarse, w_up, closing_weight):
@@ -214,46 +271,64 @@
             jnp.where(last_x, 3, 99),
             jnp.where(first_y, 0, -99),
             jnp.where(last_y, 3, 99),
+            ix & 1,
         ]
     ).astype(jnp.int32)
-    left, right = both_ways(volume[:, 8:16], volume[:, 0:8], "sx")
-    rows = dot(volume.reshape(512, 256), place(512, 16, 5), TN)
-    rows = rows + dot(left.reshape(256, 256), place(256, 8, -3), TN)
-    rows = (rows + dot(right.reshape(256, 256), place(256, 8, 21), TN)).astype(BF)
-    below, above = both_ways(rows[176:256], rows[0:80], "sy")
-    skip, coarse = call(
-        first_kernel,
-        [((384, 768), BF), ((6, 8, 512), BF)],
-        [((3, 416, 896), BF), ((512, 768), BF)],
-        5,
+    odd = (ix & 1) == 1
+    own = dot(volume.reshape(512, 256), place_own(), TN).astype(BF)
+    below, above = both_ways(own[176:256], own[0:80], "sy")
+    own = jnp.concatenate([below, own, above], axis=0)
+    left, right = own[:, :256], own[:, 256:]
+    far, near = swaps(jnp.where(odd, right, left), jnp.where(odd, left, right), "sx")
+    w1, dwr = call(
+        prepare_first_kernel, [((9, 256, 512), BF), ((16, 128, 128), BF)], [((2048, 128), F32)], 2, False, 1 << 27, 12
+    )(w_first, down_weight)
+    skip, cells = ((384, 256), BF), ((4, 8, 512), BF)
+    skip_near, skip_own, to_far, coarse_own = call(
+        near_kernel,
+        [skip, skip, cells, ((2, 8, 512), BF)],
+        [((3, 416, 512), BF), ((512, 512), BF)],
+        4,
         True,
         2 << 30,
         24,
-    )(
-        bounds,
-        below,
-        rows,
-        above,
-        first_banded(w_first),
-        down_weight.reshape(128, 16, 128).transpose(1, 0, 2),
+    )(bounds, own, near, w1, dwr)
+    far_cells = swap(to_far, "sx", 1)
+    skip_far, to_near = call(
+        far_kernel, [skip, cells], [((3, 416, 512), BF), ((512, 256), BF)], 5, True, 1 << 30, 24
+    )(bounds, own, far, w1, dwr, coarse_own)
+    near_cells = swap(to_near, "sx", 0)
+    skip_weight, up_weight, wupr = call(
+        prepare_last_kernel,
+        [((9, 256, 512), BF), ((9, 256, 512), BF), ((16, 128, 128), BF)],
+        [((2048, 128), F32)],
+        2,
+        False,
+        1 << 28,
+        16,
+    )(closing_weight, w_up)
+    (part,) = call(skip_kernel, [((2, 256, 256), F32)], [((3, 288, 768), BF)], 4, True, 2 << 30, 16)(
+        bounds, skip_near, skip_own, skip_far, skip_weight
     )
-    (part,) = call(skip_kernel, [((2, 256, 256), F32)], [((3, 288, 768), BF)], 2, False, 2 << 30, 16)(
-        skip, closing_banded(closing_weight[:, :, :32])
-    )
+    odd_order = jnp.concatenate([near_cells, to_far[:2], to_near, far_cells], axis=0)
+    even_order = jnp.concatenate([far_cells, to_near, to_far[2:], near_cells], axis=0)
+    coarse = jnp.where(odd, odd_order, even_order)
     before, after = both_ways(coarse[:, 0:4], coarse[:, 2:6], "sy")
-    coarse = jnp.concatenate([before, coarse[:, 0:6], after, jnp.zeros((6, 2, 512), BF)], axis=1)
-    before, after = both_ways(coarse[0:4], coarse[2:6], "sx")
-    coarse = jnp.concatenate([before, coarse, after], axis=0)
-    w_up_rows = lax.optimization_barrier(w_up.T).reshape(128, 16, 128).transpose(1, 0, 2)
+    coarse = jnp.concatenate([before, coarse[:, 0:6], after, jnp.zeros((14, 2, 512), BF)], axis=1)
     (result,) = call(
         last_kernel,
         [((32, 16, 256), BF)],
-        [((3, 224, 512), BF), ((512, 768), F32), ((288, 768), F32), ((3, 288, 768), BF)],
+        [
+            ((3, 224, 512), BF),
+            ((512, 768), F32),
+            ((288, 768), F32),
+            ((3, 288, 768), BF),
+        ],
         5,
         True,
         3 << 30,
         32,
-    )(bounds, coarse, w_coarse, w_up_rows, closing_banded(closing_weight[:, :, 32:]), part)
+    )(bounds, coarse, w_coarse, wupr, up_weight, part)
     return result
 
 

time: 109 us -> 93.9 us (0.86)
  the two profiles are of different devices: /device:TPU:62 before, /device:TPU:417 now
where the time goes in v4:
time: 93.9 us; the launch traced here: 93.6 us
  starting transfers between devices  46.5 us (50%)
  Pallas kernels  23.4 us (25%)
  waiting for transfers between devices  21.6 us (23%)
  local copies, waits for them, and re-layouts  1.17 us (1%)
    ppermute x4, starting transfers between devices, swap(): return lax.ppermute(array, axis, pairs + [(j, i) for i, j in pairs])  23.6 us
    ppermute x2, starting transfers between devices, both_ways(): lax.ppermute(array_up, axis, up)  18.9 us
    ppermute x4, waiting for transfers between devices, swap(): return lax.ppermute(array, axis, pairs + [(j, i) for i, j in pairs])  16.4 us
    pallas_call x1, Pallas kernels, local(): call(last_kernel, [((32, 16, 256), BF)], [((3, 224, 512), BF), ((512, 768...  9.42 us
    pallas_call x1, Pallas kernels, local(): call(near_kernel, [skip, skip, cells, ((2, 8, 512), BF)], [((3, 416, 512)...  5.39 us
    ppermute x2, waiting for transfers between devices, both_ways(): lax.ppermute(array_down, axis, down)  5.12 us
    ppermute x2, starting transfers between devices, both_ways(): lax.ppermute(array_down, axis, down)  4.02 us
    pallas_call x1, Pallas kernels, local(): call(far_kernel, [skip, cells], [((3, 416, 512), BF), ((512, 256), BF)],...  2.53 us
  transfers between devices with their start and end apart: 8, of which 4 were waited for; matrix products, arithmetic and copies ran while one was open for 0% of the time, Pallas kernels for 12%

profile of v4, /device:TPU:417, one launch (start us, length us, event | category | flops | bytes accessed | tf_op | source)
XLA Modules:
  0.0 93.6 jit_solution(11364233929507389725)
XLA Ops:
  0.0 0.0 copy-start
  0.0 0.0 copy-start.4
  0.0 0.0 copy-start.5
  0.0 0.9 copy-done
  1.0 0.0 copy-start.1
  1.0 0.0 copy-start.2
  1.0 0.5 fusion
  1.5 3.2 %collective-permute-start = (bf16[80,512]{1,0:T(8,128)(2,1)S(1)}, bf16[80,512]{1,0:T(8,128)(2,1)S(1)}, u32[]{:S(2)}, u32[]{:S(2)}) collective-permute-start(bf16[80,512]{1,0:T(8,128)(2,1)S(1)} %get-tuple-element.29), channel_id=1, source_target_pairs={{0,1},{1,2},{2,3},{3,4},{4,5},{5,6},{6,7},{7,8},{8,9},{9,10},{10,1... | collective-permute-start | bytes 245768 | tf_op jit(solution)/shard_map/ppermute | solution.py:248
  4.7 1.9 %collective-permute-start.1 = (bf16[80,512]{1,0:T(8,128)(2,1)S(1)}, bf16[80,512]{1,0:T(8,128)(2,1)S(1)}, u32[]{:S(2)}, u32[]{:S(2)}) collective-permute-start(bf16[80,512]{1,0:T(8,128)(2,1)S(1)} %get-tuple-element.30), channel_id=1, source_target_pairs={{1,0},{2,1},{3,2},{4,3},{5,4},{6,5},{7,6},{8,7},{9,8},{10,9},{11,1... | collective-permute-start | bytes 245768 | tf_op jit(solution)/shard_map/ppermute | solution.py:248
  6.6 0.0 collective-permute-done
  6.6 3.8 %collective-permute-done.1 = bf16[80,512]{1,0:T(8,128)(2,1)S(1)} collective-permute-done((bf16[80,512]{1,0:T(8,128)(2,1)S(1)}, bf16[80,512]{1,0:T(8,128)(2,1)S(1)}, u32[]{:S(2)}, u32[]{:S(2)}) %collective-permute-start.1) | collective-permute-done | bytes 81952 | tf_op jit(solution)/shard_map/ppermute | solution.py:248
  10.5 3.2 %collective-permute-start.3 = (bf16[416,256]{1,0:T(8,128)(2,1)S(1)}, bf16[416,256]{1,0:T(8,128)(2,1)S(1)}, u32[]{:S(2)}, u32[]{:S(2)}) collective-permute-start(bf16[416,256]{1,0:T(8,128)(2,1)S(1)} %get-tuple-element.28), channel_id=1, source_target_pairs={{0,16},{32,48},{64,80},{96,112},{128,144},{160,176},{192,208},{224... | collective-permute-start | bytes 638984 | tf_op jit(solution)/shard_map/ppermute | solution.py:253
  13.8 0.1 pad.3.clone
  13.9 0.1 stack.33.bounds
  13.9 0.0 copy-done.4
  13.9 0.0 copy-done.5
  14.0 2.4 %shard_map.67 = (bf16[9,256,512]{2,1,0:T(8,128)(2,1)S(1)}, bf16[9,256,512]{2,1,0:T(8,128)(2,1)S(1)}, bf16[16,128,128]{2,1,0:T(8,128)(2,1)S(1)}) custom-call(bf16[27,32,64]{2,1,0:T(8,128)(2,1)S(1)} %copy-done.5, bf16[128,2048]{1,0:T(8,128)(2,1)S(1)} %copy-done.4), custom_call_target="tpu_custom_call" | custom-call | flops 268435456 | bytes 4194304 | tf_op jit(solution)/shard_map/pallas_call | solution.py:301
  16.4 9.0 %collective-permute-start.2 = (bf16[416,256]{1,0:T(8,128)(2,1)S(1)}, bf16[416,256]{1,0:T(8,128)(2,1)S(1)}, u32[]{:S(2)}, u32[]{:S(2)}) collective-permute-start(bf16[416,256]{1,0:T(8,128)(2,1)S(1)} %get-tuple-element.27), channel_id=1, source_target_pairs={{16,32},{48,64},{80,96},{112,128},{144,160},{176,192},{208,224},{2... | collective-permute-start | bytes 638984 | tf_op jit(solution)/shard_map/ppermute | solution.py:253
  25.3 0.0 copy-done.1
  25.4 0.0 copy-done.2
  25.4 1.6 %shard_map.64 = (bf16[9,256,512]{2,1,0:T(8,128)(2,1)S(1)}, bf16[16,128,128]{2,1,0:T(8,128)(2,1)S(1)}) custom-call(bf16[27,32,32]{2,1,0:T(8,128)(2,1)S(1)} %copy-done.2, bf16[2048,128]{1,0:T(8,128)(2,1)S(1)} %copy-done.1), custom_call_target="tpu_custom_call" | custom-call | flops 134217728 | bytes 4194304 | tf_op jit(solution)/shard_map/pallas_call | solution.py:283
  26.9 0.0 collective-permute-done.3.near
  26.9 5.4 %shard_map.65 = (bf16[384,256]{1,0:T(8,128)(2,1)S(1)}, bf16[384,256]{1,0:T(8,128)(2,1)S(1)}, bf16[4,8,512]{2,1,0:T(8,128)(2,1)S(1)}, bf16[2,8,512]{2,1,0:T(8,128)(2,1)S(1)}) custom-call(s32[9]{0:T(128)S(1)} %stack.33.bounds, bf16[416,512]{1,0:T(8,128)(2,1)S(1)} %pad_maximum_fusion.own, bf16[416,256]{1,0:T(8,128)(2,1)S(1)} %collective-permute-done.3.near, ...), custom_call_target="tpu_custom_call" | custom-call | flops 2147483648 | bytes 4194304 | tf_op jit(solution)/shard_map/pallas_call | solution.py:287
  32.3 8.4 %collective-permute-done.2.far = bf16[416,256]{1,0:T(8,128)(2,1)S(1)} collective-permute-done((bf16[416,256]{1,0:T(8,128)(2,1)S(1)}, bf16[416,256]{1,0:T(8,128)(2,1)S(1)}, u32[]{:S(2)}, u32[]{:S(2)}) %collective-permute-start.2) | collective-permute-done | bytes 213024 | tf_op jit(solution)/shard_map/ppermute | solution.py:253
  40.7 2.5 %shard_map.66 = (bf16[384,256]{1,0:T(8,128)(2,1)S(1)}, bf16[4,8,512]{2,1,0:T(8,128)(2,1)S(1)}) custom-call(s32[9]{0:T(128)S(1)} %stack.33.bounds, bf16[416,512]{1,0:T(8,128)(2,1)S(1)} %pad_maximum_fusion.own, bf16[416,256]{1,0:T(8,128)(2,1)S(1)} %collective-permute-done.2.far, bf16[9,256,512]{2,1,0:T(8,128)(2,1)S(1)} %get-tuple-element.16.w1, ...), custom_call_target="tpu_custom_call" | custom-call | flops 1073741824 | bytes 4194304 | tf_op jit(solution)/shard_map/pallas_call | solution.py:297
  43.2 1.9 %collective-permute-start.4 = (bf16[4,8,512]{2,1,0:T(8,128)(2,1)S(1)}, bf16[4,8,512]{2,1,0:T(8,128)(2,1)S(1)}, u32[]{:S(2)}, u32[]{:S(2)}) collective-permute-start(bf16[4,8,512]{2,1,0:T(8,128)(2,1)S(1)} %get-tuple-element.19), channel_id=1, source_target_pairs={{0,16},{32,48},{64,80},{96,112},{128,144},{160,176},{192,208},{224... | collective-permute-start | bytes 98312 | tf_op jit(solution)/shard_map/ppermute | solution.py:253
  45.2 9.5 %collective-permute-start.5 = (bf16[4,8,512]{2,1,0:T(8,128)(2,1)S(1)}, bf16[4,8,512]{2,1,0:T(8,128)(2,1)S(1)}, u32[]{:S(2)}, u32[]{:S(2)}) collective-permute-start(bf16[4,8,512]{2,1,0:T(8,128)(2,1)S(1)} %get-tuple-element.20), channel_id=1, source_target_pairs={{16,32},{48,64},{80,96},{112,128},{144,160},{176,192},{208,224},{2... | collective-permute-start | bytes 98312 | tf_op jit(solution)/shard_map/ppermute | solution.py:253
  54.7 0.0 collective-permute-done.4
  54.7 8.1 %collective-permute-done.5 = bf16[4,8,512]{2,1,0:T(8,128)(2,1)S(1)} collective-permute-done((bf16[4,8,512]{2,1,0:T(8,128)(2,1)S(1)}, bf16[4,8,512]{2,1,0:T(8,128)(2,1)S(1)}, u32[]{:S(2)}, u32[]{:S(2)}) %collective-permute-start.5) | collective-permute-done | bytes 32800 | tf_op jit(solution)/shard_map/ppermute | solution.py:253
  62.8 15.7 %collective-permute-start.6 = (bf16[14,4,512]{2,1,0:T(4,128)(2,1)S(1)}, bf16[14,4,512]{2,1,0:T(4,128)(2,1)S(1)}, u32[]{:S(2)}, u32[]{:S(2)}) collective-permute-start(bf16[14,4,512]{2,1,0:T(4,128)(2,1)S(1)} %get-tuple-element.31), channel_id=1, source_target_pairs={{0,1},{1,2},{2,3},{3,4},{4,5},{5,6},{6,7},{7,8},{8,9},{9,10},{10,1... | collective-permute-start | bytes 172040 | tf_op jit(solution)/shard_map/ppermute | solution.py:248
  78.5 2.1 %collective-permute-start.7 = (bf16[14,4,512]{2,1,0:T(4,128)(2,1)S(1)}, bf16[14,4,512]{2,1,0:T(4,128)(2,1)S(1)}, u32[]{:S(2)}, u32[]{:S(2)}) collective-permute-start(bf16[14,4,512]{2,1,0:T(4,128)(2,1)S(1)} %get-tuple-element.32), channel_id=1, source_target_pairs={{1,0},{2,1},{3,2},{4,3},{5,4},{6,5},{7,6},{8,7},{9,8},{10,9},{11,1... | collective-permute-start | bytes 172040 | tf_op jit(solution)/shard_map/ppermute | solution.py:248
  80.6 0.0 copy-start.3
  80.6 2.1 %shard_map.68.part_ref = f32[2,256,256]{2,1,0:T(8,128)S(1)} custom-call(s32[9]{0:T(128)S(1)} %stack.33.bounds, bf16[384,256]{1,0:T(8,128)(2,1)S(1)} %get-tuple-element.23.near, bf16[384,256]{1,0:T(8,128)(2,1)S(1)} %get-tuple-element.24.own, bf16[384,256]{1,0:T(8,128)(2,1)S(1)} %get-tuple-element.25.far, bf16[9,256,512]{2,1,0:T(8,128)(2,1)S(1)} %get-tuple-element.26.weight), custom_call_target="tpu_custom_call" | custom-call | flops 2147483648 | bytes 4194304 | tf_op jit(solution)/shard_map/pallas_call | solution.py:310
  82.7 0.0 collective-permute-done.6
  82.7 1.3 %collective-permute-done.7 = bf16[14,4,512]{2,1,0:T(4,128)(2,1)S(1)} collective-permute-done((bf16[14,4,512]{2,1,0:T(4,128)(2,1)S(1)}, bf16[14,4,512]{2,1,0:T(4,128)(2,1)S(1)}, u32[]{:S(2)}, u32[]{:S(2)}) %collective-permute-start.7) | collective-permute-done | bytes 57376 | tf_op jit(solution)/shard_map/ppermute | solution.py:248
  84.0 0.1 maximum_maximum_fusion.coarse_ref
  84.1 0.0 copy-done.3
  84.1 9.4 %shard_map.69 = bf16[32,16,256]{2,1,0:T(8,128)(2,1)} custom-call(s32[9]{0:T(128)S(1)} %stack.33.bounds, bf16[14,16,512]{2,1,0:T(8,128)(2,1)S(1)} %maximum_maximum_fusion.coarse_ref, bf16[4,27,128,128]{3,2,1,0:T(8,128)(2,1)S(1)} %copy-done.3, bf16[16,128,128]{2,1,0:T(8,128)(2,1)S(1)} %get-tuple-element.21.wupr, ...), custom_call_target="tpu_custom_call" | custom-call | flops 3221225472 | bytes 4194304 | tf_op jit(solution)/shard_map/pallas_call | solution.py:318
  (9 shorter events, 0.2 us)
Async XLA Ops:
  0.0 1.0 %copy-start = (bf16[32,16,256]{2,1,0:T(8,128)(2,1)S(1)}, bf16[32,16,256]{2,1,0:T(8,128)(2,1)}, u32[]{:S(2)}) copy-start(bf16[32,16,256]{2,1,0:T(8,128)(2,1)} %param.6) | copy-start | bytes 786436
  0.0 13.9 %copy-start.4 = (bf16[128,2048]{1,0:T(8,128)(2,1)S(1)}, bf16[128,2048]{1,0:T(8,128)(2,1)}, u32[]{:S(2)}) copy-start(bf16[128,2048]{1,0:T(8,128)(2,1)} %up.1) | copy-start | bytes 1572868
  0.0 13.9 %copy-start.5 = (bf16[27,32,64]{2,1,0:T(8,128)(2,1)S(1)}, bf16[27,32,64]{2,1,0:T(8,128)(2,1)}, u32[]{:S(2)}) copy-start(bf16[27,32,64]{2,1,0:T(8,128)(2,1)} %closing.1) | copy-start | bytes 331780
  1.0 24.4 %copy-start.1 = (bf16[2048,128]{1,0:T(8,128)(2,1)S(1)}, bf16[2048,128]{1,0:T(8,128)(2,1)}, u32[]{:S(2)}) copy-start(bf16[2048,128]{1,0:T(8,128)(2,1)} %down.1) | copy-start | bytes 1572868
  1.0 24.4 %copy-start.2 = (bf16[27,32,32]{2,1,0:T(8,128)(2,1)S(1)}, bf16[27,32,32]{2,1,0:T(8,128)(2,1)}, u32[]{:S(2)}) copy-start(bf16[27,32,32]{2,1,0:T(8,128)(2,1)} %first.1) | copy-start | bytes 165892
  1.5 5.2 %collective-permute-start = (bf16[80,512]{1,0:T(8,128)(2,1)S(1)}, bf16[80,512]{1,0:T(8,128)(2,1)S(1)}, u32[]{:S(2)}, u32[]{:S(2)}) collective-permute-start(bf16[80,512]{1,0:T(8,128)(2,1)S(1)} %get-tuple-element.29), channel_id=1, source_target_pairs={{0,1},{1,2},{2,3},{3,4},{4,5},{5,6},{6,7},{7,8},{8,9},{9,10},{10,1... | collective-permute-start | bytes 245768 | tf_op jit(solution)/shard_map/ppermute | solution.py:248
  4.7 5.8 %collective-permute-start.1 = (bf16[80,512]{1,0:T(8,128)(2,1)S(1)}, bf16[80,512]{1,0:T(8,128)(2,1)S(1)}, u32[]{:S(2)}, u32[]{:S(2)}) collective-permute-start(bf16[80,512]{1,0:T(8,128)(2,1)S(1)} %get-tuple-element.30), channel_id=1, source_target_pairs={{1,0},{2,1},{3,2},{4,3},{5,4},{6,5},{7,6},{8,7},{9,8},{10,9},{11,1... | collective-permute-start | bytes 245768 | tf_op jit(solution)/shard_map/ppermute | solution.py:248
  10.5 16.4 %collective-permute-start.3 = (bf16[416,256]{1,0:T(8,128)(2,1)S(1)}, bf16[416,256]{1,0:T(8,128)(2,1)S(1)}, u32[]{:S(2)}, u32[]{:S(2)}) collective-permute-start(bf16[416,256]{1,0:T(8,128)(2,1)S(1)} %get-tuple-element.28), channel_id=1, source_target_pairs={{0,16},{32,48},{64,80},{96,112},{128,144},{160,176},{192,208},{224... | collective-permute-start | bytes 638984 | tf_op jit(solution)/shard_map/ppermute | solution.py:253
  16.4 24.3 %collective-permute-start.2 = (bf16[416,256]{1,0:T(8,128)(2,1)S(1)}, bf16[416,256]{1,0:T(8,128)(2,1)S(1)}, u32[]{:S(2)}, u32[]{:S(2)}) collective-permute-start(bf16[416,256]{1,0:T(8,128)(2,1)S(1)} %get-tuple-element.27), channel_id=1, source_target_pairs={{16,32},{48,64},{80,96},{112,128},{144,160},{176,192},{208,224},{2... | collective-permute-start | bytes 638984 | tf_op jit(solution)/shard_map/ppermute | solution.py:253
  43.2 11.4 %collective-permute-start.4 = (bf16[4,8,512]{2,1,0:T(8,128)(2,1)S(1)}, bf16[4,8,512]{2,1,0:T(8,128)(2,1)S(1)}, u32[]{:S(2)}, u32[]{:S(2)}) collective-permute-start(bf16[4,8,512]{2,1,0:T(8,128)(2,1)S(1)} %get-tuple-element.19), channel_id=1, source_target_pairs={{0,16},{32,48},{64,80},{96,112},{128,144},{160,176},{192,208},{224... | collective-permute-start | bytes 98312 | tf_op jit(solution)/shard_map/ppermute | solution.py:253
  45.2 17.6 %collective-permute-start.5 = (bf16[4,8,512]{2,1,0:T(8,128)(2,1)S(1)}, bf16[4,8,512]{2,1,0:T(8,128)(2,1)S(1)}, u32[]{:S(2)}, u32[]{:S(2)}) collective-permute-start(bf16[4,8,512]{2,1,0:T(8,128)(2,1)S(1)} %get-tuple-element.20), channel_id=1, source_target_pairs={{16,32},{48,64},{80,96},{112,128},{144,160},{176,192},{208,224},{2... | collective-permute-start | bytes 98312 | tf_op jit(solution)/shard_map/ppermute | solution.py:253
  62.8 19.8 %collective-permute-start.6 = (bf16[14,4,512]{2,1,0:T(4,128)(2,1)S(1)}, bf16[14,4,512]{2,1,0:T(4,128)(2,1)S(1)}, u32[]{:S(2)}, u32[]{:S(2)}) collective-permute-start(bf16[14,4,512]{2,1,0:T(4,128)(2,1)S(1)} %get-tuple-element.31), channel_id=1, source_target_pairs={{0,1},{1,2},{2,3},{3,4},{4,5},{5,6},{6,7},{7,8},{8,9},{9,10},{10,1... | collective-permute-start | bytes 172040 | tf_op jit(solution)/shard_map/ppermute | solution.py:248
  78.5 5.5 %collective-permute-start.7 = (bf16[14,4,512]{2,1,0:T(4,128)(2,1)S(1)}, bf16[14,4,512]{2,1,0:T(4,128)(2,1)S(1)}, u32[]{:S(2)}, u32[]{:S(2)}) collective-permute-start(bf16[14,4,512]{2,1,0:T(4,128)(2,1)S(1)} %get-tuple-element.32), channel_id=1, source_target_pairs={{1,0},{2,1},{3,2},{4,3},{5,4},{6,5},{7,6},{8,7},{9,8},{10,9},{11,1... | collective-permute-start | bytes 172040 | tf_op jit(solution)/shard_map/ppermute | solution.py:248
  80.6 3.5 %copy-start.3 = (bf16[4,27,128,128]{3,2,1,0:T(8,128)(2,1)S(1)}, bf16[4,27,128,128]{3,2,1,0:T(8,128)(2,1)}, u32[]{:S(2)}) copy-start(bf16[4,27,128,128]{3,2,1,0:T(8,128)(2,1)} %w_coarse.1) | copy-start | bytes 10616836

commit v5 on v4

--- a/solution.py
+++ b/solution.py
@@ -241,20 +241,15 @@
     return ones_where((lane & 31 == r >> 4) & (lane >> 5 == r & 15))
 
 
-def both_ways(array_up, array_down, axis):
-    size = lax.axis_size(axis)
-    up = [(i, i + 1) for i in range(size - 1)]
-    down = [(j, i) for i, j in up]
-    return lax.ppermute(array_up, axis, up), lax.ppermute(array_down, axis, down)
-
-
 def swap(array, axis, start):
     pairs = [(i, i + 1) for i in range(start, lax.axis_size(axis) - 1, 2)]
     return lax.ppermute(array, axis, pairs + [(j, i) for i, j in pairs])
 
 
-def swaps(first, second, axis):
-    return swap(first, axis, 1), swap(second, axis, 0)
+def y_neighbours(bottom, top, odd_y):
+    chips = swap(jnp.where(odd_y, top, bottom), "sy", 1)
+    cores = swap(jnp.where(odd_y, bottom, top), "sy", 0)
+    return jnp.where(odd_y, cores, chips), jnp.where(odd_y, chips, cores)
 
 
 def local(volume, w_first, down_weight, w_coarse, w_up, closing_weight):
@@ -276,10 +271,12 @@
     ).astype(jnp.int32)
     odd = (ix & 1) == 1
     own = dot(volume.reshape(512, 256), place_own(), TN).astype(BF)
-    below, above = both_ways(own[176:256], own[0:80], "sy")
+    odd_y = (iy & 1) == 1
+    below, above = y_neighbours(own[0:80], own[176:256], odd_y)
     own = jnp.concatenate([below, own, above], axis=0)
     left, right = own[:, :256], own[:, 256:]
-    far, near = swaps(jnp.where(odd, right, left), jnp.where(odd, left, right), "sx")
+    near = swap(jnp.where(odd, left, right), "sx", 0)
+    far = swap(jnp.where(odd, right, left), "sx", 1)
     w1, dwr = call(
         prepare_first_kernel, [((9, 256, 512), BF), ((16, 128, 128), BF)], [((2048, 128), F32)], 2, False, 1 << 27, 12
     )(w_first, down_weight)
@@ -313,7 +310,7 @@
     odd_order = jnp.concatenate([near_cells, to_far[:2], to_near, far_cells], axis=0)
     even_order = jnp.concatenate([far_cells, to_near, to_far[2:], near_cells], axis=0)
     coarse = jnp.where(odd, odd_order, even_order)
-    before, after = both_ways(coarse[:, 0:4], coarse[:, 2:6], "sy")
+    before, after = y_neighbours(coarse[:, 2:6], coarse[:, 0:4], odd_y)
     coarse = jnp.concatenate([before, coarse[:, 0:6], after, jnp.zeros((14, 2, 512), BF)], axis=1)
     (result,) = call(
         last_kernel,

time: 93.9 us -> 92.7 us (0.987)
  the two profiles are of different devices: /device:TPU:417 before, /device:TPU:449 now
where the time goes in v5:
time: 92.7 us; the launch traced here: 92.4 us
  waiting for transfers between devices  37.6 us (41%)
  starting transfers between devices  29.2 us (31%)
  Pallas kernels  23.4 us (25%)
  local copies, waits for them, and re-layouts  1.1 us (1%)
    ppermute x8, waiting for transfers between devices, swap(): return lax.ppermute(array, axis, pairs + [(j, i) for i, j in pairs])  37.6 us
    ppermute x8, starting transfers between devices, swap(): return lax.ppermute(array, axis, pairs + [(j, i) for i, j in pairs])  29.2 us
    pallas_call x1, Pallas kernels, local(): call(last_kernel, [((32, 16, 256), BF)], [((3, 224, 512), BF), ((512, 768...  9.42 us
    pallas_call x1, Pallas kernels, local(): call(near_kernel, [skip, skip, cells, ((2, 8, 512), BF)], [((3, 416, 512)...  5.39 us
    pallas_call x1, Pallas kernels, local(): call(far_kernel, [skip, cells], [((3, 416, 512), BF), ((512, 256), BF)],...  2.53 us
    pallas_call x1, Pallas kernels, local(): call(prepare_last_kernel, [((9, 256, 512), BF), ((9, 256, 512), BF), ((16...  2.4 us
    pallas_call x1, Pallas kernels, local(): call(skip_kernel, [((2, 256, 256), F32)], [((3, 288, 768), BF)], 4, True,...  2.05 us
  transfers between devices with their start and end apart: 8, of which 4 were waited for; matrix products, arithmetic and copies ran while one was open for 0% of the time, Pallas kernels for 12%

profile of v5, /device:TPU:449, one launch (start us, length us, event | category | flops | bytes accessed | tf_op | source)
XLA Modules:
  0.0 92.4 jit_solution(16379404160296217618)
XLA Ops:
  0.0 0.0 copy-start
  0.0 0.0 copy-start.4
  0.0 0.0 copy-start.5
  0.0 0.9 copy-done
  1.0 0.0 copy-start.1
  1.0 0.0 copy-start.2
  1.0 0.5 fusion
  1.5 2.6 %collective-permute-start = (bf16[80,512]{1,0:T(8,128)(2,1)S(1)}, bf16[80,512]{1,0:T(8,128)(2,1)S(1)}, u32[]{:S(2)}, u32[]{:S(2)}) collective-permute-start(bf16[80,512]{1,0:T(8,128)(2,1)S(1)} %get-tuple-element.29), channel_id=1, source_target_pairs={{0,1},{2,3},{4,5},{6,7},{8,9},{10,11},{12,13},{14,15},{1,0},{3,2},... | collective-permute-start | bytes 245768 | tf_op jit(solution)/shard_map/ppermute | solution.py:246
  4.1 2.5 %collective-permute-start.1 = (bf16[80,512]{1,0:T(8,128)(2,1)S(1)}, bf16[80,512]{1,0:T(8,128)(2,1)S(1)}, u32[]{:S(2)}, u32[]{:S(2)}) collective-permute-start(bf16[80,512]{1,0:T(8,128)(2,1)S(1)} %get-tuple-element.30), channel_id=1, source_target_pairs={{1,2},{3,4},{5,6},{7,8},{9,10},{11,12},{13,14},{2,1},{4,3},{6,5},{... | collective-permute-start | bytes 245768 | tf_op jit(solution)/shard_map/ppermute | solution.py:246
  6.6 0.0 collective-permute-done
  6.6 3.2 %collective-permute-done.1 = bf16[80,512]{1,0:T(8,128)(2,1)S(1)} collective-permute-done((bf16[80,512]{1,0:T(8,128)(2,1)S(1)}, bf16[80,512]{1,0:T(8,128)(2,1)S(1)}, u32[]{:S(2)}, u32[]{:S(2)}) %collective-permute-start.1) | collective-permute-done | bytes 81952 | tf_op jit(solution)/shard_map/ppermute | solution.py:246
  9.9 3.2 %collective-permute-start.3 = (bf16[416,256]{1,0:T(8,128)(2,1)S(1)}, bf16[416,256]{1,0:T(8,128)(2,1)S(1)}, u32[]{:S(2)}, u32[]{:S(2)}) collective-permute-start(bf16[416,256]{1,0:T(8,128)(2,1)S(1)} %get-tuple-element.28), channel_id=1, source_target_pairs={{0,16},{32,48},{64,80},{96,112},{128,144},{160,176},{192,208},{224... | collective-permute-start | bytes 638984 | tf_op jit(solution)/shard_map/ppermute | solution.py:246
  13.2 0.1 pad.3.clone
  13.3 0.1 stack.33.bounds
  13.3 0.0 copy-done.4
  13.4 0.0 copy-done.5
  13.4 2.4 %shard_map.67 = (bf16[9,256,512]{2,1,0:T(8,128)(2,1)S(1)}, bf16[9,256,512]{2,1,0:T(8,128)(2,1)S(1)}, bf16[16,128,128]{2,1,0:T(8,128)(2,1)S(1)}) custom-call(bf16[27,32,64]{2,1,0:T(8,128)(2,1)S(1)} %copy-done.5, bf16[128,2048]{1,0:T(8,128)(2,1)S(1)} %copy-done.4), custom_call_target="tpu_custom_call" | custom-call | flops 268435456 | bytes 4194304 | tf_op jit(solution)/shard_map/pallas_call | solution.py:298
  15.8 9.0 %collective-permute-start.2 = (bf16[416,256]{1,0:T(8,128)(2,1)S(1)}, bf16[416,256]{1,0:T(8,128)(2,1)S(1)}, u32[]{:S(2)}, u32[]{:S(2)}) collective-permute-start(bf16[416,256]{1,0:T(8,128)(2,1)S(1)} %get-tuple-element.27), channel_id=1, source_target_pairs={{16,32},{48,64},{80,96},{112,128},{144,160},{176,192},{208,224},{2... | collective-permute-start | bytes 638984 | tf_op jit(solution)/shard_map/ppermute | solution.py:246
  24.7 0.0 copy-done.1
  24.8 0.0 copy-done.2
  24.8 1.6 %shard_map.64 = (bf16[9,256,512]{2,1,0:T(8,128)(2,1)S(1)}, bf16[16,128,128]{2,1,0:T(8,128)(2,1)S(1)}) custom-call(bf16[27,32,32]{2,1,0:T(8,128)(2,1)S(1)} %copy-done.2, bf16[2048,128]{1,0:T(8,128)(2,1)S(1)} %copy-done.1), custom_call_target="tpu_custom_call" | custom-call | flops 134217728 | bytes 4194304 | tf_op jit(solution)/shard_map/pallas_call | solution.py:280
  26.3 0.0 collective-permute-done.3.near
  26.3 5.4 %shard_map.65 = (bf16[384,256]{1,0:T(8,128)(2,1)S(1)}, bf16[384,256]{1,0:T(8,128)(2,1)S(1)}, bf16[4,8,512]{2,1,0:T(8,128)(2,1)S(1)}, bf16[2,8,512]{2,1,0:T(8,128)(2,1)S(1)}) custom-call(s32[9]{0:T(128)S(1)} %stack.33.bounds, bf16[416,512]{1,0:T(8,128)(2,1)S(1)} %pad_maximum_fusion.own, bf16[416,256]{1,0:T(8,128)(2,1)S(1)} %collective-permute-done.3.near, ...), custom_call_target="tpu_custom_call" | custom-call | flops 2147483648 | bytes 4194304 | tf_op jit(solution)/shard_map/pallas_call | solution.py:284
  31.7 19.6 %collective-permute-done.2.far = bf16[416,256]{1,0:T(8,128)(2,1)S(1)} collective-permute-done((bf16[416,256]{1,0:T(8,128)(2,1)S(1)}, bf16[416,256]{1,0:T(8,128)(2,1)S(1)}, u32[]{:S(2)}, u32[]{:S(2)}) %collective-permute-start.2) | collective-permute-done | bytes 213024 | tf_op jit(solution)/shard_map/ppermute | solution.py:246
  51.3 2.5 %shard_map.66 = (bf16[384,256]{1,0:T(8,128)(2,1)S(1)}, bf16[4,8,512]{2,1,0:T(8,128)(2,1)S(1)}) custom-call(s32[9]{0:T(128)S(1)} %stack.33.bounds, bf16[416,512]{1,0:T(8,128)(2,1)S(1)} %pad_maximum_fusion.own, bf16[416,256]{1,0:T(8,128)(2,1)S(1)} %collective-permute-done.2.far, bf16[9,256,512]{2,1,0:T(8,128)(2,1)S(1)} %get-tuple-element.16.w1, ...), custom_call_target="tpu_custom_call" | custom-call | flops 1073741824 | bytes 4194304 | tf_op jit(solution)/shard_map/pallas_call | solution.py:294
  53.9 1.9 %collective-permute-start.4 = (bf16[4,8,512]{2,1,0:T(8,128)(2,1)S(1)}, bf16[4,8,512]{2,1,0:T(8,128)(2,1)S(1)}, u32[]{:S(2)}, u32[]{:S(2)}) collective-permute-start(bf16[4,8,512]{2,1,0:T(8,128)(2,1)S(1)} %get-tuple-element.19), channel_id=1, source_target_pairs={{0,16},{32,48},{64,80},{96,112},{128,144},{160,176},{192,208},{224... | collective-permute-start | bytes 98312 | tf_op jit(solution)/shard_map/ppermute | solution.py:246
  55.8 4.1 %collective-permute-start.5 = (bf16[4,8,512]{2,1,0:T(8,128)(2,1)S(1)}, bf16[4,8,512]{2,1,0:T(8,128)(2,1)S(1)}, u32[]{:S(2)}, u32[]{:S(2)}) collective-permute-start(bf16[4,8,512]{2,1,0:T(8,128)(2,1)S(1)} %get-tuple-element.20), channel_id=1, source_target_pairs={{16,32},{48,64},{80,96},{112,128},{144,160},{176,192},{208,224},{2... | collective-permute-start | bytes 98312 | tf_op jit(solution)/shard_map/ppermute | solution.py:246
  59.9 0.0 collective-permute-done.4
  60.0 13.5 %collective-permute-done.5 = bf16[4,8,512]{2,1,0:T(8,128)(2,1)S(1)} collective-permute-done((bf16[4,8,512]{2,1,0:T(8,128)(2,1)S(1)}, bf16[4,8,512]{2,1,0:T(8,128)(2,1)S(1)}, u32[]{:S(2)}, u32[]{:S(2)}) %collective-permute-start.5) | collective-permute-done | bytes 32800 | tf_op jit(solution)/shard_map/ppermute | solution.py:246
  73.4 0.1 broadcast_select_fusion.9
  73.5 3.8 %collective-permute-start.6 = (bf16[14,4,512]{2,1,0:T(4,128)(2,1)S(1)}, bf16[14,4,512]{2,1,0:T(4,128)(2,1)S(1)}, u32[]{:S(2)}, u32[]{:S(2)}) collective-permute-start(bf16[14,4,512]{2,1,0:T(4,128)(2,1)S(1)} %get-tuple-element.35), channel_id=1, source_target_pairs={{0,1},{2,3},{4,5},{6,7},{8,9},{10,11},{12,13},{14,15},{1,0},{3,2},... | collective-permute-start | bytes 172040 | tf_op jit(solution)/shard_map/ppermute | solution.py:246
  77.3 2.1 %collective-permute-start.7 = (bf16[14,4,512]{2,1,0:T(4,128)(2,1)S(1)}, bf16[14,4,512]{2,1,0:T(4,128)(2,1)S(1)}, u32[]{:S(2)}, u32[]{:S(2)}) collective-permute-start(bf16[14,4,512]{2,1,0:T(4,128)(2,1)S(1)} %get-tuple-element.36), channel_id=1, source_target_pairs={{1,2},{3,4},{5,6},{7,8},{9,10},{11,12},{13,14},{2,1},{4,3},{6,5},{... | collective-permute-start | bytes 172040 | tf_op jit(solution)/shard_map/ppermute | solution.py:246
  79.4 0.0 copy-start.3
  79.4 2.1 %shard_map.68.part_ref = f32[2,256,256]{2,1,0:T(8,128)S(1)} custom-call(s32[9]{0:T(128)S(1)} %stack.33.bounds, bf16[384,256]{1,0:T(8,128)(2,1)S(1)} %get-tuple-element.23.near, bf16[384,256]{1,0:T(8,128)(2,1)S(1)} %get-tuple-element.24.own, bf16[384,256]{1,0:T(8,128)(2,1)S(1)} %get-tuple-element.25.far, bf16[9,256,512]{2,1,0:T(8,128)(2,1)S(1)} %get-tuple-element.26.weight), custom_call_target="tpu_custom_call" | custom-call | flops 2147483648 | bytes 4194304 | tf_op jit(solution)/shard_map/pallas_call | solution.py:307
  81.5 0.0 collective-permute-done.6
  81.5 1.3 %collective-permute-done.7 = bf16[14,4,512]{2,1,0:T(4,128)(2,1)S(1)} collective-permute-done((bf16[14,4,512]{2,1,0:T(4,128)(2,1)S(1)}, bf16[14,4,512]{2,1,0:T(4,128)(2,1)S(1)}, u32[]{:S(2)}, u32[]{:S(2)}) %collective-permute-start.7) | collective-permute-done | bytes 57376 | tf_op jit(solution)/shard_map/ppermute | solution.py:246
  82.8 0.1 maximum_maximum_fusion.coarse_ref
  83.0 0.0 copy-done.3
  83.0 9.4 %shard_map.69 = bf16[32,16,256]{2,1,0:T(8,128)(2,1)} custom-call(s32[9]{0:T(128)S(1)} %stack.33.bounds, bf16[14,16,512]{2,1,0:T(8,128)(2,1)S(1)} %maximum_maximum_fusion.coarse_ref, bf16[4,27,128,128]{3,2,1,0:T(8,128)(2,1)S(1)} %copy-done.3, bf16[16,128,128]{2,1,0:T(8,128)(2,1)S(1)} %get-tuple-element.21.wupr, ...), custom_call_target="tpu_custom_call" | custom-call | flops 3221225472 | bytes 4194304 | tf_op jit(solution)/shard_map/pallas_call | solution.py:315
  (10 shorter events, 0.2 us)
Async XLA Ops:
  0.0 1.0 %copy-start = (bf16[32,16,256]{2,1,0:T(8,128)(2,1)S(1)}, bf16[32,16,256]{2,1,0:T(8,128)(2,1)}, u32[]{:S(2)}) copy-start(bf16[32,16,256]{2,1,0:T(8,128)(2,1)} %param.6) | copy-start | bytes 786436
  0.0 13.3 %copy-start.4 = (bf16[128,2048]{1,0:T(8,128)(2,1)S(1)}, bf16[128,2048]{1,0:T(8,128)(2,1)}, u32[]{:S(2)}) copy-start(bf16[128,2048]{1,0:T(8,128)(2,1)} %up.1) | copy-start | bytes 1572868
  0.0 13.3 %copy-start.5 = (bf16[27,32,64]{2,1,0:T(8,128)(2,1)S(1)}, bf16[27,32,64]{2,1,0:T(8,128)(2,1)}, u32[]{:S(2)}) copy-start(bf16[27,32,64]{2,1,0:T(8,128)(2,1)} %closing.1) | copy-start | bytes 331780
  1.0 23.8 %copy-start.1 = (bf16[2048,128]{1,0:T(8,128)(2,1)S(1)}, bf16[2048,128]{1,0:T(8,128)(2,1)}, u32[]{:S(2)}) copy-start(bf16[2048,128]{1,0:T(8,128)(2,1)} %down.1) | copy-start | bytes 1572868
  1.0 23.8 %copy-start.2 = (bf16[27,32,32]{2,1,0:T(8,128)(2,1)S(1)}, bf16[27,32,32]{2,1,0:T(8,128)(2,1)}, u32[]{:S(2)}) copy-start(bf16[27,32,32]{2,1,0:T(8,128)(2,1)} %first.1) | copy-start | bytes 165892
  1.5 5.2 %collective-permute-start = (bf16[80,512]{1,0:T(8,128)(2,1)S(1)}, bf16[80,512]{1,0:T(8,128)(2,1)S(1)}, u32[]{:S(2)}, u32[]{:S(2)}) collective-permute-start(bf16[80,512]{1,0:T(8,128)(2,1)S(1)} %get-tuple-element.29), channel_id=1, source_target_pairs={{0,1},{2,3},{4,5},{6,7},{8,9},{10,11},{12,13},{14,15},{1,0},{3,2},... | collective-permute-start | bytes 245768 | tf_op jit(solution)/shard_map/ppermute | solution.py:246
  4.1 5.8 %collective-permute-start.1 = (bf16[80,512]{1,0:T(8,128)(2,1)S(1)}, bf16[80,512]{1,0:T(8,128)(2,1)S(1)}, u32[]{:S(2)}, u32[]{:S(2)}) collective-permute-start(bf16[80,512]{1,0:T(8,128)(2,1)S(1)} %get-tuple-element.30), channel_id=1, source_target_pairs={{1,2},{3,4},{5,6},{7,8},{9,10},{11,12},{13,14},{2,1},{4,3},{6,5},{... | collective-permute-start | bytes 245768 | tf_op jit(solution)/shard_map/ppermute | solution.py:246
  9.9 16.4 %collective-permute-start.3 = (bf16[416,256]{1,0:T(8,128)(2,1)S(1)}, bf16[416,256]{1,0:T(8,128)(2,1)S(1)}, u32[]{:S(2)}, u32[]{:S(2)}) collective-permute-start(bf16[416,256]{1,0:T(8,128)(2,1)S(1)} %get-tuple-element.28), channel_id=1, source_target_pairs={{0,16},{32,48},{64,80},{96,112},{128,144},{160,176},{192,208},{224... | collective-permute-start | bytes 638984 | tf_op jit(solution)/shard_map/ppermute | solution.py:246
  15.8 35.6 %collective-permute-start.2 = (bf16[416,256]{1,0:T(8,128)(2,1)S(1)}, bf16[416,256]{1,0:T(8,128)(2,1)S(1)}, u32[]{:S(2)}, u32[]{:S(2)}) collective-permute-start(bf16[416,256]{1,0:T(8,128)(2,1)S(1)} %get-tuple-element.27), channel_id=1, source_target_pairs={{16,32},{48,64},{80,96},{112,128},{144,160},{176,192},{208,224},{2... | collective-permute-start | bytes 638984 | tf_op jit(solution)/shard_map/ppermute | solution.py:246
  53.9 6.1 %collective-permute-start.4 = (bf16[4,8,512]{2,1,0:T(8,128)(2,1)S(1)}, bf16[4,8,512]{2,1,0:T(8,128)(2,1)S(1)}, u32[]{:S(2)}, u32[]{:S(2)}) collective-permute-start(bf16[4,8,512]{2,1,0:T(8,128)(2,1)S(1)} %get-tuple-element.19), channel_id=1, source_target_pairs={{0,16},{32,48},{64,80},{96,112},{128,144},{160,176},{192,208},{224... | collective-permute-start | bytes 98312 | tf_op jit(solution)/shard_map/ppermute | solution.py:246
  55.8 17.6 %collective-permute-start.5 = (bf16[4,8,512]{2,1,0:T(8,128)(2,1)S(1)}, bf16[4,8,512]{2,1,0:T(8,128)(2,1)S(1)}, u32[]{:S(2)}, u32[]{:S(2)}) collective-permute-start(bf16[4,8,512]{2,1,0:T(8,128)(2,1)S(1)} %get-tuple-element.20), channel_id=1, source_target_pairs={{16,32},{48,64},{80,96},{112,128},{144,160},{176,192},{208,224},{2... | collective-permute-start | bytes 98312 | tf_op jit(solution)/shard_map/ppermute | solution.py:246
  73.5 8.0 %collective-permute-start.6 = (bf16[14,4,512]{2,1,0:T(4,128)(2,1)S(1)}, bf16[14,4,512]{2,1,0:T(4,128)(2,1)S(1)}, u32[]{:S(2)}, u32[]{:S(2)}) collective-permute-start(bf16[14,4,512]{2,1,0:T(4,128)(2,1)S(1)} %get-tuple-element.35), channel_id=1, source_target_pairs={{0,1},{2,3},{4,5},{6,7},{8,9},{10,11},{12,13},{14,15},{1,0},{3,2},... | collective-permute-start | bytes 172040 | tf_op jit(solution)/shard_map/ppermute | solution.py:246
  77.3 5.5 %collective-permute-start.7 = (bf16[14,4,512]{2,1,0:T(4,128)(2,1)S(1)}, bf16[14,4,512]{2,1,0:T(4,128)(2,1)S(1)}, u32[]{:S(2)}, u32[]{:S(2)}) collective-permute-start(bf16[14,4,512]{2,1,0:T(4,128)(2,1)S(1)} %get-tuple-element.36), channel_id=1, source_target_pairs={{1,2},{3,4},{5,6},{7,8},{9,10},{11,12},{13,14},{2,1},{4,3},{6,5},{... | collective-permute-start | bytes 172040 | tf_op jit(solution)/shard_map/ppermute | solution.py:246
  79.4 3.6 %copy-start.3 = (bf16[4,27,128,128]{3,2,1,0:T(8,128)(2,1)S(1)}, bf16[4,27,128,128]{3,2,1,0:T(8,128)(2,1)}, u32[]{:S(2)}) copy-start(bf16[4,27,128,128]{3,2,1,0:T(8,128)(2,1)} %w_coarse.1) | copy-start | bytes 10616836

commit v6 on v5

--- a/solution.py
+++ b/solution.py
@@ -37,11 +37,40 @@
     return jnp.where(fine == (y - first) * NZ + z, 1.0, 0.0).astype(BF)
 
 
+def moved(value, start, target):
+    lane = iota(value.shape, 1)
+    return jnp.where(lane >> 5 == target // 32, pltpu.roll(value, (target - start) % 128, 1), 0.0)
+
+
+def packed(joined, tile, fifth_tile, start):
+    fifth = joined[:, 128 * fifth_tile : 128 * fifth_tile + 128]
+    blocks = [moved(fifth[104 * k : 104 * k + 104], start, 32 * k) for k in range(4)]
+    return jnp.concatenate(
+        [joined[:, 128 * tile : 128 * tile + 128], (blocks[0] + blocks[1]) + (blocks[2] + blocks[3])], axis=0
+    )
+
+
+def pack_kernel(bounds, own, chips, cores, joined_ref, to_near, to_far):
+    odd, odd_y = bounds[8] == 1, bounds[9] == 1
+    chip, core = chips[...].astype(F32), cores[...].astype(F32)
+    joined = jnp.concatenate(
+        [jnp.where(odd_y, core, chip), own[...].astype(F32), jnp.where(odd_y, chip, core)], axis=0
+    )
+    joined_ref[...] = joined.astype(BF)
+    left, right = packed(joined, 0, 1, 0), packed(joined, 3, 2, 96)
+    to_far[...] = jnp.where(odd, right, left).astype(BF)
+    to_near[...] = jnp.where(odd, left, right).astype(BF)
+
+
 def side_window(own, halo, halo_at_left, lanes):
     tile = lanes.start // 128
     other = slice(128 * (tile ^ 2), 128 * (tile ^ 2) + 128)
-    here = slice(128 * (tile & 1), 128 * (tile & 1) + 128)
-    outer, inner = halo[:, here].astype(F32), own[:, other].astype(F32)
+    inner = own[:, other].astype(F32)
+    if tile in (1, 2):
+        outer = halo[0:416].astype(F32)
+    else:
+        fifth = halo[416:520].astype(F32)
+        outer = jnp.concatenate([moved(fifth, 32 * k, 96 if tile == 0 else 0) for k in range(4)], axis=0)
     return jnp.where(halo_at_left, outer, inner) if tile < 2 else jnp.where(halo_at_left, inner, outer)
 
 
@@ -246,10 +275,10 @@
     return lax.ppermute(array, axis, pairs + [(j, i) for i, j in pairs])
 
 
-def y_neighbours(bottom, top, odd_y):
+def y_swaps(bottom, top, odd_y):
     chips = swap(jnp.where(odd_y, top, bottom), "sy", 1)
     cores = swap(jnp.where(odd_y, bottom, top), "sy", 0)
-    return jnp.where(odd_y, cores, chips), jnp.where(odd_y, chips, cores)
+    return chips, cores
 
 
 def local(volume, w_first, down_weight, w_coarse, w_up, closing_weight):
@@ -267,16 +296,18 @@
             jnp.where(first_y, 0, -99),
             jnp.where(last_y, 3, 99),
             ix & 1,
+            iy & 1,
         ]
     ).astype(jnp.int32)
     odd = (ix & 1) == 1
     own = dot(volume.reshape(512, 256), place_own(), TN).astype(BF)
     odd_y = (iy & 1) == 1
-    below, above = y_neighbours(own[0:80], own[176:256], odd_y)
-    own = jnp.concatenate([below, own, above], axis=0)
-    left, right = own[:, :256], own[:, 256:]
-    near = swap(jnp.where(odd, left, right), "sx", 0)
-    far = swap(jnp.where(odd, right, left), "sx", 1)
+    chips, cores = y_swaps(own[0:80], own[176:256], odd_y)
+    own, to_near, to_far = call(
+        pack_kernel, [((416, 512), BF), ((520, 128), BF), ((520, 128), BF)], [], 3, True, 1 << 20, 8
+    )(bounds, own, chips, cores)
+    near = swap(to_near, "sx", 0)
+    far = swap(to_far, "sx", 1)
     w1, dwr = call(
         prepare_first_kernel, [((9, 256, 512), BF), ((16, 128, 128), BF)], [((2048, 128), F32)], 2, False, 1 << 27, 12
     )(w_first, down_weight)
@@ -310,7 +341,8 @@
     odd_order = jnp.concatenate([near_cells, to_far[:2], to_near, far_cells], axis=0)
     even_order = jnp.concatenate([far_cells, to_near, to_far[2:], near_cells], axis=0)
     coarse = jnp.where(odd, odd_order, even_order)
-    before, after = y_neighbours(coarse[:, 2:6], coarse[:, 0:4], odd_y)
+    chips, cores = y_swaps(coarse[:, 2:6], coarse[:, 0:4], odd_y)
+    before, after = jnp.where(odd_y, cores, chips), jnp.where(odd_y, chips, cores)
     coarse = jnp.concatenate([before, coarse[:, 0:6], after, jnp.zeros((14, 2, 512), BF)], axis=1)
     (result,) = call(
         last_kernel,

time: 92.7 us -> 86 us (0.928)
  the two profiles are of different devices: /device:TPU:449 before, /device:TPU:289 now
where the time goes in v6:
time: 86 us; the launch traced here: 85.7 us
  waiting for transfers between devices  36.5 us (42%)
  Pallas kernels  24.2 us (28%)
  starting transfers between devices  22.8 us (27%)
  local copies, waits for them, and re-layouts  1.08 us (1%)
    ppermute x8, waiting for transfers between devices, swap(): return lax.ppermute(array, axis, pairs + [(j, i) for i, j in pairs])  36.5 us
    ppermute x8, starting transfers between devices, swap(): return lax.ppermute(array, axis, pairs + [(j, i) for i, j in pairs])  22.8 us
    pallas_call x1, Pallas kernels, local(): call(last_kernel, [((32, 16, 256), BF)], [((3, 224, 512), BF), ((512, 768...  9.42 us
    pallas_call x1, Pallas kernels, local(): call(near_kernel, [skip, skip, cells, ((2, 8, 512), BF)], [((3, 416, 512)...  5.42 us
    pallas_call x1, Pallas kernels, local(): call(far_kernel, [skip, cells], [((3, 416, 512), BF), ((512, 256), BF)],...  2.67 us
    pallas_call x1, Pallas kernels, local(): call(prepare_last_kernel, [((9, 256, 512), BF), ((9, 256, 512), BF), ((16...  2.4 us
    pallas_call x1, Pallas kernels, local(): call(skip_kernel, [((2, 256, 256), F32)], [((3, 288, 768), BF)], 4, True,...  2.07 us
  transfers between devices with their start and end apart: 8, of which 6 were waited for; matrix products, arithmetic and copies ran while one was open for 0% of the time, Pallas kernels for 13%

profile of v6, /device:TPU:289, one launch (start us, length us, event | category | flops | bytes accessed | tf_op | source)
XLA Modules:
  0.0 85.7 jit_solution(13939223266845532160)
XLA Ops:
  0.0 0.0 copy-start
  0.0 0.0 copy-start.2
  0.0 0.0 copy-start.1
  0.0 0.0 copy-start.4
  0.0 0.0 copy-start.5
  0.1 0.9 %copy-done = bf16[32,16,256]{2,1,0:T(8,128)(2,1)S(1)} copy-done((bf16[32,16,256]{2,1,0:T(8,128)(2,1)S(1)}, bf16[32,16,256]{2,1,0:T(8,128)(2,1)}, u32[]{:S(2)}) %copy-start) | copy-done | bytes 262168
  1.0 0.5 fusion.own
  1.5 3.2 %collective-permute-start = (bf16[80,512]{1,0:T(8,128)(2,1)S(1)}, bf16[80,512]{1,0:T(8,128)(2,1)S(1)}, u32[]{:S(2)}, u32[]{:S(2)}) collective-permute-start(bf16[80,512]{1,0:T(8,128)(2,1)S(1)} %get-tuple-element.34), channel_id=1, source_target_pairs={{1,2},{3,4},{5,6},{7,8},{9,10},{11,12},{13,14},{2,1},{4,3},{6,5},{... | collective-permute-start | bytes 245768 | tf_op jit(solution)/shard_map/ppermute | solution.py:275
  4.7 1.9 %collective-permute-start.1 = (bf16[80,512]{1,0:T(8,128)(2,1)S(1)}, bf16[80,512]{1,0:T(8,128)(2,1)S(1)}, u32[]{:S(2)}, u32[]{:S(2)}) collective-permute-start(bf16[80,512]{1,0:T(8,128)(2,1)S(1)} %get-tuple-element.33), channel_id=1, source_target_pairs={{0,1},{2,3},{4,5},{6,7},{8,9},{10,11},{12,13},{14,15},{1,0},{3,2},... | collective-permute-start | bytes 245768 | tf_op jit(solution)/shard_map/ppermute | solution.py:275
  6.7 0.1 stack.37.bounds
  6.7 0.8 collective-permute-done.chips
  7.5 0.3 collective-permute-done.1.cores
  7.9 0.7 shard_map.64
  8.6 3.2 %collective-permute-start.3 = (bf16[520,128]{1,0:T(8,128)(2,1)S(1)}, bf16[520,128]{1,0:T(8,128)(2,1)S(1)}, u32[]{:S(2)}, u32[]{:S(2)}) collective-permute-start(bf16[520,128]{1,0:T(8,128)(2,1)S(1)} %get-tuple-element.23), channel_id=1, source_target_pairs={{0,16},{32,48},{64,80},{96,112},{128,144},{160,176},{192,208},{224... | collective-permute-start | bytes 399368 | tf_op jit(solution)/shard_map/ppermute | solution.py:275
  11.8 0.1 pad.3.clone
  11.9 0.0 copy-done.2
  11.9 0.0 copy-done.1
  11.9 1.6 %shard_map.65 = (bf16[9,256,512]{2,1,0:T(8,128)(2,1)S(1)}, bf16[16,128,128]{2,1,0:T(8,128)(2,1)S(1)}) custom-call(bf16[27,32,32]{2,1,0:T(8,128)(2,1)S(1)} %copy-done.2, bf16[2048,128]{1,0:T(8,128)(2,1)S(1)} %copy-done.1), custom_call_target="tpu_custom_call" | custom-call | flops 134217728 | bytes 4194304 | tf_op jit(solution)/shard_map/pallas_call | solution.py:311
  13.4 0.0 copy-done.4
  13.4 0.0 copy-done.5
  13.4 2.4 %shard_map.68 = (bf16[9,256,512]{2,1,0:T(8,128)(2,1)S(1)}, bf16[9,256,512]{2,1,0:T(8,128)(2,1)S(1)}, bf16[16,128,128]{2,1,0:T(8,128)(2,1)S(1)}) custom-call(bf16[27,32,64]{2,1,0:T(8,128)(2,1)S(1)} %copy-done.5, bf16[128,2048]{1,0:T(8,128)(2,1)S(1)} %copy-done.4), custom_call_target="tpu_custom_call" | custom-call | flops 268435456 | bytes 4194304 | tf_op jit(solution)/shard_map/pallas_call | solution.py:329
  15.8 4.2 %collective-permute-start.2 = (bf16[520,128]{1,0:T(8,128)(2,1)S(1)}, bf16[520,128]{1,0:T(8,128)(2,1)S(1)}, u32[]{:S(2)}, u32[]{:S(2)}) collective-permute-start(bf16[520,128]{1,0:T(8,128)(2,1)S(1)} %get-tuple-element.20), channel_id=1, source_target_pairs={{16,32},{48,64},{80,96},{112,128},{144,160},{176,192},{208,224},{2... | collective-permute-start | bytes 399368 | tf_op jit(solution)/shard_map/ppermute | solution.py:275
  20.0 0.0 collective-permute-done.3.near
  20.0 5.4 %shard_map.66 = (bf16[384,256]{1,0:T(8,128)(2,1)S(1)}, bf16[384,256]{1,0:T(8,128)(2,1)S(1)}, bf16[4,8,512]{2,1,0:T(8,128)(2,1)S(1)}, bf16[2,8,512]{2,1,0:T(8,128)(2,1)S(1)}) custom-call(s32[10]{0:T(128)S(1)} %stack.37.bounds, bf16[416,512]{1,0:T(8,128)(2,1)S(1)} %get-tuple-element.19.own, bf16[520,128]{1,0:T(8,128)(2,1)S(1)} %collective-permute-done.3.near, ...), custom_call_target="tpu_custom_call" | custom-call | flops 2147483648 | bytes 4194304 | tf_op jit(solution)/shard_map/pallas_call | solution.py:315
  25.5 18.4 %collective-permute-done.2.far = bf16[520,128]{1,0:T(8,128)(2,1)S(1)} collective-permute-done((bf16[520,128]{1,0:T(8,128)(2,1)S(1)}, bf16[520,128]{1,0:T(8,128)(2,1)S(1)}, u32[]{:S(2)}, u32[]{:S(2)}) %collective-permute-start.2) | collective-permute-done | bytes 133152 | tf_op jit(solution)/shard_map/ppermute | solution.py:275
  43.9 2.7 %shard_map.67 = (bf16[384,256]{1,0:T(8,128)(2,1)S(1)}, bf16[4,8,512]{2,1,0:T(8,128)(2,1)S(1)}) custom-call(s32[10]{0:T(128)S(1)} %stack.37.bounds, bf16[416,512]{1,0:T(8,128)(2,1)S(1)} %get-tuple-element.19.own, bf16[520,128]{1,0:T(8,128)(2,1)S(1)} %collective-permute-done.2.far, bf16[9,256,512]{2,1,0:T(8,128)(2,1)S(1)} %get-tuple-element.21.w1, ...), custom_call_target="tpu_custom_call" | custom-call | flops 1073741824 | bytes 4194304 | tf_op jit(solution)/shard_map/pallas_call | solution.py:325
  46.6 1.9 %collective-permute-start.4 = (bf16[4,8,512]{2,1,0:T(8,128)(2,1)S(1)}, bf16[4,8,512]{2,1,0:T(8,128)(2,1)S(1)}, u32[]{:S(2)}, u32[]{:S(2)}) collective-permute-start(bf16[4,8,512]{2,1,0:T(8,128)(2,1)S(1)} %get-tuple-element.25), channel_id=1, source_target_pairs={{0,16},{32,48},{64,80},{96,112},{128,144},{160,176},{192,208},{224... | collective-permute-start | bytes 98312 | tf_op jit(solution)/shard_map/ppermute | solution.py:275
  48.5 1.9 %collective-permute-start.5 = (bf16[4,8,512]{2,1,0:T(8,128)(2,1)S(1)}, bf16[4,8,512]{2,1,0:T(8,128)(2,1)S(1)}, u32[]{:S(2)}, u32[]{:S(2)}) collective-permute-start(bf16[4,8,512]{2,1,0:T(8,128)(2,1)S(1)} %get-tuple-element.26), channel_id=1, source_target_pairs={{16,32},{48,64},{80,96},{112,128},{144,160},{176,192},{208,224},{2... | collective-permute-start | bytes 98312 | tf_op jit(solution)/shard_map/ppermute | solution.py:275
  50.4 0.8 collective-permute-done.4
  51.2 14.9 %collective-permute-done.5 = bf16[4,8,512]{2,1,0:T(8,128)(2,1)S(1)} collective-permute-done((bf16[4,8,512]{2,1,0:T(8,128)(2,1)S(1)}, bf16[4,8,512]{2,1,0:T(8,128)(2,1)S(1)}, u32[]{:S(2)}, u32[]{:S(2)}) %collective-permute-start.5) | collective-permute-done | bytes 32800 | tf_op jit(solution)/shard_map/ppermute | solution.py:275
  66.1 0.1 broadcast_select_fusion.5
  66.2 4.4 %collective-permute-start.6 = (bf16[14,4,512]{2,1,0:T(4,128)(2,1)S(1)}, bf16[14,4,512]{2,1,0:T(4,128)(2,1)S(1)}, u32[]{:S(2)}, u32[]{:S(2)}) collective-permute-start(bf16[14,4,512]{2,1,0:T(4,128)(2,1)S(1)} %get-tuple-element.37), channel_id=1, source_target_pairs={{0,1},{2,3},{4,5},{6,7},{8,9},{10,11},{12,13},{14,15},{1,0},{3,2},... | collective-permute-start | bytes 172040 | tf_op jit(solution)/shard_map/ppermute | solution.py:275
  70.6 2.1 %collective-permute-start.7 = (bf16[14,4,512]{2,1,0:T(4,128)(2,1)S(1)}, bf16[14,4,512]{2,1,0:T(4,128)(2,1)S(1)}, u32[]{:S(2)}, u32[]{:S(2)}) collective-permute-start(bf16[14,4,512]{2,1,0:T(4,128)(2,1)S(1)} %get-tuple-element.38), channel_id=1, source_target_pairs={{1,2},{3,4},{5,6},{7,8},{9,10},{11,12},{13,14},{2,1},{4,3},{6,5},{... | collective-permute-start | bytes 172040 | tf_op jit(solution)/shard_map/ppermute | solution.py:275
  72.7 0.0 copy-start.3
  72.7 2.1 %shard_map.69.part_ref = f32[2,256,256]{2,1,0:T(8,128)S(1)} custom-call(s32[10]{0:T(128)S(1)} %stack.37.bounds, bf16[384,256]{1,0:T(8,128)(2,1)S(1)} %get-tuple-element.29.near, bf16[384,256]{1,0:T(8,128)(2,1)S(1)} %get-tuple-element.30.own, bf16[384,256]{1,0:T(8,128)(2,1)S(1)} %get-tuple-element.31.far, bf16[9,256,512]{2,1,0:T(8,128)(2,1)S(1)} %get-tuple-element.32.weight), custom_call_target="tpu_custom_call" | custom-call | flops 2147483648 | bytes 4194304 | tf_op jit(solution)/shard_map/pallas_call | solution.py:338
  74.8 0.0 collective-permute-done.6
  74.8 1.3 %collective-permute-done.7 = bf16[14,4,512]{2,1,0:T(4,128)(2,1)S(1)} collective-permute-done((bf16[14,4,512]{2,1,0:T(4,128)(2,1)S(1)}, bf16[14,4,512]{2,1,0:T(4,128)(2,1)S(1)}, u32[]{:S(2)}, u32[]{:S(2)}) %collective-permute-start.7) | collective-permute-done | bytes 57376 | tf_op jit(solution)/shard_map/ppermute | solution.py:275
  76.1 0.1 maximum_maximum_fusion.coarse_ref
  76.3 0.0 copy-done.3
  76.3 9.4 %shard_map.70 = bf16[32,16,256]{2,1,0:T(8,128)(2,1)} custom-call(s32[10]{0:T(128)S(1)} %stack.37.bounds, bf16[14,16,512]{2,1,0:T(8,128)(2,1)S(1)} %maximum_maximum_fusion.coarse_ref, bf16[4,27,128,128]{3,2,1,0:T(8,128)(2,1)S(1)} %copy-done.3, bf16[16,128,128]{2,1,0:T(8,128)(2,1)S(1)} %get-tuple-element.27.wupr, ...), custom_call_target="tpu_custom_call" | custom-call | flops 3221225472 | bytes 4194304 | tf_op jit(solution)/shard_map/pallas_call | solution.py:347
  (7 shorter events, 0.1 us)
Async XLA Ops:
  0.0 1.0 %copy-start = (bf16[32,16,256]{2,1,0:T(8,128)(2,1)S(1)}, bf16[32,16,256]{2,1,0:T(8,128)(2,1)}, u32[]{:S(2)}) copy-start(bf16[32,16,256]{2,1,0:T(8,128)(2,1)} %param.6) | copy-start | bytes 786436
  0.0 11.9 %copy-start.2 = (bf16[27,32,32]{2,1,0:T(8,128)(2,1)S(1)}, bf16[27,32,32]{2,1,0:T(8,128)(2,1)}, u32[]{:S(2)}) copy-start(bf16[27,32,32]{2,1,0:T(8,128)(2,1)} %first.1) | copy-start | bytes 165892
  0.0 11.9 %copy-start.1 = (bf16[2048,128]{1,0:T(8,128)(2,1)S(1)}, bf16[2048,128]{1,0:T(8,128)(2,1)}, u32[]{:S(2)}) copy-start(bf16[2048,128]{1,0:T(8,128)(2,1)} %down.1) | copy-start | bytes 1572868
  0.0 13.4 %copy-start.4 = (bf16[128,2048]{1,0:T(8,128)(2,1)S(1)}, bf16[128,2048]{1,0:T(8,128)(2,1)}, u32[]{:S(2)}) copy-start(bf16[128,2048]{1,0:T(8,128)(2,1)} %up.1) | copy-start | bytes 1572868
  0.0 13.4 %copy-start.5 = (bf16[27,32,64]{2,1,0:T(8,128)(2,1)S(1)}, bf16[27,32,64]{2,1,0:T(8,128)(2,1)}, u32[]{:S(2)}) copy-start(bf16[27,32,64]{2,1,0:T(8,128)(2,1)} %closing.1) | copy-start | bytes 331780
  1.5 6.0 %collective-permute-start = (bf16[80,512]{1,0:T(8,128)(2,1)S(1)}, bf16[80,512]{1,0:T(8,128)(2,1)S(1)}, u32[]{:S(2)}, u32[]{:S(2)}) collective-permute-start(bf16[80,512]{1,0:T(8,128)(2,1)S(1)} %get-tuple-element.34), channel_id=1, source_target_pairs={{1,2},{3,4},{5,6},{7,8},{9,10},{11,12},{13,14},{2,1},{4,3},{6,5},{... | collective-permute-start | bytes 245768 | tf_op jit(solution)/shard_map/ppermute | solution.py:275
  4.7 3.2 %collective-permute-start.1 = (bf16[80,512]{1,0:T(8,128)(2,1)S(1)}, bf16[80,512]{1,0:T(8,128)(2,1)S(1)}, u32[]{:S(2)}, u32[]{:S(2)}) collective-permute-start(bf16[80,512]{1,0:T(8,128)(2,1)S(1)} %get-tuple-element.33), channel_id=1, source_target_pairs={{0,1},{2,3},{4,5},{6,7},{8,9},{10,11},{12,13},{14,15},{1,0},{3,2},... | collective-permute-start | bytes 245768 | tf_op jit(solution)/shard_map/ppermute | solution.py:275
  8.6 11.5 %collective-permute-start.3 = (bf16[520,128]{1,0:T(8,128)(2,1)S(1)}, bf16[520,128]{1,0:T(8,128)(2,1)S(1)}, u32[]{:S(2)}, u32[]{:S(2)}) collective-permute-start(bf16[520,128]{1,0:T(8,128)(2,1)S(1)} %get-tuple-element.23), channel_id=1, source_target_pairs={{0,16},{32,48},{64,80},{96,112},{128,144},{160,176},{192,208},{224... | collective-permute-start | bytes 399368 | tf_op jit(solution)/shard_map/ppermute | solution.py:275
  15.8 28.0 %collective-permute-start.2 = (bf16[520,128]{1,0:T(8,128)(2,1)S(1)}, bf16[520,128]{1,0:T(8,128)(2,1)S(1)}, u32[]{:S(2)}, u32[]{:S(2)}) collective-permute-start(bf16[520,128]{1,0:T(8,128)(2,1)S(1)} %get-tuple-element.20), channel_id=1, source_target_pairs={{16,32},{48,64},{80,96},{112,128},{144,160},{176,192},{208,224},{2... | collective-permute-start | bytes 399368 | tf_op jit(solution)/shard_map/ppermute | solution.py:275
  46.6 4.7 %collective-permute-start.4 = (bf16[4,8,512]{2,1,0:T(8,128)(2,1)S(1)}, bf16[4,8,512]{2,1,0:T(8,128)(2,1)S(1)}, u32[]{:S(2)}, u32[]{:S(2)}) collective-permute-start(bf16[4,8,512]{2,1,0:T(8,128)(2,1)S(1)} %get-tuple-element.25), channel_id=1, source_target_pairs={{0,16},{32,48},{64,80},{96,112},{128,144},{160,176},{192,208},{224... | collective-permute-start | bytes 98312 | tf_op jit(solution)/shard_map/ppermute | solution.py:275
  48.5 17.6 %collective-permute-start.5 = (bf16[4,8,512]{2,1,0:T(8,128)(2,1)S(1)}, bf16[4,8,512]{2,1,0:T(8,128)(2,1)S(1)}, u32[]{:S(2)}, u32[]{:S(2)}) collective-permute-start(bf16[4,8,512]{2,1,0:T(8,128)(2,1)S(1)} %get-tuple-element.26), channel_id=1, source_target_pairs={{16,32},{48,64},{80,96},{112,128},{144,160},{176,192},{208,224},{2... | collective-permute-start | bytes 98312 | tf_op jit(solution)/shard_map/ppermute | solution.py:275
  66.2 8.6 %collective-permute-start.6 = (bf16[14,4,512]{2,1,0:T(4,128)(2,1)S(1)}, bf16[14,4,512]{2,1,0:T(4,128)(2,1)S(1)}, u32[]{:S(2)}, u32[]{:S(2)}) collective-permute-start(bf16[14,4,512]{2,1,0:T(4,128)(2,1)S(1)} %get-tuple-element.37), channel_id=1, source_target_pairs={{0,1},{2,3},{4,5},{6,7},{8,9},{10,11},{12,13},{14,15},{1,0},{3,2},... | collective-permute-start | bytes 172040 | tf_op jit(solution)/shard_map/ppermute | solution.py:275
  70.6 5.5 %collective-permute-start.7 = (bf16[14,4,512]{2,1,0:T(4,128)(2,1)S(1)}, bf16[14,4,512]{2,1,0:T(4,128)(2,1)S(1)}, u32[]{:S(2)}, u32[]{:S(2)}) collective-permute-start(bf16[14,4,512]{2,1,0:T(4,128)(2,1)S(1)} %get-tuple-element.38), channel_id=1, source_target_pairs={{1,2},{3,4},{5,6},{7,8},{9,10},{11,12},{13,14},{2,1},{4,3},{6,5},{... | collective-permute-start | bytes 172040 | tf_op jit(solution)/shard_map/ppermute | solution.py:275
  72.7 3.6 %copy-start.3 = (bf16[4,27,128,128]{3,2,1,0:T(8,128)(2,1)S(1)}, bf16[4,27,128,128]{3,2,1,0:T(8,128)(2,1)}, u32[]{:S(2)}) copy-start(bf16[4,27,128,128]{3,2,1,0:T(8,128)(2,1)} %w_coarse.1) | copy-start | bytes 10616836

commit v7 on v6

--- a/solution.py
+++ b/solution.py
@@ -62,32 +62,45 @@
     to_near[...] = jnp.where(odd, left, right).astype(BF)
 
 
-def side_window(own, halo, halo_at_left, lanes):
-    tile = lanes.start // 128
-    other = slice(128 * (tile ^ 2), 128 * (tile ^ 2) + 128)
-    inner = own[:, other].astype(F32)
-    if tile in (1, 2):
-        outer = halo[0:416].astype(F32)
-    else:
-        fifth = halo[416:520].astype(F32)
-        outer = jnp.concatenate([moved(fifth, 32 * k, 96 if tile == 0 else 0) for k in range(4)], axis=0)
-    return jnp.where(halo_at_left, outer, inner) if tile < 2 else jnp.where(halo_at_left, inner, outer)
-
-
-def fine_groups(windows, bounds, w1, dwr, skip_refs, coarse_refs, vz, grouped):
+def own_window(own):
+    return [own[:, 128 * tile : 128 * tile + 128].astype(F32) for tile in range(4)]
+
+
+def side_window(own, halo, halo_at_left):
+    tiles = own_window(own)
+    fifth = halo[416:520].astype(F32)
+    at_end, at_start = (
+        jnp.concatenate([moved(fifth, 32 * k, lane) for k in range(4)], axis=0)
+        for lane in (96, 0)
+    )
+    close = halo[0:416].astype(F32)
+    left, right = (at_end, close, tiles[0], tiles[1]), (tiles[2], tiles[3], close, at_start)
+    return [jnp.where(halo_at_left, one, other) for one, other in zip(left, right)]
+
+
+def fill_edges(before, after, rows, target):
+    lane = iota((rows, 128), 1)
+    both = jnp.where(lane >= 96, before, jnp.where(lane < 32, after, 0.0))
+    low, middle, high = z_shifts(both, rows)
+    target[:, 0:128] = (pltpu.roll(low, 32, 1) + pltpu.roll(middle, 96, 1)).astype(BF)
+    target[:, 128:256] = pltpu.roll(high, 32, 1).astype(BF)
+
+
+def fine_groups(windows, bounds, w1, w1_edge, dwr, skip_refs, coarse_refs, vz, edges, grouped):
     to_groups = regroup(512, 384, 0, 0)
     y = (iota((384, 256), 0) >> 4) - 4
     plane = iota((384, 256), 1) >> 5
     y_inside = (y >= bounds[2]) & (y <= bounds[3])
-    for k, (window, first_x) in enumerate(windows):
-        for tile in range(4):
-            lanes = slice(128 * tile, 128 * tile + 128)
-            for oz, shifted in enumerate(z_shifts(window(lanes), 416)):
-                vz[oz, :, lanes] = shifted.astype(BF)
+    for k, (tiles, first_x) in enumerate(windows):
+        for half in range(2):
+            for oz, shifted in enumerate(z_shifts(tiles[1 + half], 416)):
+                vz[k, oz, :, 128 * half : 128 * half + 128] = shifted.astype(BF)
+        fill_edges(tiles[0], tiles[3], 416, edges.at[k])
         summed = jnp.zeros((384, 256), F32)
         for oy in range(3):
             for oz in range(3):
-                summed += dot(vz[oz, 16 * oy : 16 * oy + 384], w1[3 * oy + oz], NT)
+                summed += dot(vz[k, oz, 16 * oy : 16 * oy + 384], w1[3 * oy + oz], NT)
+            summed += dot(edges[k, 16 * oy : 16 * oy + 384], w1_edge[oy], NT)
         x = plane + first_x
         inside = y_inside & (x >= bounds[0]) & (x <= bounds[1])
         skip = jnp.where(inside, jnp.maximum(summed, 0.0), 0.0).astype(BF)
@@ -112,58 +125,59 @@
                 target[first_a + a % 2, :, 128 * z : 128 * z + 128] = cell
 
 
-def near_kernel(bounds, own, near, w1, dwr, skip_near, skip_own, to_far, coarse_own, vz, grouped):
+def near_kernel(bounds, own, near, w1, w1_edge, dwr, skip_near, skip_own, to_far, coarse_own, vz, edges, grouped):
     odd = bounds[8] == 1
     first_near, first_own = 2 - 2 * bounds[8], 2 * bounds[8]
-    windows = (
-        (lambda lanes: side_window(own, near, odd, lanes), jnp.where(odd, -4, 12)),
-        (lambda lanes: own[:, lanes].astype(F32), 4),
-    )
+    windows = ((side_window(own, near, odd), jnp.where(odd, -4, 12)), (own_window(own), 4))
     coarse = ([(to_far, first_near)], [(to_far, first_own), (coarse_own, 0)])
-    fine_groups(windows, bounds, w1, dwr, (skip_near, skip_own), coarse, vz, grouped)
-
-
-def far_kernel(bounds, own, far, w1, dwr, coarse_own, skip_far, to_near, vz, grouped):
+    fine_groups(windows, bounds, w1, w1_edge, dwr, (skip_near, skip_own), coarse, vz, edges, grouped)
+
+
+def far_kernel(bounds, own, far, w1, w1_edge, dwr, coarse_own, skip_far, to_near, vz, edges, grouped):
     to_near[pl.ds(2 - 2 * bounds[8], 2)] = coarse_own[...]
     even = bounds[8] == 0
-    windows = ((lambda lanes: side_window(own, far, even, lanes), jnp.where(even, -4, 12)),)
-    fine_groups(windows, bounds, w1, dwr, (skip_far,), ([(to_near, 2 * bounds[8])],), vz, grouped)
-
-
-def closing_sum(weight, scratch, g):
+    windows = ((side_window(own, far, even), jnp.where(even, -4, 12)),)
+    coarse = ([(to_near, 2 * bounds[8])],)
+    fine_groups(windows, bounds, w1, w1_edge, dwr, (skip_far,), coarse, vz, edges, grouped)
+
+
+def fill_shifts(tile_of, middle, edges):
+    for tile in range(1, 5):
+        for oz, shifted in enumerate(z_shifts(tile_of(tile), 288)):
+            middle[oz, :, 128 * tile - 128 : 128 * tile] = shifted.astype(BF)
+    for g in range(2):
+        fill_edges(tile_of(2 * g), tile_of(2 * g + 3), 288, edges.at[g])
+
+
+def closing_sum(weight, weight_edge, middle, edges, g):
     summed = jnp.zeros((256, 256), F32)
     for oy in range(3):
+        rows = slice(16 * oy, 16 * oy + 256)
         for oz in range(3):
-            summed += dot(
-                weight[3 * oy + oz], scratch[oz, 16 * oy : 16 * oy + 256, 256 * g : 256 * g + 512], NT
-            )
+            summed += dot(weight[3 * oy + oz], middle[oz, rows, 256 * g : 256 * g + 256], NT)
+        summed += dot(weight_edge[oy], edges[g, rows], NT)
     return summed
 
 
-def fill_shifts(value_of, scratch):
-    for tile in range(6):
-        lanes = slice(128 * tile, 128 * tile + 128)
-        for k, shifted in enumerate(z_shifts(value_of(lanes), 288)):
-            scratch[k, :, lanes] = shifted.astype(BF)
-
-
-def skip_kernel(bounds, near, own, far, weight, out_ref, scratch):
+def skip_kernel(bounds, near, own, far, weight, weight_edge, out_ref, middle, edges):
     odd = bounds[8] == 1
 
-    def value_of(lanes):
-        group, half = divmod(lanes.start // 128, 2)
+    def tile_of(tile):
+        group, half = divmod(tile, 2)
         here = slice(128 * half, 128 * half + 128)
         if group == 1:
             return own[48:336, here].astype(F32)
         first, second = near[48:336, here].astype(F32), far[48:336, here].astype(F32)
         return jnp.where(odd, first, second) if group == 0 else jnp.where(odd, second, first)
 
-    fill_shifts(value_of, scratch)
+    fill_shifts(tile_of, middle, edges)
     for g in range(2):
-        out_ref[g] = closing_sum(weight, scratch, g)
-
-
-def last_kernel(bounds, coarse_ref, w_coarse, wupr, weight, part_ref, out_ref, state, raw, up, scratch):
+        out_ref[g] = closing_sum(weight, weight_edge, middle, edges, g)
+
+
+def last_kernel(
+    bounds, coarse_ref, w_coarse, wupr, weight, weight_edge, part_ref, out_ref, state, raw, up, middle_ref, edges
+):
     value = coarse_ref[...].reshape(224, 512).astype(F32)
     for layer in range(4):
         rows_in = (14 - 2 * layer) * 16
@@ -203,26 +217,34 @@
     from_groups = regroup(288, 512, 1, 3)
     for g in range(3):
         up[:, 256 * g : 256 * g + 256] = dot(from_groups, raw[:, 256 * g : 256 * g + 256].astype(BF), NN)
-    fill_shifts(lambda lanes: up[:, lanes], scratch)
+    fill_shifts(lambda tile: up[:, 128 * tile : 128 * tile + 128], middle_ref, edges)
     row, column = iota((256, 256), 0), iota((256, 256), 1)
     to_channels = jnp.where(column == ((row & 7) << 5) + (row >> 3), 1.0, 0.0).astype(BF)
     for g in range(2):
-        total = (closing_sum(weight, scratch, g) + part_ref[g]).astype(BF)
+        total = (closing_sum(weight, weight_edge, middle_ref, edges, g) + part_ref[g]).astype(BF)
         out_ref[:, 8 * g : 8 * g + 8, :] = dot(to_channels, total, NN).reshape(32, 8, 256).astype(BF)
 
 
-def banded(source, target, channels):
+def banded(source, target, edge_target, channels):
     inputs = source.shape[2]
-    repeat = iota((inputs, 512), 0) - channels == iota((inputs, 512), 1) & 31
+    repeat = iota((inputs, 256), 0) - channels == iota((inputs, 256), 1) & 31
     repeat = jnp.where(repeat, 1.0, 0.0).astype(BF)
-    plane = (iota((32, 512), 1) >> 5) - 3
-    for t in range(9):
-        tiled = dot(jnp.concatenate([source[t], source[t + 9], source[t + 18]], axis=0), repeat, NN)
-        for x in range(8):
-            rows = jnp.where(plane == x + 2, tiled[64:], 0.0)
-            rows = jnp.where(plane == x + 1, tiled[32:64], rows)
-            rows = jnp.where(plane == x, tiled[:32], rows)
-            target[t, 32 * x : 32 * x + 32] = rows.astype(BF)
+    plane = iota((32, 256), 1) >> 5
+    for oy in range(3):
+        before = after = jnp.zeros((32, 256), F32)
+        for oz in range(3):
+            t = 3 * oy + oz
+            tiled = dot(jnp.concatenate([source[t], source[t + 9], source[t + 18]], axis=0), repeat, NN)
+            for x in range(8):
+                rows = jnp.where(plane == x + 1, tiled[64:], 0.0)
+                rows = jnp.where(plane == x, tiled[32:64], rows)
+                rows = jnp.where(plane == x - 1, tiled[:32], rows)
+                target[t, 32 * x : 32 * x + 32] = rows.astype(BF)
+            before = jnp.where(plane == 2 * oz, tiled[:32], before)
+            after = jnp.where(plane == 2 * oz + 1, tiled[64:], after)
+        edge_target[oy, 0:32] = before.astype(BF)
+        edge_target[oy, 32:224] = jnp.zeros((192, 256), BF)
+        edge_target[oy, 224:256] = after.astype(BF)
 
 
 def by_offset(tall, target):
@@ -231,15 +253,15 @@
             target[i, 32 * x : 32 * x + 32] = tall[pl.ds(16 * x + i, 32, stride=64), :].astype(BF)
 
 
-def prepare_first_kernel(first, down, w1, dwr, tall):
-    banded(first, w1, 0)
+def prepare_first_kernel(first, down, w1, w1_edge, dwr, tall):
+    banded(first, w1, w1_edge, 0)
     tall[...] = down[...].astype(F32)
     by_offset(tall, dwr)
 
 
-def prepare_last_kernel(closing, up, skip_weight, up_weight, wupr, tall):
-    banded(closing, skip_weight, 0)
-    banded(closing, up_weight, 32)
+def prepare_last_kernel(closing, up, skip_weight, skip_edge, up_weight, up_edge, wupr, tall):
+    banded(closing, skip_weight, skip_edge, 0)
+    banded(closing, up_weight, up_edge, 32)
     for k in range(16):
         tall[128 * k : 128 * k + 128] = up[:, 128 * k : 128 * k + 128].astype(F32).T
     by_offset(tall, wupr)
@@ -308,35 +330,37 @@
     )(bounds, own, chips, cores)
     near = swap(to_near, "sx", 0)
     far = swap(to_far, "sx", 1)
-    w1, dwr = call(
-        prepare_first_kernel, [((9, 256, 512), BF), ((16, 128, 128), BF)], [((2048, 128), F32)], 2, False, 1 << 27, 12
+    weight, edge, offsets = ((9, 256, 256), BF), ((3, 256, 256), BF), ((16, 128, 128), BF)
+    w1, w1_edge, dwr = call(
+        prepare_first_kernel, [weight, edge, offsets], [((2048, 128), F32)], 2, False, 1 << 27, 8
     )(w_first, down_weight)
     skip, cells = ((384, 256), BF), ((4, 8, 512), BF)
     skip_near, skip_own, to_far, coarse_own = call(
         near_kernel,
         [skip, skip, cells, ((2, 8, 512), BF)],
-        [((3, 416, 512), BF), ((512, 512), BF)],
-        4,
+        [((2, 3, 416, 256), BF), ((2, 416, 256), BF), ((512, 512), BF)],
+        5,
         True,
         2 << 30,
-        24,
-    )(bounds, own, near, w1, dwr)
+        10,
+    )(bounds, own, near, w1, w1_edge, dwr)
     far_cells = swap(to_far, "sx", 1)
     skip_far, to_near = call(
-        far_kernel, [skip, cells], [((3, 416, 512), BF), ((512, 256), BF)], 5, True, 1 << 30, 24
-    )(bounds, own, far, w1, dwr, coarse_own)
+        far_kernel,
+        [skip, cells],
+        [((1, 3, 416, 256), BF), ((1, 416, 256), BF), ((512, 256), BF)],
+        6,
+        True,
+        1 << 30,
+        10,
+    )(bounds, own, far, w1, w1_edge, dwr, coarse_own)
     near_cells = swap(to_near, "sx", 0)
-    skip_weight, up_weight, wupr = call(
-        prepare_last_kernel,
-        [((9, 256, 512), BF), ((9, 256, 512), BF), ((16, 128, 128), BF)],
-        [((2048, 128), F32)],
-        2,
-        False,
-        1 << 28,
-        16,
+    skip_weight, skip_edge, up_weight, up_edge, wupr = call(
+        prepare_last_kernel, [weight, edge, weight, edge, offsets], [((2048, 128), F32)], 2, False, 1 << 28, 10
     )(closing_weight, w_up)
-    (part,) = call(skip_kernel, [((2, 256, 256), F32)], [((3, 288, 768), BF)], 4, True, 2 << 30, 16)(
-        bounds, skip_near, skip_own, skip_far, skip_weight
+    shifts = [((3, 288, 512), BF), ((2, 288, 256), BF)]
+    (part,) = call(skip_kernel, [((2, 256, 256), F32)], shifts, 5, True, 2 << 30, 8)(
+        bounds, skip_near, skip_own, skip_far, skip_weight, skip_edge
     )
     odd_order = jnp.concatenate([near_cells, to_far[:2], to_near, far_cells], axis=0)
     even_order = jnp.concatenate([far_cells, to_near, to_far[2:], near_cells], axis=0)
@@ -347,17 +371,12 @@
     (result,) = call(
         last_kernel,
         [((32, 16, 256), BF)],
-        [
-            ((3, 224, 512), BF),
-            ((512, 768), F32),
-            ((288, 768), F32),
-            ((3, 288, 768), BF),
-        ],
-        5,
+        [((3, 224, 512), BF), ((512, 768), F32), ((288, 768), F32)] + shifts,
+        6,
         True,
         3 << 30,
-        32,
-    )(bounds, coarse, w_coarse, wupr, up_weight, part)
+        16,
+    )(bounds, coarse, w_coarse, wupr, up_weight, up_edge, part)
     return result
 
 

time: 86 us -> 84 us (0.977)
  Pallas kernels: 24.2 us -> 20.6 us
  waiting for transfers between devices: 36.5 us -> 37.8 us
    pallas_call x5, Pallas kernels: 14.1 us -> 11.3 us  [the longest x1 4.37 us: local(): call(near_kernel, [skip, skip, cells, ((2, 8, 512), BF)], [((2, 3, 416, 2...]
    ppermute x8, waiting for transfers between devices: 36.5 us -> 37.8 us  [swap(): return lax.ppermute(array, axis, pairs + [(j, i) for i, j in pairs])]
  transfers between devices with their start and end apart: 8 -> 8, of which waited for: 6 -> 6; matrix products, arithmetic and copies ran while one was open for 0% -> 0% of each run, Pallas kernels for 13% -> 11%
where the time goes in v7:
time: 84 us; the launch traced here: 83.7 us
  waiting for transfers between devices  37.8 us (45%)
  starting transfers between devices  23 us (27%)
  Pallas kernels  20.6 us (25%)
  local copies, waits for them, and re-layouts  1.13 us (1%)
    ppermute x8, waiting for transfers between devices, swap(): return lax.ppermute(array, axis, pairs + [(j, i) for i, j in pairs])  37.8 us
    ppermute x8, starting transfers between devices, swap(): return lax.ppermute(array, axis, pairs + [(j, i) for i, j in pairs])  23 us
    pallas_call x1, Pallas kernels, local(): call(last_kernel, [((32, 16, 256), BF)], [((3, 224, 512), BF), ((512, 768...  8.65 us
    pallas_call x1, Pallas kernels, local(): call(near_kernel, [skip, skip, cells, ((2, 8, 512), BF)], [((2, 3, 416, 2...  4.37 us
    pallas_call x1, Pallas kernels, local(): call(far_kernel, [skip, cells], [((1, 3, 416, 256), BF), ((1, 416, 256),...  2.28 us
    pallas_call x1, Pallas kernels, local(): call(skip_kernel, [((2, 256, 256), F32)], shifts, 5, True, 2 << 30, 8)  1.84 us
    pallas_call x1, Pallas kernels, local(): call(prepare_last_kernel, [weight, edge, weight, edge, offsets], [((2048,...  1.7 us
  transfers between devices with their start and end apart: 8, of which 6 were waited for; matrix products, arithmetic and copies ran while one was open for 0% of the time, Pallas kernels for 11%

profile of v7, /device:TPU:289, one launch (start us, length us, event | category | flops | bytes accessed | tf_op | source)
XLA Modules:
  0.0 83.7 jit_solution(11600403849550430278)
XLA Ops:
  0.0 0.0 copy-start
  0.0 0.9 %copy-done = bf16[32,16,256]{2,1,0:T(8,128)(2,1)S(1)} copy-done((bf16[32,16,256]{2,1,0:T(8,128)(2,1)S(1)}, bf16[32,16,256]{2,1,0:T(8,128)(2,1)}, u32[]{:S(2)}) %copy-start) | copy-done | bytes 262168
  1.0 0.0 copy-start.1
  1.0 0.0 copy-start.2
  1.0 0.5 fusion.own
  1.5 0.0 copy-start.4
  1.5 0.0 copy-start.5
  1.5 3.3 %collective-permute-start = (bf16[80,512]{1,0:T(8,128)(2,1)S(1)}, bf16[80,512]{1,0:T(8,128)(2,1)S(1)}, u32[]{:S(2)}, u32[]{:S(2)}) collective-permute-start(bf16[80,512]{1,0:T(8,128)(2,1)S(1)} %get-tuple-element.40), channel_id=1, source_target_pairs={{1,2},{3,4},{5,6},{7,8},{9,10},{11,12},{13,14},{2,1},{4,3},{6,5},{... | collective-permute-start | bytes 245768 | tf_op jit(solution)/shard_map/ppermute | solution.py:297
  4.9 1.9 %collective-permute-start.1 = (bf16[80,512]{1,0:T(8,128)(2,1)S(1)}, bf16[80,512]{1,0:T(8,128)(2,1)S(1)}, u32[]{:S(2)}, u32[]{:S(2)}) collective-permute-start(bf16[80,512]{1,0:T(8,128)(2,1)S(1)} %get-tuple-element.39), channel_id=1, source_target_pairs={{0,1},{2,3},{4,5},{6,7},{8,9},{10,11},{12,13},{14,15},{1,0},{3,2},... | collective-permute-start | bytes 245768 | tf_op jit(solution)/shard_map/ppermute | solution.py:297
  6.8 0.1 stack.37.bounds
  6.9 0.8 collective-permute-done.chips
  7.7 0.3 collective-permute-done.1.cores
  8.0 0.7 shard_map.64
  8.7 3.2 %collective-permute-start.3 = (bf16[520,128]{1,0:T(8,128)(2,1)S(1)}, bf16[520,128]{1,0:T(8,128)(2,1)S(1)}, u32[]{:S(2)}, u32[]{:S(2)}) collective-permute-start(bf16[520,128]{1,0:T(8,128)(2,1)S(1)} %get-tuple-element.27), channel_id=1, source_target_pairs={{0,16},{32,48},{64,80},{96,112},{128,144},{160,176},{192,208},{224... | collective-permute-start | bytes 399368 | tf_op jit(solution)/shard_map/ppermute | solution.py:297
  11.9 0.1 pad.3.clone
  12.0 0.0 copy-done.1
  12.0 0.0 copy-done.2
  12.0 1.1 %shard_map.65 = (bf16[9,256,256]{2,1,0:T(8,128)(2,1)S(1)}, bf16[3,256,256]{2,1,0:T(8,128)(2,1)S(1)}, bf16[16,128,128]{2,1,0:T(8,128)(2,1)S(1)}) custom-call(bf16[27,32,32]{2,1,0:T(8,128)(2,1)S(1)} %copy-done.2, bf16[2048,128]{1,0:T(8,128)(2,1)S(1)} %copy-done.1), custom_call_target="tpu_custom_call" | custom-call | flops 134217728 | bytes 4194304 | tf_op jit(solution)/shard_map/pallas_call | solution.py:334
  13.2 0.0 copy-done.4
  13.2 0.0 copy-done.5
  13.2 1.7 %shard_map.68 = (bf16[9,256,256]{2,1,0:T(8,128)(2,1)S(1)}, bf16[3,256,256]{2,1,0:T(8,128)(2,1)S(1)}, bf16[9,256,256]{2,1,0:T(8,128)(2,1)S(1)}, bf16[3,256,256]{2,1,0:T(8,128)(2,1)S(1)}, bf16[16,128,128]{2,1,0:T(8,128)(2,1)S(1)}) custom-call(bf16[27,32,64]{2,1,0:T(8,128)(2,1)S(1)} %copy-done.5, bf16[128,2048]{1,0:T(8,128)(2,1)S(1)} %copy-done.4), custom_call_target="tpu_custom_call" | custom-call | flops 268435456 | bytes 4194304 | tf_op jit(solution)/shard_map/pallas_call | solution.py:358
  14.9 4.2 %collective-permute-start.2 = (bf16[520,128]{1,0:T(8,128)(2,1)S(1)}, bf16[520,128]{1,0:T(8,128)(2,1)S(1)}, u32[]{:S(2)}, u32[]{:S(2)}) collective-permute-start(bf16[520,128]{1,0:T(8,128)(2,1)S(1)} %get-tuple-element.23), channel_id=1, source_target_pairs={{16,32},{48,64},{80,96},{112,128},{144,160},{176,192},{208,224},{2... | collective-permute-start | bytes 399368 | tf_op jit(solution)/shard_map/ppermute | solution.py:297
  19.0 0.0 collective-permute-done.3.near
  19.1 4.4 %shard_map.66 = (bf16[384,256]{1,0:T(8,128)(2,1)S(1)}, bf16[384,256]{1,0:T(8,128)(2,1)S(1)}, bf16[4,8,512]{2,1,0:T(8,128)(2,1)S(1)}, bf16[2,8,512]{2,1,0:T(8,128)(2,1)S(1)}) custom-call(s32[10]{0:T(128)S(1)} %stack.37.bounds, bf16[416,512]{1,0:T(8,128)(2,1)S(1)} %get-tuple-element.22.own, bf16[520,128]{1,0:T(8,128)(2,1)S(1)} %collective-permute-done.3.near, ...), custom_call_target="tpu_custom_call" | custom-call | flops 2147483648 | bytes 4194304 | tf_op jit(solution)/shard_map/pallas_call | solution.py:338
  23.4 19.5 %collective-permute-done.2.far = bf16[520,128]{1,0:T(8,128)(2,1)S(1)} collective-permute-done((bf16[520,128]{1,0:T(8,128)(2,1)S(1)}, bf16[520,128]{1,0:T(8,128)(2,1)S(1)}, u32[]{:S(2)}, u32[]{:S(2)}) %collective-permute-start.2) | collective-permute-done | bytes 133152 | tf_op jit(solution)/shard_map/ppermute | solution.py:297
  42.9 2.3 %shard_map.67 = (bf16[384,256]{1,0:T(8,128)(2,1)S(1)}, bf16[4,8,512]{2,1,0:T(8,128)(2,1)S(1)}) custom-call(s32[10]{0:T(128)S(1)} %stack.37.bounds, bf16[416,512]{1,0:T(8,128)(2,1)S(1)} %get-tuple-element.22.own, bf16[520,128]{1,0:T(8,128)(2,1)S(1)} %collective-permute-done.2.far, bf16[9,256,256]{2,1,0:T(8,128)(2,1)S(1)} %get-tuple-element.24.w1, ...), custom_call_target="tpu_custom_call" | custom-call | flops 1073741824 | bytes 4194304 | tf_op jit(solution)/shard_map/pallas_call | solution.py:348
  45.2 1.9 %collective-permute-start.4 = (bf16[4,8,512]{2,1,0:T(8,128)(2,1)S(1)}, bf16[4,8,512]{2,1,0:T(8,128)(2,1)S(1)}, u32[]{:S(2)}, u32[]{:S(2)}) collective-permute-start(bf16[4,8,512]{2,1,0:T(8,128)(2,1)S(1)} %get-tuple-element.29), channel_id=1, source_target_pairs={{0,16},{32,48},{64,80},{96,112},{128,144},{160,176},{192,208},{224... | collective-permute-start | bytes 98312 | tf_op jit(solution)/shard_map/ppermute | solution.py:297
  47.2 1.9 %collective-permute-start.5 = (bf16[4,8,512]{2,1,0:T(8,128)(2,1)S(1)}, bf16[4,8,512]{2,1,0:T(8,128)(2,1)S(1)}, u32[]{:S(2)}, u32[]{:S(2)}) collective-permute-start(bf16[4,8,512]{2,1,0:T(8,128)(2,1)S(1)} %get-tuple-element.30), channel_id=1, source_target_pairs={{16,32},{48,64},{80,96},{112,128},{144,160},{176,192},{208,224},{2... | collective-permute-start | bytes 98312 | tf_op jit(solution)/shard_map/ppermute | solution.py:297
  49.1 0.8 collective-permute-done.4
  49.9 14.9 %collective-permute-done.5 = bf16[4,8,512]{2,1,0:T(8,128)(2,1)S(1)} collective-permute-done((bf16[4,8,512]{2,1,0:T(8,128)(2,1)S(1)}, bf16[4,8,512]{2,1,0:T(8,128)(2,1)S(1)}, u32[]{:S(2)}, u32[]{:S(2)}) %collective-permute-start.5) | collective-permute-done | bytes 32800 | tf_op jit(solution)/shard_map/ppermute | solution.py:297
  64.8 0.1 broadcast_select_fusion.5
  64.9 4.5 %collective-permute-start.6 = (bf16[14,4,512]{2,1,0:T(4,128)(2,1)S(1)}, bf16[14,4,512]{2,1,0:T(4,128)(2,1)S(1)}, u32[]{:S(2)}, u32[]{:S(2)}) collective-permute-start(bf16[14,4,512]{2,1,0:T(4,128)(2,1)S(1)} %get-tuple-element.43), channel_id=1, source_target_pairs={{0,1},{2,3},{4,5},{6,7},{8,9},{10,11},{12,13},{14,15},{1,0},{3,2},... | collective-permute-start | bytes 172040 | tf_op jit(solution)/shard_map/ppermute | solution.py:297
  69.3 2.1 %collective-permute-start.7 = (bf16[14,4,512]{2,1,0:T(4,128)(2,1)S(1)}, bf16[14,4,512]{2,1,0:T(4,128)(2,1)S(1)}, u32[]{:S(2)}, u32[]{:S(2)}) collective-permute-start(bf16[14,4,512]{2,1,0:T(4,128)(2,1)S(1)} %get-tuple-element.44), channel_id=1, source_target_pairs={{1,2},{3,4},{5,6},{7,8},{9,10},{11,12},{13,14},{2,1},{4,3},{6,5},{... | collective-permute-start | bytes 172040 | tf_op jit(solution)/shard_map/ppermute | solution.py:297
  71.4 0.0 copy-start.3
  71.5 1.8 %shard_map.69.part_ref = f32[2,256,256]{2,1,0:T(8,128)S(1)} custom-call(s32[10]{0:T(128)S(1)} %stack.37.bounds, bf16[384,256]{1,0:T(8,128)(2,1)S(1)} %get-tuple-element.34.near, bf16[384,256]{1,0:T(8,128)(2,1)S(1)} %get-tuple-element.35.own, bf16[384,256]{1,0:T(8,128)(2,1)S(1)} %get-tuple-element.36.far, bf16[9,256,256]{2,1,0:T(8,128)(2,1)S(1)} %get-tuple-element.37.weight, ...), custom_call_target="tpu_custom_call" | custom-call | flops 2147483648 | bytes 4194304 | tf_op jit(solution)/shard_map/pallas_call | solution.py:362
  73.3 0.0 collective-permute-done.6
  73.3 1.5 %collective-permute-done.7 = bf16[14,4,512]{2,1,0:T(4,128)(2,1)S(1)} collective-permute-done((bf16[14,4,512]{2,1,0:T(4,128)(2,1)S(1)}, bf16[14,4,512]{2,1,0:T(4,128)(2,1)S(1)}, u32[]{:S(2)}, u32[]{:S(2)}) %collective-permute-start.7) | collective-permute-done | bytes 57376 | tf_op jit(solution)/shard_map/ppermute | solution.py:297
  74.9 0.1 maximum_maximum_fusion.coarse_ref
  75.0 0.0 copy-done.3
  75.0 8.7 %shard_map.70 = bf16[32,16,256]{2,1,0:T(8,128)(2,1)} custom-call(s32[10]{0:T(128)S(1)} %stack.37.bounds, bf16[14,16,512]{2,1,0:T(8,128)(2,1)S(1)} %maximum_maximum_fusion.coarse_ref, bf16[4,27,128,128]{3,2,1,0:T(8,128)(2,1)S(1)} %copy-done.3, bf16[16,128,128]{2,1,0:T(8,128)(2,1)S(1)} %get-tuple-element.31.wupr, ...), custom_call_target="tpu_custom_call" | custom-call | flops 3221225472 | bytes 4194304 | tf_op jit(solution)/shard_map/pallas_call | solution.py:371
  (7 shorter events, 0.1 us)
Async XLA Ops:
  0.0 1.0 %copy-start = (bf16[32,16,256]{2,1,0:T(8,128)(2,1)S(1)}, bf16[32,16,256]{2,1,0:T(8,128)(2,1)}, u32[]{:S(2)}) copy-start(bf16[32,16,256]{2,1,0:T(8,128)(2,1)} %param.6) | copy-start | bytes 786436
  1.0 11.1 %copy-start.1 = (bf16[2048,128]{1,0:T(8,128)(2,1)S(1)}, bf16[2048,128]{1,0:T(8,128)(2,1)}, u32[]{:S(2)}) copy-start(bf16[2048,128]{1,0:T(8,128)(2,1)} %down.1) | copy-start | bytes 1572868
  1.0 11.1 %copy-start.2 = (bf16[27,32,32]{2,1,0:T(8,128)(2,1)S(1)}, bf16[27,32,32]{2,1,0:T(8,128)(2,1)}, u32[]{:S(2)}) copy-start(bf16[27,32,32]{2,1,0:T(8,128)(2,1)} %first.1) | copy-start | bytes 165892
  1.5 11.7 %copy-start.4 = (bf16[128,2048]{1,0:T(8,128)(2,1)S(1)}, bf16[128,2048]{1,0:T(8,128)(2,1)}, u32[]{:S(2)}) copy-start(bf16[128,2048]{1,0:T(8,128)(2,1)} %up.1) | copy-start | bytes 1572868
  1.5 11.7 %copy-start.5 = (bf16[27,32,64]{2,1,0:T(8,128)(2,1)S(1)}, bf16[27,32,64]{2,1,0:T(8,128)(2,1)}, u32[]{:S(2)}) copy-start(bf16[27,32,64]{2,1,0:T(8,128)(2,1)} %closing.1) | copy-start | bytes 331780
  1.5 6.2 %collective-permute-start = (bf16[80,512]{1,0:T(8,128)(2,1)S(1)}, bf16[80,512]{1,0:T(8,128)(2,1)S(1)}, u32[]{:S(2)}, u32[]{:S(2)}) collective-permute-start(bf16[80,512]{1,0:T(8,128)(2,1)S(1)} %get-tuple-element.40), channel_id=1, source_target_pairs={{1,2},{3,4},{5,6},{7,8},{9,10},{11,12},{13,14},{2,1},{4,3},{6,5},{... | collective-permute-start | bytes 245768 | tf_op jit(solution)/shard_map/ppermute | solution.py:297
  4.9 3.2 %collective-permute-start.1 = (bf16[80,512]{1,0:T(8,128)(2,1)S(1)}, bf16[80,512]{1,0:T(8,128)(2,1)S(1)}, u32[]{:S(2)}, u32[]{:S(2)}) collective-permute-start(bf16[80,512]{1,0:T(8,128)(2,1)S(1)} %get-tuple-element.39), channel_id=1, source_target_pairs={{0,1},{2,3},{4,5},{6,7},{8,9},{10,11},{12,13},{14,15},{1,0},{3,2},... | collective-permute-start | bytes 245768 | tf_op jit(solution)/shard_map/ppermute | solution.py:297
  8.7 10.3 %collective-permute-start.3 = (bf16[520,128]{1,0:T(8,128)(2,1)S(1)}, bf16[520,128]{1,0:T(8,128)(2,1)S(1)}, u32[]{:S(2)}, u32[]{:S(2)}) collective-permute-start(bf16[520,128]{1,0:T(8,128)(2,1)S(1)} %get-tuple-element.27), channel_id=1, source_target_pairs={{0,16},{32,48},{64,80},{96,112},{128,144},{160,176},{192,208},{224... | collective-permute-start | bytes 399368 | tf_op jit(solution)/shard_map/ppermute | solution.py:297
  14.9 28.1 %collective-permute-start.2 = (bf16[520,128]{1,0:T(8,128)(2,1)S(1)}, bf16[520,128]{1,0:T(8,128)(2,1)S(1)}, u32[]{:S(2)}, u32[]{:S(2)}) collective-permute-start(bf16[520,128]{1,0:T(8,128)(2,1)S(1)} %get-tuple-element.23), channel_id=1, source_target_pairs={{16,32},{48,64},{80,96},{112,128},{144,160},{176,192},{208,224},{2... | collective-permute-start | bytes 399368 | tf_op jit(solution)/shard_map/ppermute | solution.py:297
  45.2 4.7 %collective-permute-start.4 = (bf16[4,8,512]{2,1,0:T(8,128)(2,1)S(1)}, bf16[4,8,512]{2,1,0:T(8,128)(2,1)S(1)}, u32[]{:S(2)}, u32[]{:S(2)}) collective-permute-start(bf16[4,8,512]{2,1,0:T(8,128)(2,1)S(1)} %get-tuple-element.29), channel_id=1, source_target_pairs={{0,16},{32,48},{64,80},{96,112},{128,144},{160,176},{192,208},{224... | collective-permute-start | bytes 98312 | tf_op jit(solution)/shard_map/ppermute | solution.py:297
  47.2 17.6 %collective-permute-start.5 = (bf16[4,8,512]{2,1,0:T(8,128)(2,1)S(1)}, bf16[4,8,512]{2,1,0:T(8,128)(2,1)S(1)}, u32[]{:S(2)}, u32[]{:S(2)}) collective-permute-start(bf16[4,8,512]{2,1,0:T(8,128)(2,1)S(1)} %get-tuple-element.30), channel_id=1, source_target_pairs={{16,32},{48,64},{80,96},{112,128},{144,160},{176,192},{208,224},{2... | collective-permute-start | bytes 98312 | tf_op jit(solution)/shard_map/ppermute | solution.py:297
  64.9 8.5 %collective-permute-start.6 = (bf16[14,4,512]{2,1,0:T(4,128)(2,1)S(1)}, bf16[14,4,512]{2,1,0:T(4,128)(2,1)S(1)}, u32[]{:S(2)}, u32[]{:S(2)}) collective-permute-start(bf16[14,4,512]{2,1,0:T(4,128)(2,1)S(1)} %get-tuple-element.43), channel_id=1, source_target_pairs={{0,1},{2,3},{4,5},{6,7},{8,9},{10,11},{12,13},{14,15},{1,0},{3,2},... | collective-permute-start | bytes 172040 | tf_op jit(solution)/shard_map/ppermute | solution.py:297
  69.3 5.5 %collective-permute-start.7 = (bf16[14,4,512]{2,1,0:T(4,128)(2,1)S(1)}, bf16[14,4,512]{2,1,0:T(4,128)(2,1)S(1)}, u32[]{:S(2)}, u32[]{:S(2)}) collective-permute-start(bf16[14,4,512]{2,1,0:T(4,128)(2,1)S(1)} %get-tuple-element.44), channel_id=1, source_target_pairs={{1,2},{3,4},{5,6},{7,8},{9,10},{11,12},{13,14},{2,1},{4,3},{6,5},{... | collective-permute-start | bytes 172040 | tf_op jit(solution)/shard_map/ppermute | solution.py:297
  71.4 3.6 %copy-start.3 = (bf16[4,27,128,128]{3,2,1,0:T(8,128)(2,1)S(1)}, bf16[4,27,128,128]{3,2,1,0:T(8,128)(2,1)}, u32[]{:S(2)}) copy-start(bf16[4,27,128,128]{3,2,1,0:T(8,128)(2,1)} %w_coarse.1) | copy-start | bytes 10616836

commit v8 on v7

--- a/solution.py
+++ b/solution.py
@@ -1,5 +1,6 @@
 import jax
 import jax.numpy as jnp
+import numpy as np
 from jax import lax
 from jax.experimental import pallas as pl
 from jax.experimental.pallas import tpu as pltpu
@@ -28,13 +29,11 @@
     return before, value, after
 
 
-def regroup(rows, columns, row_dim, first):
-    coarse = iota((rows, columns), row_dim)
-    fine = iota((rows, columns), 1 - row_dim)
-    offset = coarse >> 5
-    y = 4 * (coarse & 7) + (offset >> 2)
-    z = 4 * ((coarse >> 3) & 3) + (offset & 3)
-    return jnp.where(fine == (y - first) * NZ + z, 1.0, 0.0).astype(BF)
+def regroup():
+    coarse, fine = np.arange(512)[:, None], np.arange(384)[None]
+    y = 4 * (coarse & 7) + (coarse >> 7)
+    z = 4 * (coarse >> 3 & 3) + (coarse >> 5 & 3)
+    return fine == y * NZ + z
 
 
 def moved(value, start, target):
@@ -86,8 +85,7 @@
     target[:, 128:256] = pltpu.roll(high, 32, 1).astype(BF)
 
 
-def fine_groups(windows, bounds, w1, w1_edge, dwr, skip_refs, coarse_refs, vz, edges, grouped):
-    to_groups = regroup(512, 384, 0, 0)
+def fine_groups(windows, bounds, to_groups, w1, w1_edge, dwr, skip_refs, coarse_refs, vz, edges, grouped):
     y = (iota((384, 256), 0) >> 4) - 4
     plane = iota((384, 256), 1) >> 5
     y_inside = (y >= bounds[2]) & (y <= bounds[3])
@@ -105,7 +103,7 @@
         inside = y_inside & (x >= bounds[0]) & (x <= bounds[1])
         skip = jnp.where(inside, jnp.maximum(summed, 0.0), 0.0).astype(BF)
         skip_refs[k][...] = skip
-        grouped[:, 256 * k : 256 * k + 256] = dot(to_groups, skip, NN).astype(BF)
+        grouped[:, 256 * k : 256 * k + 256] = dot(to_groups[...], skip, NN).astype(BF)
     count = 2 * len(windows)
     coarse = jnp.zeros((32 * count, 128), F32)
     for i in range(0, 16, 2):
@@ -125,20 +123,25 @@
                 target[first_a + a % 2, :, 128 * z : 128 * z + 128] = cell
 
 
-def near_kernel(bounds, own, near, w1, w1_edge, dwr, skip_near, skip_own, to_far, coarse_own, vz, edges, grouped):
-    odd = bounds[8] == 1
-    first_near, first_own = 2 - 2 * bounds[8], 2 * bounds[8]
-    windows = ((side_window(own, near, odd), jnp.where(odd, -4, 12)), (own_window(own), 4))
-    coarse = ([(to_far, first_near)], [(to_far, first_own), (coarse_own, 0)])
-    fine_groups(windows, bounds, w1, w1_edge, dwr, (skip_near, skip_own), coarse, vz, edges, grouped)
-
-
-def far_kernel(bounds, own, far, w1, w1_edge, dwr, coarse_own, skip_far, to_near, vz, edges, grouped):
-    to_near[pl.ds(2 - 2 * bounds[8], 2)] = coarse_own[...]
-    even = bounds[8] == 0
-    windows = ((side_window(own, far, even), jnp.where(even, -4, 12)),)
-    coarse = ([(to_near, 2 * bounds[8])],)
-    fine_groups(windows, bounds, w1, w1_edge, dwr, (skip_far,), coarse, vz, edges, grouped)
+def own_kernel(bounds, own, groups, w1, w1_edge, dwr, skip_own, coarse_own, vz, edges, grouped):
+    coarse = ([(coarse_own, 0)],)
+    windows = ((own_window(own), 4),)
+    fine_groups(windows, bounds, groups, w1, w1_edge, dwr, (skip_own,), coarse, vz, edges, grouped)
+
+
+def side_kernel(at_left, bounds, own, halo, groups, w1, w1_edge, dwr, coarse_own, skip, cells, vz, edges, grouped):
+    cells[pl.ds(2 * at_left, 2)] = coarse_own[...]
+    windows = ((side_window(own, halo, at_left == 1), 12 - 16 * at_left),)
+    coarse = ([(cells, 2 - 2 * at_left)],)
+    fine_groups(windows, bounds, groups, w1, w1_edge, dwr, (skip,), coarse, vz, edges, grouped)
+
+
+def near_kernel(bounds, *refs):
+    side_kernel(bounds[8], bounds, *refs)
+
+
+def far_kernel(bounds, *refs):
+    side_kernel(1 - bounds[8], bounds, *refs)
 
 
 def fill_shifts(tile_of, middle, edges):
@@ -176,15 +179,35 @@
 
 
 def last_kernel(
-    bounds, coarse_ref, w_coarse, wupr, weight, weight_edge, part_ref, out_ref, state, raw, up, middle_ref, edges
+    bounds,
+    coarse_ref,
+    w_coarse,
+    wupr,
+    from_groups,
+    weight,
+    weight_edge,
+    part_ref,
+    out_ref,
+    state,
+    narrow,
+    raw,
+    up,
+    middle_ref,
+    edges,
 ):
     value = coarse_ref[...].reshape(224, 512).astype(F32)
     for layer in range(4):
-        rows_in = (14 - 2 * layer) * 16
-        rows = rows_in - 32
-        state[0, :rows_in] = value.astype(BF)
-        state[1, :rows_in] = pltpu.roll(value, rows_in - 1, 0).astype(BF)
-        state[2, :rows_in] = pltpu.roll(value, rows_in - 2, 0).astype(BF)
+        span = 12 - 2 * layer
+        width = 16 if layer < 2 else 8
+        for ob in range(3):
+            shifted = pltpu.roll(value, value.shape[0] - ob, 0) if ob else value
+            if layer == 2:
+                shifted = jnp.concatenate([shifted[16 * a : 16 * a + 8] for a in range(10)], axis=0)
+            if layer < 2:
+                state[ob, : 16 * (span + 2)] = shifted.astype(BF)
+            else:
+                narrow[ob, : 8 * (span + 2)] = shifted
+        rows = span * width
         low = jnp.zeros((rows, 256), F32)
         high = jnp.zeros((rows, 256), F32)
         zero = jnp.zeros((128, 128), BF)
@@ -194,17 +217,28 @@
                 middle = jnp.concatenate(w, axis=1)
                 w_low = jnp.concatenate([jnp.concatenate([w[1], w[2], zero], axis=1), middle], axis=0)
                 w_high = jnp.concatenate([middle, jnp.concatenate([zero, w[0], w[1]], axis=1)], axis=0)
-                low += dot(state[ob, 16 * oa : 16 * oa + rows, 0:384], w_low, NT)
-                high += dot(state[ob, 16 * oa : 16 * oa + rows, 128:512], w_high, NT)
-        index = iota((rows, 512), 0)
-        a = (index >> 4) - 4 + layer
-        b = index & 15
-        kept = (a >= bounds[4]) & (a <= bounds[5]) & (b < 12 - 2 * layer)
-        kept = kept & (b - 4 + layer >= bounds[6]) & (b - 4 + layer <= bounds[7])
-        value = jnp.where(kept, jnp.maximum(jnp.concatenate([low, high], axis=1), 0.0), 0.0)
+                if layer < 2:
+                    cells = state[ob, 16 * oa : 16 * oa + rows]
+                else:
+                    cells = narrow[ob, 8 * oa : 8 * oa + rows].astype(BF)
+                low += dot(cells[:, 0:384], w_low, NT)
+                high += dot(cells[:, 128:512], w_high, NT)
+        index = iota((rows, 128), 0)
+        a = index // width - 4 + layer
+        b = index % width - 4 + layer
+        kept = (a >= bounds[4]) & (a <= bounds[5]) & (b < 8 - layer)
+        kept = kept & (b >= bounds[6]) & (b <= bounds[7])
+        value = jnp.concatenate(
+            [
+                jnp.where(kept, jnp.maximum(half[:, side : side + 128], 0.0), 0.0)
+                for half in (low, high)
+                for side in (0, 128)
+            ],
+            axis=1,
+        )
         value = value.astype(BF).astype(F32)
     cells = jnp.concatenate(
-        [value[16 * a : 16 * a + 8, 128 * z : 128 * z + 128] for z in range(4) for a in range(6)], axis=0
+        [value[8 * a : 8 * a + 8, 128 * z : 128 * z + 128] for z in range(4) for a in range(6)], axis=0
     ).astype(BF)
     for i in range(0, 16, 2):
         pair = dot(cells, jnp.concatenate([wupr[i], wupr[i + 1]], axis=0), NT)
@@ -214,9 +248,8 @@
                     raw[32 * (i + half) + 8 * z : 32 * (i + half) + 8 * z + 8, 128 * a : 128 * a + 128] = pair[
                         48 * z + 8 * a : 48 * z + 8 * a + 8, 128 * half : 128 * half + 128
                     ]
-    from_groups = regroup(288, 512, 1, 3)
     for g in range(3):
-        up[:, 256 * g : 256 * g + 256] = dot(from_groups, raw[:, 256 * g : 256 * g + 256].astype(BF), NN)
+        up[:, 256 * g : 256 * g + 256] = dot(from_groups[...], raw[:, 256 * g : 256 * g + 256].astype(BF), NN)
     fill_shifts(lambda tile: up[:, 128 * tile : 128 * tile + 128], middle_ref, edges)
     row, column = iota((256, 256), 0), iota((256, 256), 1)
     to_channels = jnp.where(column == ((row & 7) << 5) + (row >> 3), 1.0, 0.0).astype(BF)
@@ -328,32 +361,25 @@
     own, to_near, to_far = call(
         pack_kernel, [((416, 512), BF), ((520, 128), BF), ((520, 128), BF)], [], 3, True, 1 << 20, 8
     )(bounds, own, chips, cores)
+    far = swap(to_far, "sx", 1)
     near = swap(to_near, "sx", 0)
-    far = swap(to_far, "sx", 1)
     weight, edge, offsets = ((9, 256, 256), BF), ((3, 256, 256), BF), ((16, 128, 128), BF)
     w1, w1_edge, dwr = call(
         prepare_first_kernel, [weight, edge, offsets], [((2048, 128), F32)], 2, False, 1 << 27, 8
     )(w_first, down_weight)
     skip, cells = ((384, 256), BF), ((4, 8, 512), BF)
-    skip_near, skip_own, to_far, coarse_own = call(
-        near_kernel,
-        [skip, skip, cells, ((2, 8, 512), BF)],
-        [((2, 3, 416, 256), BF), ((2, 416, 256), BF), ((512, 512), BF)],
-        5,
-        True,
-        2 << 30,
-        10,
-    )(bounds, own, near, w1, w1_edge, dwr)
+    groups = jnp.asarray(regroup(), BF)
+    scratch = [((1, 3, 416, 256), BF), ((1, 416, 256), BF), ((512, 256), BF)]
+    skip_own, coarse_own = call(own_kernel, [skip, ((2, 8, 512), BF)], scratch, 5, True, 1 << 30, 10)(
+        bounds, own, groups, w1, w1_edge, dwr
+    )
+    skip_near, to_far = call(near_kernel, [skip, cells], scratch, 7, True, 1 << 30, 10)(
+        bounds, own, near, groups, w1, w1_edge, dwr, coarse_own
+    )
     far_cells = swap(to_far, "sx", 1)
-    skip_far, to_near = call(
-        far_kernel,
-        [skip, cells],
-        [((1, 3, 416, 256), BF), ((1, 416, 256), BF), ((512, 256), BF)],
-        6,
-        True,
-        1 << 30,
-        10,
-    )(bounds, own, far, w1, w1_edge, dwr, coarse_own)
+    skip_far, to_near = call(far_kernel, [skip, cells], scratch, 7, True, 1 << 30, 10)(
+        bounds, own, far, groups, w1, w1_edge, dwr, coarse_own
+    )
     near_cells = swap(to_near, "sx", 0)
     skip_weight, skip_edge, up_weight, up_edge, wupr = call(
         prepare_last_kernel, [weight, edge, weight, edge, offsets], [((2048, 128), F32)], 2, False, 1 << 28, 10
@@ -371,12 +397,12 @@
     (result,) = call(
         last_kernel,
         [((32, 16, 256), BF)],
-        [((3, 224, 512), BF), ((512, 768), F32), ((288, 768), F32)] + shifts,
-        6,
+        [((3, 224, 512), BF), ((3, 80, 512), F32), ((512, 768), F32), ((288, 768), F32)] + shifts,
+        7,
         True,
         3 << 30,
         16,
-    )(bounds, coarse, w_coarse, wupr, up_weight, up_edge, part)
+    )(bounds, coarse, w_coarse, wupr, jnp.asarray(regroup().T[48:336], BF), up_weight, up_edge, part)
     return result
 
 

time: 84 us -> 80.7 us (0.961)
  the two profiles are of different devices: /device:TPU:289 before, /device:TPU:127 now
where the time goes in v8:
time: 80.7 us; the launch traced here: 80.4 us
  starting transfers between devices  50.4 us (62%)
  Pallas kernels  20.6 us (26%)
  waiting for transfers between devices  7.08 us (9%)
  local copies, waits for them, and re-layouts  1.14 us (1%)
    ppermute x8, starting transfers between devices, swap(): return lax.ppermute(array, axis, pairs + [(j, i) for i, j in pairs])  50.4 us
    pallas_call x1, Pallas kernels, local(): call(last_kernel, [((32, 16, 256), BF)], [((3, 224, 512), BF), ((3, 80, 5...  8.65 us
    ppermute x8, waiting for transfers between devices, swap(): return lax.ppermute(array, axis, pairs + [(j, i) for i, j in pairs])  7.08 us
    pallas_call x1, Pallas kernels, local(): call(near_kernel, [skip, cells], scratch, 7, True, 1 << 30, 10)  2.24 us
    pallas_call x1, Pallas kernels, local(): call(far_kernel, [skip, cells], scratch, 7, True, 1 << 30, 10)  2.23 us
    pallas_call x1, Pallas kernels, local(): call(own_kernel, [skip, ((2, 8, 512), BF)], scratch, 5, True, 1 << 30, 10)  2.14 us
    pallas_call x1, Pallas kernels, local(): call(skip_kernel, [((2, 256, 256), F32)], shifts, 5, True, 2 << 30, 8)  1.84 us
    pallas_call x1, Pallas kernels, local(): call(prepare_last_kernel, [weight, edge, weight, edge, offsets], [((2048,...  1.69 us
  transfers between devices with their start and end apart: 8, of which 4 were waited for; matrix products, arithmetic and copies ran while one was open for 0% of the time, Pallas kernels for 14%

profile of v8, /device:TPU:127, one launch (start us, length us, event | category | flops | bytes accessed | tf_op | source)
XLA Modules:
  0.0 80.4 jit_solution(10489954946147913306)
XLA Ops:
  0.0 0.0 copy-start
  0.0 0.9 %copy-done = bf16[32,16,256]{2,1,0:T(8,128)(2,1)S(1)} copy-done((bf16[32,16,256]{2,1,0:T(8,128)(2,1)S(1)}, bf16[32,16,256]{2,1,0:T(8,128)(2,1)}, u32[]{:S(2)}) %copy-start) | copy-done | bytes 262168
  1.0 0.0 copy-start.1
  1.0 0.0 copy-start.2
  1.0 0.5 fusion.own
  1.5 0.0 copy-start.4
  1.5 0.0 copy-start.5
  1.5 0.0 copy-start.6
  1.5 5.4 %collective-permute-start = (bf16[80,512]{1,0:T(8,128)(2,1)S(1)}, bf16[80,512]{1,0:T(8,128)(2,1)S(1)}, u32[]{:S(2)}, u32[]{:S(2)}) collective-permute-start(bf16[80,512]{1,0:T(8,128)(2,1)S(1)} %get-tuple-element.40), channel_id=1, source_target_pairs={{1,2},{3,4},{5,6},{7,8},{9,10},{11,12},{13,14},{2,1},{4,3},{6,5},{... | collective-permute-start | bytes 245768 | tf_op jit(solution)/shard_map/ppermute | solution.py:330
  7.0 1.9 %collective-permute-start.1 = (bf16[80,512]{1,0:T(8,128)(2,1)S(1)}, bf16[80,512]{1,0:T(8,128)(2,1)S(1)}, u32[]{:S(2)}, u32[]{:S(2)}) collective-permute-start(bf16[80,512]{1,0:T(8,128)(2,1)S(1)} %get-tuple-element.39), channel_id=1, source_target_pairs={{0,1},{2,3},{4,5},{6,7},{8,9},{10,11},{12,13},{14,15},{1,0},{3,2},... | collective-permute-start | bytes 245768 | tf_op jit(solution)/shard_map/ppermute | solution.py:330
  8.9 0.1 pad.3.clone
  9.0 0.1 stack.37.bounds
  9.1 0.0 collective-permute-done.chips
  9.1 1.0 %collective-permute-done.1.cores = bf16[80,512]{1,0:T(8,128)(2,1)S(1)} collective-permute-done((bf16[80,512]{1,0:T(8,128)(2,1)S(1)}, bf16[80,512]{1,0:T(8,128)(2,1)S(1)}, u32[]{:S(2)}, u32[]{:S(2)}) %collective-permute-start.1) | collective-permute-done | bytes 81952 | tf_op jit(solution)/shard_map/ppermute | solution.py:330
  10.1 0.7 shard_map.82
  10.8 10.8 %collective-permute-start.2 = (bf16[520,128]{1,0:T(8,128)(2,1)S(1)}, bf16[520,128]{1,0:T(8,128)(2,1)S(1)}, u32[]{:S(2)}, u32[]{:S(2)}) collective-permute-start(bf16[520,128]{1,0:T(8,128)(2,1)S(1)} %get-tuple-element.23), channel_id=1, source_target_pairs={{16,32},{48,64},{80,96},{112,128},{144,160},{176,192},{208,224},{2... | collective-permute-start | bytes 399368 | tf_op jit(solution)/shard_map/ppermute | solution.py:330
  21.6 0.0 copy-done.1
  21.7 0.0 copy-done.2
  21.7 1.1 %shard_map.83 = (bf16[9,256,256]{2,1,0:T(8,128)(2,1)S(1)}, bf16[3,256,256]{2,1,0:T(8,128)(2,1)S(1)}, bf16[16,128,128]{2,1,0:T(8,128)(2,1)S(1)}) custom-call(bf16[27,32,32]{2,1,0:T(8,128)(2,1)S(1)} %copy-done.2, bf16[2048,128]{1,0:T(8,128)(2,1)S(1)} %copy-done.1), custom_call_target="tpu_custom_call" | custom-call | flops 134217728 | bytes 4194304 | tf_op jit(solution)/shard_map/pallas_call | solution.py:367
  22.8 0.0 copy-done.4
  22.8 0.0 copy-done.5
  22.8 1.7 %shard_map.87 = (bf16[9,256,256]{2,1,0:T(8,128)(2,1)S(1)}, bf16[3,256,256]{2,1,0:T(8,128)(2,1)S(1)}, bf16[9,256,256]{2,1,0:T(8,128)(2,1)S(1)}, bf16[3,256,256]{2,1,0:T(8,128)(2,1)S(1)}, bf16[16,128,128]{2,1,0:T(8,128)(2,1)S(1)}) custom-call(bf16[27,32,64]{2,1,0:T(8,128)(2,1)S(1)} %copy-done.5, bf16[128,2048]{1,0:T(8,128)(2,1)S(1)} %copy-done.4), custom_call_target="tpu_custom_call" | custom-call | flops 268435456 | bytes 4194304 | tf_op jit(solution)/shard_map/pallas_call | solution.py:384
  24.5 1.9 %collective-permute-start.4 = (bf16[520,128]{1,0:T(8,128)(2,1)S(1)}, bf16[520,128]{1,0:T(8,128)(2,1)S(1)}, u32[]{:S(2)}, u32[]{:S(2)}) collective-permute-start(bf16[520,128]{1,0:T(8,128)(2,1)S(1)} %get-tuple-element.29), channel_id=1, source_target_pairs={{0,16},{32,48},{64,80},{96,112},{128,144},{160,176},{192,208},{224... | collective-permute-start | bytes 399368 | tf_op jit(solution)/shard_map/ppermute | solution.py:330
  26.4 0.0 copy-done.6
  26.5 2.1 %shard_map.84 = (bf16[384,256]{1,0:T(8,128)(2,1)S(1)}, bf16[2,8,512]{2,1,0:T(8,128)(2,1)S(1)}) custom-call(s32[10]{0:T(128)S(1)} %stack.37.bounds, bf16[416,512]{1,0:T(8,128)(2,1)S(1)} %get-tuple-element.22.own.refs_0_, bf16[512,384]{1,0:T(8,128)(2,1)S(1)} %copy-done.6, bf16[9,256,256]{2,1,0:T(8,128)(2,1)S(1)} %get-tuple-element.24.w1.refs_3_, ...), custom_call_target="tpu_custom_call" | custom-call | flops 1073741824 | bytes 4194304 | tf_op jit(solution)/shard_map/pallas_call | solution.py:373
  28.6 2.1 %collective-permute-done.2.refs_1_ = bf16[520,128]{1,0:T(8,128)(2,1)S(1)} collective-permute-done((bf16[520,128]{1,0:T(8,128)(2,1)S(1)}, bf16[520,128]{1,0:T(8,128)(2,1)S(1)}, u32[]{:S(2)}, u32[]{:S(2)}) %collective-permute-start.2) | collective-permute-done | bytes 133152 | tf_op jit(solution)/shard_map/ppermute | solution.py:330
  30.7 2.2 %shard_map.85 = (bf16[384,256]{1,0:T(8,128)(2,1)S(1)}, bf16[4,8,512]{2,1,0:T(8,128)(2,1)S(1)}) custom-call(s32[10]{0:T(128)S(1)} %stack.37.bounds, bf16[416,512]{1,0:T(8,128)(2,1)S(1)} %get-tuple-element.22.own.refs_0_, bf16[520,128]{1,0:T(8,128)(2,1)S(1)} %collective-permute-done.2.refs_1_, bf16[512,384]{1,0:T(8,128)(2,1)S(1)} %copy-done.6, ...), custom_call_target="tpu_custom_call" | custom-call | flops 1073741824 | bytes 4194304 | tf_op jit(solution)/shard_map/pallas_call | solution.py:380
  32.9 1.9 %collective-permute-start.3 = (bf16[4,8,512]{2,1,0:T(8,128)(2,1)S(1)}, bf16[4,8,512]{2,1,0:T(8,128)(2,1)S(1)}, u32[]{:S(2)}, u32[]{:S(2)}) collective-permute-start(bf16[4,8,512]{2,1,0:T(8,128)(2,1)S(1)} %get-tuple-element.28), channel_id=1, source_target_pairs={{0,16},{32,48},{64,80},{96,112},{128,144},{160,176},{192,208},{224... | collective-permute-start | bytes 98312 | tf_op jit(solution)/shard_map/ppermute | solution.py:330
  34.8 0.0 collective-permute-done.4.refs_1_
  34.8 2.2 %shard_map.86 = (bf16[384,256]{1,0:T(8,128)(2,1)S(1)}, bf16[4,8,512]{2,1,0:T(8,128)(2,1)S(1)}) custom-call(s32[10]{0:T(128)S(1)} %stack.37.bounds, bf16[416,512]{1,0:T(8,128)(2,1)S(1)} %get-tuple-element.22.own.refs_0_, bf16[520,128]{1,0:T(8,128)(2,1)S(1)} %collective-permute-done.4.refs_1_, bf16[512,384]{1,0:T(8,128)(2,1)S(1)} %copy-done.6, ...), custom_call_target="tpu_custom_call" | custom-call | flops 1073741824 | bytes 4194304 | tf_op jit(solution)/shard_map/pallas_call | solution.py:376
  37.1 17.0 %collective-permute-start.5 = (bf16[4,8,512]{2,1,0:T(8,128)(2,1)S(1)}, bf16[4,8,512]{2,1,0:T(8,128)(2,1)S(1)}, u32[]{:S(2)}, u32[]{:S(2)}) collective-permute-start(bf16[4,8,512]{2,1,0:T(8,128)(2,1)S(1)} %get-tuple-element.30), channel_id=1, source_target_pairs={{16,32},{48,64},{80,96},{112,128},{144,160},{176,192},{208,224},{2... | collective-permute-start | bytes 98312 | tf_op jit(solution)/shard_map/ppermute | solution.py:330
  54.1 0.0 collective-permute-done.3
  54.2 1.3 %collective-permute-done.5 = bf16[4,8,512]{2,1,0:T(8,128)(2,1)S(1)} collective-permute-done((bf16[4,8,512]{2,1,0:T(8,128)(2,1)S(1)}, bf16[4,8,512]{2,1,0:T(8,128)(2,1)S(1)}, u32[]{:S(2)}, u32[]{:S(2)}) %collective-permute-start.5) | collective-permute-done | bytes 32800 | tf_op jit(solution)/shard_map/ppermute | solution.py:330
  55.5 0.1 broadcast_select_fusion.5
  55.5 9.3 %collective-permute-start.6 = (bf16[14,4,512]{2,1,0:T(4,128)(2,1)S(1)}, bf16[14,4,512]{2,1,0:T(4,128)(2,1)S(1)}, u32[]{:S(2)}, u32[]{:S(2)}) collective-permute-start(bf16[14,4,512]{2,1,0:T(4,128)(2,1)S(1)} %get-tuple-element.43), channel_id=1, source_target_pairs={{0,1},{2,3},{4,5},{6,7},{8,9},{10,11},{12,13},{14,15},{1,0},{3,2},... | collective-permute-start | bytes 172040 | tf_op jit(solution)/shard_map/ppermute | solution.py:330
  64.8 2.1 %collective-permute-start.7 = (bf16[14,4,512]{2,1,0:T(4,128)(2,1)S(1)}, bf16[14,4,512]{2,1,0:T(4,128)(2,1)S(1)}, u32[]{:S(2)}, u32[]{:S(2)}) collective-permute-start(bf16[14,4,512]{2,1,0:T(4,128)(2,1)S(1)} %get-tuple-element.44), channel_id=1, source_target_pairs={{1,2},{3,4},{5,6},{7,8},{9,10},{11,12},{13,14},{2,1},{4,3},{6,5},{... | collective-permute-start | bytes 172040 | tf_op jit(solution)/shard_map/ppermute | solution.py:330
  66.9 0.0 copy-start.3
  66.9 0.0 copy-start.7
  67.0 1.8 %shard_map.88.part_ref = f32[2,256,256]{2,1,0:T(8,128)S(1)} custom-call(s32[10]{0:T(128)S(1)} %stack.37.bounds, bf16[384,256]{1,0:T(8,128)(2,1)S(1)} %get-tuple-element.34.near, bf16[384,256]{1,0:T(8,128)(2,1)S(1)} %get-tuple-element.35.own, bf16[384,256]{1,0:T(8,128)(2,1)S(1)} %get-tuple-element.36.far, bf16[9,256,256]{2,1,0:T(8,128)(2,1)S(1)} %get-tuple-element.37.weight, ...), custom_call_target="tpu_custom_call" | custom-call | flops 2147483648 | bytes 4194304 | tf_op jit(solution)/shard_map/pallas_call | solution.py:388
  68.8 0.0 collective-permute-done.6
  68.8 2.7 %collective-permute-done.7 = bf16[14,4,512]{2,1,0:T(4,128)(2,1)S(1)} collective-permute-done((bf16[14,4,512]{2,1,0:T(4,128)(2,1)S(1)}, bf16[14,4,512]{2,1,0:T(4,128)(2,1)S(1)}, u32[]{:S(2)}, u32[]{:S(2)}) %collective-permute-start.7) | collective-permute-done | bytes 57376 | tf_op jit(solution)/shard_map/ppermute | solution.py:330
  71.6 0.1 maximum_maximum_fusion.coarse_ref
  71.7 0.0 copy-done.3
  71.7 0.0 copy-done.7
  71.7 8.6 %shard_map.89 = bf16[32,16,256]{2,1,0:T(8,128)(2,1)} custom-call(s32[10]{0:T(128)S(1)} %stack.37.bounds, bf16[14,16,512]{2,1,0:T(8,128)(2,1)S(1)} %maximum_maximum_fusion.coarse_ref, bf16[4,27,128,128]{3,2,1,0:T(8,128)(2,1)S(1)} %copy-done.3, bf16[16,128,128]{2,1,0:T(8,128)(2,1)S(1)} %get-tuple-element.31.wupr, bf16[288,512]{1,0:T(8,128)(2,1)S(1)} %copy-done.7, ...), custom_call_target="tpu_custom_call" | custom-call | flops 3221225472 | bytes 4194304 | tf_op jit(solution)/shard_map/pallas_call | solution.py:397
  (7 shorter events, 0.1 us)
Async XLA Ops:
  0.0 1.0 %copy-start = (bf16[32,16,256]{2,1,0:T(8,128)(2,1)S(1)}, bf16[32,16,256]{2,1,0:T(8,128)(2,1)}, u32[]{:S(2)}) copy-start(bf16[32,16,256]{2,1,0:T(8,128)(2,1)} %param.8) | copy-start | bytes 786436
  1.0 20.7 %copy-start.1 = (bf16[2048,128]{1,0:T(8,128)(2,1)S(1)}, bf16[2048,128]{1,0:T(8,128)(2,1)}, u32[]{:S(2)}) copy-start(bf16[2048,128]{1,0:T(8,128)(2,1)} %down.1) | copy-start | bytes 1572868
  1.0 20.7 %copy-start.2 = (bf16[27,32,32]{2,1,0:T(8,128)(2,1)S(1)}, bf16[27,32,32]{2,1,0:T(8,128)(2,1)}, u32[]{:S(2)}) copy-start(bf16[27,32,32]{2,1,0:T(8,128)(2,1)} %first.1) | copy-start | bytes 165892
  1.5 21.3 %copy-start.4 = (bf16[128,2048]{1,0:T(8,128)(2,1)S(1)}, bf16[128,2048]{1,0:T(8,128)(2,1)}, u32[]{:S(2)}) copy-start(bf16[128,2048]{1,0:T(8,128)(2,1)} %up.1) | copy-start | bytes 1572868
  1.5 21.3 %copy-start.5 = (bf16[27,32,64]{2,1,0:T(8,128)(2,1)S(1)}, bf16[27,32,64]{2,1,0:T(8,128)(2,1)}, u32[]{:S(2)}) copy-start(bf16[27,32,64]{2,1,0:T(8,128)(2,1)} %closing.1) | copy-start | bytes 331780
  1.5 24.9 %copy-start.6 = (bf16[512,384]{1,0:T(8,128)(2,1)S(1)}, bf16[512,384]{1,0:T(8,128)(2,1)}, u32[]{:S(2)}) copy-start(bf16[512,384]{1,0:T(8,128)(2,1)} %constant.39.clone.groups.refs_2_) | copy-start | bytes 1179652
  1.5 7.6 %collective-permute-start = (bf16[80,512]{1,0:T(8,128)(2,1)S(1)}, bf16[80,512]{1,0:T(8,128)(2,1)S(1)}, u32[]{:S(2)}, u32[]{:S(2)}) collective-permute-start(bf16[80,512]{1,0:T(8,128)(2,1)S(1)} %get-tuple-element.40), channel_id=1, source_target_pairs={{1,2},{3,4},{5,6},{7,8},{9,10},{11,12},{13,14},{2,1},{4,3},{6,5},{... | collective-permute-start | bytes 245768 | tf_op jit(solution)/shard_map/ppermute | solution.py:330
  7.0 3.2 %collective-permute-start.1 = (bf16[80,512]{1,0:T(8,128)(2,1)S(1)}, bf16[80,512]{1,0:T(8,128)(2,1)S(1)}, u32[]{:S(2)}, u32[]{:S(2)}) collective-permute-start(bf16[80,512]{1,0:T(8,128)(2,1)S(1)} %get-tuple-element.39), channel_id=1, source_target_pairs={{0,1},{2,3},{4,5},{6,7},{8,9},{10,11},{12,13},{14,15},{1,0},{3,2},... | collective-permute-start | bytes 245768 | tf_op jit(solution)/shard_map/ppermute | solution.py:330
  10.8 19.8 %collective-permute-start.2 = (bf16[520,128]{1,0:T(8,128)(2,1)S(1)}, bf16[520,128]{1,0:T(8,128)(2,1)S(1)}, u32[]{:S(2)}, u32[]{:S(2)}) collective-permute-start(bf16[520,128]{1,0:T(8,128)(2,1)S(1)} %get-tuple-element.23), channel_id=1, source_target_pairs={{16,32},{48,64},{80,96},{112,128},{144,160},{176,192},{208,224},{2... | collective-permute-start | bytes 399368 | tf_op jit(solution)/shard_map/ppermute | solution.py:330
  24.5 10.3 %collective-permute-start.4 = (bf16[520,128]{1,0:T(8,128)(2,1)S(1)}, bf16[520,128]{1,0:T(8,128)(2,1)S(1)}, u32[]{:S(2)}, u32[]{:S(2)}) collective-permute-start(bf16[520,128]{1,0:T(8,128)(2,1)S(1)} %get-tuple-element.29), channel_id=1, source_target_pairs={{0,16},{32,48},{64,80},{96,112},{128,144},{160,176},{192,208},{224... | collective-permute-start | bytes 399368 | tf_op jit(solution)/shard_map/ppermute | solution.py:330
  32.9 21.2 %collective-permute-start.3 = (bf16[4,8,512]{2,1,0:T(8,128)(2,1)S(1)}, bf16[4,8,512]{2,1,0:T(8,128)(2,1)S(1)}, u32[]{:S(2)}, u32[]{:S(2)}) collective-permute-start(bf16[4,8,512]{2,1,0:T(8,128)(2,1)S(1)} %get-tuple-element.28), channel_id=1, source_target_pairs={{0,16},{32,48},{64,80},{96,112},{128,144},{160,176},{192,208},{224... | collective-permute-start | bytes 98312 | tf_op jit(solution)/shard_map/ppermute | solution.py:330
  37.1 18.3 %collective-permute-start.5 = (bf16[4,8,512]{2,1,0:T(8,128)(2,1)S(1)}, bf16[4,8,512]{2,1,0:T(8,128)(2,1)S(1)}, u32[]{:S(2)}, u32[]{:S(2)}) collective-permute-start(bf16[4,8,512]{2,1,0:T(8,128)(2,1)S(1)} %get-tuple-element.30), channel_id=1, source_target_pairs={{16,32},{48,64},{80,96},{112,128},{144,160},{176,192},{208,224},{2... | collective-permute-start | bytes 98312 | tf_op jit(solution)/shard_map/ppermute | solution.py:330
  55.5 13.3 %collective-permute-start.6 = (bf16[14,4,512]{2,1,0:T(4,128)(2,1)S(1)}, bf16[14,4,512]{2,1,0:T(4,128)(2,1)S(1)}, u32[]{:S(2)}, u32[]{:S(2)}) collective-permute-start(bf16[14,4,512]{2,1,0:T(4,128)(2,1)S(1)} %get-tuple-element.43), channel_id=1, source_target_pairs={{0,1},{2,3},{4,5},{6,7},{8,9},{10,11},{12,13},{14,15},{1,0},{3,2},... | collective-permute-start | bytes 172040 | tf_op jit(solution)/shard_map/ppermute | solution.py:330
  64.8 6.7 %collective-permute-start.7 = (bf16[14,4,512]{2,1,0:T(4,128)(2,1)S(1)}, bf16[14,4,512]{2,1,0:T(4,128)(2,1)S(1)}, u32[]{:S(2)}, u32[]{:S(2)}) collective-permute-start(bf16[14,4,512]{2,1,0:T(4,128)(2,1)S(1)} %get-tuple-element.44), channel_id=1, source_target_pairs={{1,2},{3,4},{5,6},{7,8},{9,10},{11,12},{13,14},{2,1},{4,3},{6,5},{... | collective-permute-start | bytes 172040 | tf_op jit(solution)/shard_map/ppermute | solution.py:330
  66.9 4.8 %copy-start.3 = (bf16[4,27,128,128]{3,2,1,0:T(8,128)(2,1)S(1)}, bf16[4,27,128,128]{3,2,1,0:T(8,128)(2,1)}, u32[]{:S(2)}) copy-start(bf16[4,27,128,128]{3,2,1,0:T(8,128)(2,1)} %w_coarse.1) | copy-start | bytes 10616836
  66.9 4.8 %copy-start.7 = (bf16[288,512]{1,0:T(8,128)(2,1)S(1)}, bf16[288,512]{1,0:T(8,128)(2,1)}, u32[]{:S(2)}) copy-start(bf16[288,512]{1,0:T(8,128)(2,1)} %constant.40.clone.from_groups) | copy-start | bytes 884740

commit v9 on v7

--- a/solution.py
+++ b/solution.py
@@ -1,5 +1,6 @@
 import jax
 import jax.numpy as jnp
+import numpy as np
 from jax import lax
 from jax.experimental import pallas as pl
 from jax.experimental.pallas import tpu as pltpu
@@ -28,13 +29,11 @@
     return before, value, after
 
 
-def regroup(rows, columns, row_dim, first):
-    coarse = iota((rows, columns), row_dim)
-    fine = iota((rows, columns), 1 - row_dim)
-    offset = coarse >> 5
-    y = 4 * (coarse & 7) + (offset >> 2)
-    z = 4 * ((coarse >> 3) & 3) + (offset & 3)
-    return jnp.where(fine == (y - first) * NZ + z, 1.0, 0.0).astype(BF)
+def regroup():
+    coarse, fine = np.arange(512)[:, None], np.arange(384)[None]
+    y = 4 * (coarse & 7) + (coarse >> 7)
+    z = 4 * (coarse >> 3 & 3) + (coarse >> 5 & 3)
+    return fine == y * NZ + z
 
 
 def moved(value, start, target):
@@ -86,26 +85,31 @@
     target[:, 128:256] = pltpu.roll(high, 32, 1).astype(BF)
 
 
-def fine_groups(windows, bounds, w1, w1_edge, dwr, skip_refs, coarse_refs, vz, edges, grouped):
-    to_groups = regroup(512, 384, 0, 0)
-    y = (iota((384, 256), 0) >> 4) - 4
-    plane = iota((384, 256), 1) >> 5
-    y_inside = (y >= bounds[2]) & (y <= bounds[3])
-    for k, (tiles, first_x) in enumerate(windows):
+def fine_groups(windows, bounds, to_groups, w1, w1_edge, dwr, skip_refs, coarse_refs, vz, edges, grouped):
+    parts = 2 // len(windows)
+    rows = 384 // parts
+    chains = [(k, rows * part) for k in range(len(windows)) for part in range(parts)]
+    for k, (tiles, _) in enumerate(windows):
         for half in range(2):
             for oz, shifted in enumerate(z_shifts(tiles[1 + half], 416)):
                 vz[k, oz, :, 128 * half : 128 * half + 128] = shifted.astype(BF)
         fill_edges(tiles[0], tiles[3], 416, edges.at[k])
-        summed = jnp.zeros((384, 256), F32)
-        for oy in range(3):
-            for oz in range(3):
-                summed += dot(vz[k, oz, 16 * oy : 16 * oy + 384], w1[3 * oy + oz], NT)
-            summed += dot(edges[k, 16 * oy : 16 * oy + 384], w1_edge[oy], NT)
-        x = plane + first_x
-        inside = y_inside & (x >= bounds[0]) & (x <= bounds[1])
-        skip = jnp.where(inside, jnp.maximum(summed, 0.0), 0.0).astype(BF)
-        skip_refs[k][...] = skip
-        grouped[:, 256 * k : 256 * k + 256] = dot(to_groups, skip, NN).astype(BF)
+    summed = [jnp.zeros((rows, 256), F32) for _ in chains]
+    for oy in range(3):
+        for oz in range(4):
+            for c, (k, start) in enumerate(chains):
+                here = slice(start + 16 * oy, start + 16 * oy + rows)
+                if oz < 3:
+                    summed[c] += dot(vz[k, oz, here], w1[3 * oy + oz], NT)
+                else:
+                    summed[c] += dot(edges[k, here], w1_edge[oy], NT)
+    for c, (k, start) in enumerate(chains):
+        y = ((iota((rows, 256), 0) + start) >> 4) - 4
+        x = (iota((rows, 256), 1) >> 5) + windows[k][1]
+        inside = (y >= bounds[2]) & (y <= bounds[3]) & (x >= bounds[0]) & (x <= bounds[1])
+        skip_refs[k][start : start + rows] = jnp.where(inside, jnp.maximum(summed[c], 0.0), 0.0).astype(BF)
+    for k in range(len(windows)):
+        grouped[:, 256 * k : 256 * k + 256] = dot(to_groups[...], skip_refs[k][...], NN).astype(BF)
     count = 2 * len(windows)
     coarse = jnp.zeros((32 * count, 128), F32)
     for i in range(0, 16, 2):
@@ -125,20 +129,20 @@
                 target[first_a + a % 2, :, 128 * z : 128 * z + 128] = cell
 
 
-def near_kernel(bounds, own, near, w1, w1_edge, dwr, skip_near, skip_own, to_far, coarse_own, vz, edges, grouped):
+def near_kernel(bounds, own, near, groups, w1, w1_edge, dwr, skip_near, skip_own, to_far, coarse_own, vz, edges, grouped):
     odd = bounds[8] == 1
     first_near, first_own = 2 - 2 * bounds[8], 2 * bounds[8]
     windows = ((side_window(own, near, odd), jnp.where(odd, -4, 12)), (own_window(own), 4))
     coarse = ([(to_far, first_near)], [(to_far, first_own), (coarse_own, 0)])
-    fine_groups(windows, bounds, w1, w1_edge, dwr, (skip_near, skip_own), coarse, vz, edges, grouped)
-
-
-def far_kernel(bounds, own, far, w1, w1_edge, dwr, coarse_own, skip_far, to_near, vz, edges, grouped):
+    fine_groups(windows, bounds, groups, w1, w1_edge, dwr, (skip_near, skip_own), coarse, vz, edges, grouped)
+
+
+def far_kernel(bounds, own, far, groups, w1, w1_edge, dwr, coarse_own, skip_far, to_near, vz, edges, grouped):
     to_near[pl.ds(2 - 2 * bounds[8], 2)] = coarse_own[...]
     even = bounds[8] == 0
     windows = ((side_window(own, far, even), jnp.where(even, -4, 12)),)
     coarse = ([(to_near, 2 * bounds[8])],)
-    fine_groups(windows, bounds, w1, w1_edge, dwr, (skip_far,), coarse, vz, edges, grouped)
+    fine_groups(windows, bounds, groups, w1, w1_edge, dwr, (skip_far,), coarse, vz, edges, grouped)
 
 
 def fill_shifts(tile_of, middle, edges):
@@ -149,13 +153,16 @@
         fill_edges(tile_of(2 * g), tile_of(2 * g + 3), 288, edges.at[g])
 
 
-def closing_sum(weight, weight_edge, middle, edges, g):
-    summed = jnp.zeros((256, 256), F32)
+def closing_sums(weight, weight_edge, middle, edges):
+    summed = [jnp.zeros((256, 256), F32) for _ in range(2)]
     for oy in range(3):
         rows = slice(16 * oy, 16 * oy + 256)
-        for oz in range(3):
-            summed += dot(weight[3 * oy + oz], middle[oz, rows, 256 * g : 256 * g + 256], NT)
-        summed += dot(weight_edge[oy], edges[g, rows], NT)
+        for oz in range(4):
+            for g in range(2):
+                if oz < 3:
+                    summed[g] += dot(middle[oz, rows, 256 * g : 256 * g + 256], weight[3 * oy + oz], NT)
+                else:
+                    summed[g] += dot(edges[g, rows], weight_edge[oy], NT)
     return summed
 
 
@@ -171,13 +178,11 @@
         return jnp.where(odd, first, second) if group == 0 else jnp.where(odd, second, first)
 
     fill_shifts(tile_of, middle, edges)
-    for g in range(2):
-        out_ref[g] = closing_sum(weight, weight_edge, middle, edges, g)
-
-
-def last_kernel(
-    bounds, coarse_ref, w_coarse, wupr, weight, weight_edge, part_ref, out_ref, state, raw, up, middle_ref, edges
-):
+    for g, summed in enumerate(closing_sums(weight, weight_edge, middle, edges)):
+        out_ref[g] = summed
+
+
+def coarse_kernel(bounds, coarse_ref, w_coarse, wupr, from_groups, up, state, raw):
     value = coarse_ref[...].reshape(224, 512).astype(F32)
     for layer in range(4):
         rows_in = (14 - 2 * layer) * 16
@@ -196,12 +201,18 @@
                 w_high = jnp.concatenate([middle, jnp.concatenate([zero, w[0], w[1]], axis=1)], axis=0)
                 low += dot(state[ob, 16 * oa : 16 * oa + rows, 0:384], w_low, NT)
                 high += dot(state[ob, 16 * oa : 16 * oa + rows, 128:512], w_high, NT)
-        index = iota((rows, 512), 0)
+        index = iota((rows, 128), 0)
         a = (index >> 4) - 4 + layer
-        b = index & 15
-        kept = (a >= bounds[4]) & (a <= bounds[5]) & (b < 12 - 2 * layer)
-        kept = kept & (b - 4 + layer >= bounds[6]) & (b - 4 + layer <= bounds[7])
-        value = jnp.where(kept, jnp.maximum(jnp.concatenate([low, high], axis=1), 0.0), 0.0)
+        b = (index & 15) - 4 + layer
+        kept = (a >= bounds[4]) & (a <= bounds[5]) & (b < 8 - layer) & (b >= bounds[6]) & (b <= bounds[7])
+        value = jnp.concatenate(
+            [
+                jnp.where(kept, jnp.maximum(half[:, side : side + 128], 0.0), 0.0)
+                for half in (low, high)
+                for side in (0, 128)
+            ],
+            axis=1,
+        )
         value = value.astype(BF).astype(F32)
     cells = jnp.concatenate(
         [value[16 * a : 16 * a + 8, 128 * z : 128 * z + 128] for z in range(4) for a in range(6)], axis=0
@@ -214,15 +225,18 @@
                     raw[32 * (i + half) + 8 * z : 32 * (i + half) + 8 * z + 8, 128 * a : 128 * a + 128] = pair[
                         48 * z + 8 * a : 48 * z + 8 * a + 8, 128 * half : 128 * half + 128
                     ]
-    from_groups = regroup(288, 512, 1, 3)
     for g in range(3):
-        up[:, 256 * g : 256 * g + 256] = dot(from_groups, raw[:, 256 * g : 256 * g + 256].astype(BF), NN)
-    fill_shifts(lambda tile: up[:, 128 * tile : 128 * tile + 128], middle_ref, edges)
+        lanes = slice(256 * g, 256 * g + 256)
+        up[:, lanes] = dot(from_groups[...], raw[:, lanes].astype(BF), NN).astype(BF)
+
+
+def last_kernel(up, weight, weight_edge, part_ref, out_ref, middle, edges):
+    fill_shifts(lambda tile: up[:, 128 * tile : 128 * tile + 128].astype(F32), middle, edges)
     row, column = iota((256, 256), 0), iota((256, 256), 1)
     to_channels = jnp.where(column == ((row & 7) << 5) + (row >> 3), 1.0, 0.0).astype(BF)
-    for g in range(2):
-        total = (closing_sum(weight, weight_edge, middle_ref, edges, g) + part_ref[g]).astype(BF)
-        out_ref[:, 8 * g : 8 * g + 8, :] = dot(to_channels, total, NN).reshape(32, 8, 256).astype(BF)
+    for g, summed in enumerate(closing_sums(weight, weight_edge, middle, edges)):
+        total = (summed + part_ref[g]).astype(BF)
+        out_ref[:, 8 * g : 8 * g + 8, :] = dot(to_channels, total, NT).reshape(32, 8, 256).astype(BF)
 
 
 def banded(source, target, edge_target, channels):
@@ -335,25 +349,26 @@
         prepare_first_kernel, [weight, edge, offsets], [((2048, 128), F32)], 2, False, 1 << 27, 8
     )(w_first, down_weight)
     skip, cells = ((384, 256), BF), ((4, 8, 512), BF)
+    groups = jnp.asarray(regroup(), BF)
     skip_near, skip_own, to_far, coarse_own = call(
         near_kernel,
         [skip, skip, cells, ((2, 8, 512), BF)],
         [((2, 3, 416, 256), BF), ((2, 416, 256), BF), ((512, 512), BF)],
-        5,
+        6,
         True,
         2 << 30,
         10,
-    )(bounds, own, near, w1, w1_edge, dwr)
+    )(bounds, own, near, groups, w1, w1_edge, dwr)
     far_cells = swap(to_far, "sx", 1)
     skip_far, to_near = call(
         far_kernel,
         [skip, cells],
         [((1, 3, 416, 256), BF), ((1, 416, 256), BF), ((512, 256), BF)],
-        6,
+        7,
         True,
         1 << 30,
         10,
-    )(bounds, own, far, w1, w1_edge, dwr, coarse_own)
+    )(bounds, own, far, groups, w1, w1_edge, dwr, coarse_own)
     near_cells = swap(to_near, "sx", 0)
     skip_weight, skip_edge, up_weight, up_edge, wupr = call(
         prepare_last_kernel, [weight, edge, weight, edge, offsets], [((2048, 128), F32)], 2, False, 1 << 28, 10
@@ -368,15 +383,10 @@
     chips, cores = y_swaps(coarse[:, 2:6], coarse[:, 0:4], odd_y)
     before, after = jnp.where(odd_y, cores, chips), jnp.where(odd_y, chips, cores)
     coarse = jnp.concatenate([before, coarse[:, 0:6], after, jnp.zeros((14, 2, 512), BF)], axis=1)
-    (result,) = call(
-        last_kernel,
-        [((32, 16, 256), BF)],
-        [((3, 224, 512), BF), ((512, 768), F32), ((288, 768), F32)] + shifts,
-        6,
-        True,
-        3 << 30,
-        16,
-    )(bounds, coarse, w_coarse, wupr, up_weight, up_edge, part)
+    (up,) = call(
+        coarse_kernel, [((288, 768), BF)], [((3, 224, 512), BF), ((512, 768), F32)], 4, True, 3 << 30, 12
+    )(bounds, coarse, w_coarse, wupr, jnp.asarray(regroup().T[48:336], BF))
+    (result,) = call(last_kernel, [((32, 16, 256), BF)], shifts, 4, False, 2 << 30, 12)(up, up_weight, up_edge, part)
     return result
 
 

time: 84 us -> 83.3 us (level)
  Pallas kernels: 20.6 us -> 18.4 us
  waiting for transfers between devices: 37.8 us -> 39.3 us
    ppermute x8, waiting for transfers between devices: 37.8 us -> 39.3 us  [swap(): return lax.ppermute(array, axis, pairs + [(j, i) for i, j in pairs])]
    pallas_call x1, Pallas kernels: 4.37 us -> 2.89 us  [local(): call(near_kernel, [skip, skip, cells, ((2, 8, 512), BF)], [((2, 3, 416, 2...]
    pallas_call x1 -> x2, Pallas kernels: 8.65 us -> 7.91 us  [the longest x1 5.84 us: local(): call(coarse_kernel, [((288, 768), BF)], [((3, 224, 512), BF), ((512, 768)...]
  transfers between devices with their start and end apart: 8 -> 8, of which waited for: 6 -> 6; matrix products, arithmetic and copies ran while one was open for 0% -> 0% of each run, Pallas kernels for 11% -> 9%
where the time goes in v9:
time: 83.3 us; the launch traced here: 83 us
  waiting for transfers between devices  39.3 us (47%)
  starting transfers between devices  23 us (28%)
  Pallas kernels  18.4 us (22%)
  local copies, waits for them, and re-layouts  1.15 us (1%)
    ppermute x8, waiting for transfers between devices, swap(): return lax.ppermute(array, axis, pairs + [(j, i) for i, j in pairs])  39.3 us
    ppermute x8, starting transfers between devices, swap(): return lax.ppermute(array, axis, pairs + [(j, i) for i, j in pairs])  23 us
    pallas_call x1, Pallas kernels, local(): call(coarse_kernel, [((288, 768), BF)], [((3, 224, 512), BF), ((512, 768)...  5.84 us
    pallas_call x1, Pallas kernels, local(): call(near_kernel, [skip, skip, cells, ((2, 8, 512), BF)], [((2, 3, 416, 2...  2.89 us
    pallas_call x1, Pallas kernels, local(): call(far_kernel, [skip, cells], [((1, 3, 416, 256), BF), ((1, 416, 256),...  2.37 us
    pallas_call x1, Pallas kernels, local(): call(last_kernel, [((32, 16, 256), BF)], shifts, 4, False, 2 << 30, 12)  2.07 us
    pallas_call x1, Pallas kernels, local(): call(skip_kernel, [((2, 256, 256), F32)], shifts, 5, True, 2 << 30, 8)  1.75 us
    pallas_call x1, Pallas kernels, local(): call(prepare_last_kernel, [weight, edge, weight, edge, offsets], [((2048,...  1.69 us
  transfers between devices with their start and end apart: 8, of which 6 were waited for; matrix products, arithmetic and copies ran while one was open for 0% of the time, Pallas kernels for 9%

profile of v9, /device:TPU:289, one launch (start us, length us, event | category | flops | bytes accessed | tf_op | source)
XLA Modules:
  0.0 83.0 jit_solution(6207041418466441066)
XLA Ops:
  0.0 0.0 copy-start
  0.0 0.9 %copy-done = bf16[32,16,256]{2,1,0:T(8,128)(2,1)S(1)} copy-done((bf16[32,16,256]{2,1,0:T(8,128)(2,1)S(1)}, bf16[32,16,256]{2,1,0:T(8,128)(2,1)}, u32[]{:S(2)}) %copy-start) | copy-done | bytes 262168
  1.0 0.0 copy-start.1
  1.0 0.0 copy-start.2
  1.0 0.5 fusion.own
  1.5 0.0 copy-start.4
  1.5 0.0 copy-start.5
  1.5 0.0 copy-start.6
  1.5 3.3 %collective-permute-start = (bf16[80,512]{1,0:T(8,128)(2,1)S(1)}, bf16[80,512]{1,0:T(8,128)(2,1)S(1)}, u32[]{:S(2)}, u32[]{:S(2)}) collective-permute-start(bf16[80,512]{1,0:T(8,128)(2,1)S(1)} %get-tuple-element.40), channel_id=1, source_target_pairs={{1,2},{3,4},{5,6},{7,8},{9,10},{11,12},{13,14},{2,1},{4,3},{6,5},{... | collective-permute-start | bytes 245768 | tf_op jit(solution)/shard_map/ppermute | solution.py:311
  4.9 1.9 %collective-permute-start.1 = (bf16[80,512]{1,0:T(8,128)(2,1)S(1)}, bf16[80,512]{1,0:T(8,128)(2,1)S(1)}, u32[]{:S(2)}, u32[]{:S(2)}) collective-permute-start(bf16[80,512]{1,0:T(8,128)(2,1)S(1)} %get-tuple-element.39), channel_id=1, source_target_pairs={{0,1},{2,3},{4,5},{6,7},{8,9},{10,11},{12,13},{14,15},{1,0},{3,2},... | collective-permute-start | bytes 245768 | tf_op jit(solution)/shard_map/ppermute | solution.py:311
  6.8 0.1 stack.37.bounds
  6.9 0.8 collective-permute-done.chips
  7.7 0.3 collective-permute-done.1.cores
  8.0 0.7 shard_map.82
  8.7 3.2 %collective-permute-start.3 = (bf16[520,128]{1,0:T(8,128)(2,1)S(1)}, bf16[520,128]{1,0:T(8,128)(2,1)S(1)}, u32[]{:S(2)}, u32[]{:S(2)}) collective-permute-start(bf16[520,128]{1,0:T(8,128)(2,1)S(1)} %get-tuple-element.27), channel_id=1, source_target_pairs={{0,16},{32,48},{64,80},{96,112},{128,144},{160,176},{192,208},{224... | collective-permute-start | bytes 399368 | tf_op jit(solution)/shard_map/ppermute | solution.py:311
  12.0 0.1 pad.3.clone
  12.0 0.0 copy-done.1
  12.0 0.0 copy-done.2
  12.0 1.1 %shard_map.83 = (bf16[9,256,256]{2,1,0:T(8,128)(2,1)S(1)}, bf16[3,256,256]{2,1,0:T(8,128)(2,1)S(1)}, bf16[16,128,128]{2,1,0:T(8,128)(2,1)S(1)}) custom-call(bf16[27,32,32]{2,1,0:T(8,128)(2,1)S(1)} %copy-done.2, bf16[2048,128]{1,0:T(8,128)(2,1)S(1)} %copy-done.1), custom_call_target="tpu_custom_call" | custom-call | flops 134217728 | bytes 4194304 | tf_op jit(solution)/shard_map/pallas_call | solution.py:348
  13.2 0.0 copy-done.4
  13.2 0.0 copy-done.5
  13.2 1.7 %shard_map.86 = (bf16[9,256,256]{2,1,0:T(8,128)(2,1)S(1)}, bf16[3,256,256]{2,1,0:T(8,128)(2,1)S(1)}, bf16[9,256,256]{2,1,0:T(8,128)(2,1)S(1)}, bf16[3,256,256]{2,1,0:T(8,128)(2,1)S(1)}, bf16[16,128,128]{2,1,0:T(8,128)(2,1)S(1)}) custom-call(bf16[27,32,64]{2,1,0:T(8,128)(2,1)S(1)} %copy-done.5, bf16[128,2048]{1,0:T(8,128)(2,1)S(1)} %copy-done.4), custom_call_target="tpu_custom_call" | custom-call | flops 268435456 | bytes 4194304 | tf_op jit(solution)/shard_map/pallas_call | solution.py:373
  14.9 4.2 %collective-permute-start.2 = (bf16[520,128]{1,0:T(8,128)(2,1)S(1)}, bf16[520,128]{1,0:T(8,128)(2,1)S(1)}, u32[]{:S(2)}, u32[]{:S(2)}) collective-permute-start(bf16[520,128]{1,0:T(8,128)(2,1)S(1)} %get-tuple-element.23), channel_id=1, source_target_pairs={{16,32},{48,64},{80,96},{112,128},{144,160},{176,192},{208,224},{2... | collective-permute-start | bytes 399368 | tf_op jit(solution)/shard_map/ppermute | solution.py:311
  19.1 0.0 collective-permute-done.3.near
  19.1 0.0 copy-done.6
  19.1 2.9 %shard_map.84 = (bf16[384,256]{1,0:T(8,128)(2,1)S(1)}, bf16[384,256]{1,0:T(8,128)(2,1)S(1)}, bf16[4,8,512]{2,1,0:T(8,128)(2,1)S(1)}, bf16[2,8,512]{2,1,0:T(8,128)(2,1)S(1)}) custom-call(s32[10]{0:T(128)S(1)} %stack.37.bounds, bf16[416,512]{1,0:T(8,128)(2,1)S(1)} %get-tuple-element.22.own, bf16[520,128]{1,0:T(8,128)(2,1)S(1)} %collective-permute-done.3.near, ...), custom_call_target="tpu_custom_call" | custom-call | flops 2147483648 | bytes 4194304 | tf_op jit(solution)/shard_map/pallas_call | solution.py:353
  22.0 21.0 %collective-permute-done.2.far = bf16[520,128]{1,0:T(8,128)(2,1)S(1)} collective-permute-done((bf16[520,128]{1,0:T(8,128)(2,1)S(1)}, bf16[520,128]{1,0:T(8,128)(2,1)S(1)}, u32[]{:S(2)}, u32[]{:S(2)}) %collective-permute-start.2) | collective-permute-done | bytes 133152 | tf_op jit(solution)/shard_map/ppermute | solution.py:311
  42.9 2.4 %shard_map.85 = (bf16[384,256]{1,0:T(8,128)(2,1)S(1)}, bf16[4,8,512]{2,1,0:T(8,128)(2,1)S(1)}) custom-call(s32[10]{0:T(128)S(1)} %stack.37.bounds, bf16[416,512]{1,0:T(8,128)(2,1)S(1)} %get-tuple-element.22.own, bf16[520,128]{1,0:T(8,128)(2,1)S(1)} %collective-permute-done.2.far, bf16[512,384]{1,0:T(8,128)(2,1)S(1)} %copy-done.6, ...), custom_call_target="tpu_custom_call" | custom-call | flops 1073741824 | bytes 4194304 | tf_op jit(solution)/shard_map/pallas_call | solution.py:363
  45.3 1.9 %collective-permute-start.4 = (bf16[4,8,512]{2,1,0:T(8,128)(2,1)S(1)}, bf16[4,8,512]{2,1,0:T(8,128)(2,1)S(1)}, u32[]{:S(2)}, u32[]{:S(2)}) collective-permute-start(bf16[4,8,512]{2,1,0:T(8,128)(2,1)S(1)} %get-tuple-element.29), channel_id=1, source_target_pairs={{0,16},{32,48},{64,80},{96,112},{128,144},{160,176},{192,208},{224... | collective-permute-start | bytes 98312 | tf_op jit(solution)/shard_map/ppermute | solution.py:311
  47.2 1.9 %collective-permute-start.5 = (bf16[4,8,512]{2,1,0:T(8,128)(2,1)S(1)}, bf16[4,8,512]{2,1,0:T(8,128)(2,1)S(1)}, u32[]{:S(2)}, u32[]{:S(2)}) collective-permute-start(bf16[4,8,512]{2,1,0:T(8,128)(2,1)S(1)} %get-tuple-element.30), channel_id=1, source_target_pairs={{16,32},{48,64},{80,96},{112,128},{144,160},{176,192},{208,224},{2... | collective-permute-start | bytes 98312 | tf_op jit(solution)/shard_map/ppermute | solution.py:311
  49.2 0.8 collective-permute-done.4
  50.0 14.9 %collective-permute-done.5 = bf16[4,8,512]{2,1,0:T(8,128)(2,1)S(1)} collective-permute-done((bf16[4,8,512]{2,1,0:T(8,128)(2,1)S(1)}, bf16[4,8,512]{2,1,0:T(8,128)(2,1)S(1)}, u32[]{:S(2)}, u32[]{:S(2)}) %collective-permute-start.5) | collective-permute-done | bytes 32800 | tf_op jit(solution)/shard_map/ppermute | solution.py:311
  64.9 0.1 broadcast_select_fusion.5
  64.9 4.4 %collective-permute-start.6 = (bf16[14,4,512]{2,1,0:T(4,128)(2,1)S(1)}, bf16[14,4,512]{2,1,0:T(4,128)(2,1)S(1)}, u32[]{:S(2)}, u32[]{:S(2)}) collective-permute-start(bf16[14,4,512]{2,1,0:T(4,128)(2,1)S(1)} %get-tuple-element.43), channel_id=1, source_target_pairs={{0,1},{2,3},{4,5},{6,7},{8,9},{10,11},{12,13},{14,15},{1,0},{3,2},... | collective-permute-start | bytes 172040 | tf_op jit(solution)/shard_map/ppermute | solution.py:311
  69.4 2.1 %collective-permute-start.7 = (bf16[14,4,512]{2,1,0:T(4,128)(2,1)S(1)}, bf16[14,4,512]{2,1,0:T(4,128)(2,1)S(1)}, u32[]{:S(2)}, u32[]{:S(2)}) collective-permute-start(bf16[14,4,512]{2,1,0:T(4,128)(2,1)S(1)} %get-tuple-element.44), channel_id=1, source_target_pairs={{1,2},{3,4},{5,6},{7,8},{9,10},{11,12},{13,14},{2,1},{4,3},{6,5},{... | collective-permute-start | bytes 172040 | tf_op jit(solution)/shard_map/ppermute | solution.py:311
  71.5 0.0 copy-start.3
  71.5 0.0 copy-start.7
  71.5 1.7 %shard_map.88.part_ref = f32[2,256,256]{2,1,0:T(8,128)S(1)} custom-call(s32[10]{0:T(128)S(1)} %stack.37.bounds, bf16[384,256]{1,0:T(8,128)(2,1)S(1)} %get-tuple-element.34.near, bf16[384,256]{1,0:T(8,128)(2,1)S(1)} %get-tuple-element.35.own, bf16[384,256]{1,0:T(8,128)(2,1)S(1)} %get-tuple-element.36.far, bf16[9,256,256]{2,1,0:T(8,128)(2,1)S(1)} %get-tuple-element.37.weight, ...), custom_call_target="tpu_custom_call" | custom-call | flops 2147483648 | bytes 4194304 | tf_op jit(solution)/shard_map/pallas_call | solution.py:377
  73.3 0.0 collective-permute-done.6
  73.3 1.6 %collective-permute-done.7 = bf16[14,4,512]{2,1,0:T(4,128)(2,1)S(1)} collective-permute-done((bf16[14,4,512]{2,1,0:T(4,128)(2,1)S(1)}, bf16[14,4,512]{2,1,0:T(4,128)(2,1)S(1)}, u32[]{:S(2)}, u32[]{:S(2)}) %collective-permute-start.7) | collective-permute-done | bytes 57376 | tf_op jit(solution)/shard_map/ppermute | solution.py:311
  74.9 0.1 maximum_maximum_fusion.coarse_ref
  75.0 0.0 copy-done.3
  75.1 0.0 copy-done.7
  75.1 5.8 %shard_map.87.up = bf16[288,768]{1,0:T(8,128)(2,1)S(1)} custom-call(s32[10]{0:T(128)S(1)} %stack.37.bounds, bf16[14,16,512]{2,1,0:T(8,128)(2,1)S(1)} %maximum_maximum_fusion.coarse_ref, bf16[4,27,128,128]{3,2,1,0:T(8,128)(2,1)S(1)} %copy-done.3, bf16[16,128,128]{2,1,0:T(8,128)(2,1)S(1)} %get-tuple-element.31.wupr, bf16[288,512]{1,0:T(8,128)(2,1)S(1)} %copy-done.7), custom_call_target="tpu_custom_call" | custom-call | flops 3221225472 | bytes 4194304 | tf_op jit(solution)/shard_map/pallas_call | solution.py:386
  80.9 2.1 %shard_map.89 = bf16[32,16,256]{2,1,0:T(8,128)(2,1)} custom-call(bf16[288,768]{1,0:T(8,128)(2,1)S(1)} %shard_map.87.up, bf16[9,256,256]{2,1,0:T(8,128)(2,1)S(1)} %get-tuple-element.32.weight, bf16[3,256,256]{2,1,0:T(8,128)(2,1)S(1)} %get-tuple-element.33.weight_edge, f32[2,256,256]{2,1,0:T(8,128)S(1)} %shard_map.88.part_ref), custom_call_target="tpu_custom_call" | custom-call | flops 2147483648 | bytes 4194304 | tf_op jit(solution)/shard_map/pallas_call | solution.py:389
  (7 shorter events, 0.1 us)
Async XLA Ops:
  0.0 1.0 %copy-start = (bf16[32,16,256]{2,1,0:T(8,128)(2,1)S(1)}, bf16[32,16,256]{2,1,0:T(8,128)(2,1)}, u32[]{:S(2)}) copy-start(bf16[32,16,256]{2,1,0:T(8,128)(2,1)} %param.8) | copy-start | bytes 786436
  1.0 11.1 %copy-start.1 = (bf16[2048,128]{1,0:T(8,128)(2,1)S(1)}, bf16[2048,128]{1,0:T(8,128)(2,1)}, u32[]{:S(2)}) copy-start(bf16[2048,128]{1,0:T(8,128)(2,1)} %down.1) | copy-start | bytes 1572868
  1.0 11.1 %copy-start.2 = (bf16[27,32,32]{2,1,0:T(8,128)(2,1)S(1)}, bf16[27,32,32]{2,1,0:T(8,128)(2,1)}, u32[]{:S(2)}) copy-start(bf16[27,32,32]{2,1,0:T(8,128)(2,1)} %first.1) | copy-start | bytes 165892
  1.5 11.7 %copy-start.4 = (bf16[128,2048]{1,0:T(8,128)(2,1)S(1)}, bf16[128,2048]{1,0:T(8,128)(2,1)}, u32[]{:S(2)}) copy-start(bf16[128,2048]{1,0:T(8,128)(2,1)} %up.1) | copy-start | bytes 1572868
  1.5 11.7 %copy-start.5 = (bf16[27,32,64]{2,1,0:T(8,128)(2,1)S(1)}, bf16[27,32,64]{2,1,0:T(8,128)(2,1)}, u32[]{:S(2)}) copy-start(bf16[27,32,64]{2,1,0:T(8,128)(2,1)} %closing.1) | copy-start | bytes 331780
  1.5 17.6 %copy-start.6 = (bf16[512,384]{1,0:T(8,128)(2,1)S(1)}, bf16[512,384]{1,0:T(8,128)(2,1)}, u32[]{:S(2)}) copy-start(bf16[512,384]{1,0:T(8,128)(2,1)} %constant.39.clone.groups) | copy-start | bytes 1179652
  1.5 6.2 %collective-permute-start = (bf16[80,512]{1,0:T(8,128)(2,1)S(1)}, bf16[80,512]{1,0:T(8,128)(2,1)S(1)}, u32[]{:S(2)}, u32[]{:S(2)}) collective-permute-start(bf16[80,512]{1,0:T(8,128)(2,1)S(1)} %get-tuple-element.40), channel_id=1, source_target_pairs={{1,2},{3,4},{5,6},{7,8},{9,10},{11,12},{13,14},{2,1},{4,3},{6,5},{... | collective-permute-start | bytes 245768 | tf_op jit(solution)/shard_map/ppermute | solution.py:311
  4.9 3.2 %collective-permute-start.1 = (bf16[80,512]{1,0:T(8,128)(2,1)S(1)}, bf16[80,512]{1,0:T(8,128)(2,1)S(1)}, u32[]{:S(2)}, u32[]{:S(2)}) collective-permute-start(bf16[80,512]{1,0:T(8,128)(2,1)S(1)} %get-tuple-element.39), channel_id=1, source_target_pairs={{0,1},{2,3},{4,5},{6,7},{8,9},{10,11},{12,13},{14,15},{1,0},{3,2},... | collective-permute-start | bytes 245768 | tf_op jit(solution)/shard_map/ppermute | solution.py:311
  8.7 10.3 %collective-permute-start.3 = (bf16[520,128]{1,0:T(8,128)(2,1)S(1)}, bf16[520,128]{1,0:T(8,128)(2,1)S(1)}, u32[]{:S(2)}, u32[]{:S(2)}) collective-permute-start(bf16[520,128]{1,0:T(8,128)(2,1)S(1)} %get-tuple-element.27), channel_id=1, source_target_pairs={{0,16},{32,48},{64,80},{96,112},{128,144},{160,176},{192,208},{224... | collective-permute-start | bytes 399368 | tf_op jit(solution)/shard_map/ppermute | solution.py:311
  14.9 28.0 %collective-permute-start.2 = (bf16[520,128]{1,0:T(8,128)(2,1)S(1)}, bf16[520,128]{1,0:T(8,128)(2,1)S(1)}, u32[]{:S(2)}, u32[]{:S(2)}) collective-permute-start(bf16[520,128]{1,0:T(8,128)(2,1)S(1)} %get-tuple-element.23), channel_id=1, source_target_pairs={{16,32},{48,64},{80,96},{112,128},{144,160},{176,192},{208,224},{2... | collective-permute-start | bytes 399368 | tf_op jit(solution)/shard_map/ppermute | solution.py:311
  45.3 4.7 %collective-permute-start.4 = (bf16[4,8,512]{2,1,0:T(8,128)(2,1)S(1)}, bf16[4,8,512]{2,1,0:T(8,128)(2,1)S(1)}, u32[]{:S(2)}, u32[]{:S(2)}) collective-permute-start(bf16[4,8,512]{2,1,0:T(8,128)(2,1)S(1)} %get-tuple-element.29), channel_id=1, source_target_pairs={{0,16},{32,48},{64,80},{96,112},{128,144},{160,176},{192,208},{224... | collective-permute-start | bytes 98312 | tf_op jit(solution)/shard_map/ppermute | solution.py:311
  47.2 17.6 %collective-permute-start.5 = (bf16[4,8,512]{2,1,0:T(8,128)(2,1)S(1)}, bf16[4,8,512]{2,1,0:T(8,128)(2,1)S(1)}, u32[]{:S(2)}, u32[]{:S(2)}) collective-permute-start(bf16[4,8,512]{2,1,0:T(8,128)(2,1)S(1)} %get-tuple-element.30), channel_id=1, source_target_pairs={{16,32},{48,64},{80,96},{112,128},{144,160},{176,192},{208,224},{2... | collective-permute-start | bytes 98312 | tf_op jit(solution)/shard_map/ppermute | solution.py:311
  64.9 8.3 %collective-permute-start.6 = (bf16[14,4,512]{2,1,0:T(4,128)(2,1)S(1)}, bf16[14,4,512]{2,1,0:T(4,128)(2,1)S(1)}, u32[]{:S(2)}, u32[]{:S(2)}) collective-permute-start(bf16[14,4,512]{2,1,0:T(4,128)(2,1)S(1)} %get-tuple-element.43), channel_id=1, source_target_pairs={{0,1},{2,3},{4,5},{6,7},{8,9},{10,11},{12,13},{14,15},{1,0},{3,2},... | collective-permute-start | bytes 172040 | tf_op jit(solution)/shard_map/ppermute | solution.py:311
  69.4 5.5 %collective-permute-start.7 = (bf16[14,4,512]{2,1,0:T(4,128)(2,1)S(1)}, bf16[14,4,512]{2,1,0:T(4,128)(2,1)S(1)}, u32[]{:S(2)}, u32[]{:S(2)}) collective-permute-start(bf16[14,4,512]{2,1,0:T(4,128)(2,1)S(1)} %get-tuple-element.44), channel_id=1, source_target_pairs={{1,2},{3,4},{5,6},{7,8},{9,10},{11,12},{13,14},{2,1},{4,3},{6,5},{... | collective-permute-start | bytes 172040 | tf_op jit(solution)/shard_map/ppermute | solution.py:311
  71.5 3.6 %copy-start.3 = (bf16[4,27,128,128]{3,2,1,0:T(8,128)(2,1)S(1)}, bf16[4,27,128,128]{3,2,1,0:T(8,128)(2,1)}, u32[]{:S(2)}) copy-start(bf16[4,27,128,128]{3,2,1,0:T(8,128)(2,1)} %w_coarse.1) | copy-start | bytes 10616836
  71.5 3.6 %copy-start.7 = (bf16[288,512]{1,0:T(8,128)(2,1)S(1)}, bf16[288,512]{1,0:T(8,128)(2,1)}, u32[]{:S(2)}) copy-start(bf16[288,512]{1,0:T(8,128)(2,1)} %constant.40.clone.from_groups) | copy-start | bytes 884740

commit v10 on v9

--- a/solution.py
+++ b/solution.py
@@ -182,6 +182,14 @@
         out_ref[g] = summed
 
 
+def transpose_kernel(source, target):
+    identity = jnp.where(iota((128, 128), 0) == iota((128, 128), 1), 1.0, 0.0).astype(BF)
+    for t in range(0, source.shape[0], 4):
+        pair = dot(identity, jnp.concatenate([source[t], source[t + 1]], axis=0), NT).astype(BF)
+        target[t], target[t + 1] = pair[:, :128], pair[:, 128:]
+        target[t + 2], target[t + 3] = source[t + 2].T, source[t + 3].T
+
+
 def coarse_kernel(bounds, coarse_ref, w_coarse, wupr, from_groups, up, state, raw):
     value = coarse_ref[...].reshape(224, 512).astype(F32)
     for layer in range(4):
@@ -195,12 +203,12 @@
         zero = jnp.zeros((128, 128), BF)
         for oa in range(3):
             for ob in range(3):
-                w = [w_coarse[layer, 9 * oa + 3 * ob + oz] for oz in range(3)]
-                middle = jnp.concatenate(w, axis=1)
-                w_low = jnp.concatenate([jnp.concatenate([w[1], w[2], zero], axis=1), middle], axis=0)
-                w_high = jnp.concatenate([middle, jnp.concatenate([zero, w[0], w[1]], axis=1)], axis=0)
-                low += dot(state[ob, 16 * oa : 16 * oa + rows, 0:384], w_low, NT)
-                high += dot(state[ob, 16 * oa : 16 * oa + rows, 128:512], w_high, NT)
+                w = [w_coarse[27 * layer + 9 * oa + 3 * ob + oz] for oz in range(3)]
+                one, two = jnp.concatenate([w[1], w[0]], axis=1), jnp.concatenate([w[2], w[1]], axis=1)
+                w_low = jnp.concatenate([one, two, jnp.concatenate([zero, w[2]], axis=1)], axis=0)
+                w_high = jnp.concatenate([jnp.concatenate([w[0], zero], axis=1), one, two], axis=0)
+                low += dot(state[ob, 16 * oa : 16 * oa + rows, 0:384], w_low, NN)
+                high += dot(state[ob, 16 * oa : 16 * oa + rows, 128:512], w_high, NN)
         index = iota((rows, 128), 0)
         a = (index >> 4) - 4 + layer
         b = (index & 15) - 4 + layer
@@ -373,6 +381,10 @@
     skip_weight, skip_edge, up_weight, up_edge, wupr = call(
         prepare_last_kernel, [weight, edge, weight, edge, offsets], [((2048, 128), F32)], 2, False, 1 << 28, 10
     )(closing_weight, w_up)
+    taps = w_coarse.shape[0] * w_coarse.shape[1]
+    (w_in_out,) = call(transpose_kernel, [((taps, 128, 128), BF)], [], 1, False, 1 << 28, 8)(
+        w_coarse.reshape(taps, 128, 128)
+    )
     shifts = [((3, 288, 512), BF), ((2, 288, 256), BF)]
     (part,) = call(skip_kernel, [((2, 256, 256), F32)], shifts, 5, True, 2 << 30, 8)(
         bounds, skip_near, skip_own, skip_far, skip_weight, skip_edge
@@ -385,7 +397,7 @@
     coarse = jnp.concatenate([before, coarse[:, 0:6], after, jnp.zeros((14, 2, 512), BF)], axis=1)
     (up,) = call(
         coarse_kernel, [((288, 768), BF)], [((3, 224, 512), BF), ((512, 768), F32)], 4, True, 3 << 30, 12
-    )(bounds, coarse, w_coarse, wupr, jnp.asarray(regroup().T[48:336], BF))
+    )(bounds, coarse, w_in_out, wupr, jnp.asarray(regroup().T[48:336], BF))
     (result,) = call(last_kernel, [((32, 16, 256), BF)], shifts, 4, False, 2 << 30, 12)(up, up_weight, up_edge, part)
     return result
 

time: 83.3 us -> 85.2 us (1.023)
  local copies, waits for them, and re-layouts: 1.15 us -> 3.58 us
    unnamed x16, local copies, waits for them, and re-layouts: 0.98 us -> 3.41 us
    pallas_call x1, Pallas kernels: 5.84 us -> 4.76 us  [local(): call(coarse_kernel, [((288, 768), BF)], [((3, 224, 512), BF), ((512, 768)...]
  transfers between devices with their start and end apart: 8 -> 8, of which waited for: 6 -> 6; matrix products, arithmetic and copies ran while one was open for 0% -> 0% of each run, Pallas kernels for 9% -> 10%
where the time goes in v10:
time: 85.2 us; the launch traced here: 84.8 us
  waiting for transfers between devices  39.4 us (46%)
  starting transfers between devices  22.9 us (27%)
  Pallas kernels  18 us (21%)
  local copies, waits for them, and re-layouts  3.58 us (4%)
    ppermute x8, waiting for transfers between devices, swap(): return lax.ppermute(array, axis, pairs + [(j, i) for i, j in pairs])  39.4 us
    ppermute x8, starting transfers between devices, swap(): return lax.ppermute(array, axis, pairs + [(j, i) for i, j in pairs])  22.9 us
    pallas_call x1, Pallas kernels, local(): call(coarse_kernel, [((288, 768), BF)], [((3, 224, 512), BF), ((512, 768)...  4.76 us
    unnamed x16, local copies, waits for them, and re-layouts  3.41 us
    pallas_call x1, Pallas kernels, local(): call(near_kernel, [skip, skip, cells, ((2, 8, 512), BF)], [((2, 3, 416, 2...  2.89 us
    pallas_call x1, Pallas kernels, local(): call(far_kernel, [skip, cells], [((1, 3, 416, 256), BF), ((1, 416, 256),...  2.37 us
    pallas_call x1, Pallas kernels, local(): call(last_kernel, [((32, 16, 256), BF)], shifts, 4, False, 2 << 30, 12)  2.07 us
    pallas_call x1, Pallas kernels, local(): call(skip_kernel, [((2, 256, 256), F32)], shifts, 5, True, 2 << 30, 8)  1.75 us
  transfers between devices with their start and end apart: 8, of which 6 were waited for; matrix products, arithmetic and copies ran while one was open for 0% of the time, Pallas kernels for 10%

profile of v10, /device:TPU:289, one launch (start us, length us, event | category | flops | bytes accessed | tf_op | source)
XLA Modules:
  0.0 84.8 jit_solution(9921605108860621514)
XLA Ops:
  0.0 0.0 copy-start
  0.0 0.9 %copy-done = bf16[32,16,256]{2,1,0:T(8,128)(2,1)S(1)} copy-done((bf16[32,16,256]{2,1,0:T(8,128)(2,1)S(1)}, bf16[32,16,256]{2,1,0:T(8,128)(2,1)}, u32[]{:S(2)}) %copy-start) | copy-done | bytes 262168
  1.0 0.0 copy-start.2
  1.0 0.0 copy-start.3
  1.0 0.5 fusion.own
  1.5 3.2 %collective-permute-start = (bf16[80,512]{1,0:T(8,128)(2,1)S(1)}, bf16[80,512]{1,0:T(8,128)(2,1)S(1)}, u32[]{:S(2)}, u32[]{:S(2)}) collective-permute-start(bf16[80,512]{1,0:T(8,128)(2,1)S(1)} %get-tuple-element.40), channel_id=1, source_target_pairs={{1,2},{3,4},{5,6},{7,8},{9,10},{11,12},{13,14},{2,1},{4,3},{6,5},{... | collective-permute-start | bytes 245768 | tf_op jit(solution)/shard_map/ppermute | solution.py:319
  4.7 1.9 %collective-permute-start.1 = (bf16[80,512]{1,0:T(8,128)(2,1)S(1)}, bf16[80,512]{1,0:T(8,128)(2,1)S(1)}, u32[]{:S(2)}, u32[]{:S(2)}) collective-permute-start(bf16[80,512]{1,0:T(8,128)(2,1)S(1)} %get-tuple-element.39), channel_id=1, source_target_pairs={{0,1},{2,3},{4,5},{6,7},{8,9},{10,11},{12,13},{14,15},{1,0},{3,2},... | collective-permute-start | bytes 245768 | tf_op jit(solution)/shard_map/ppermute | solution.py:319
  6.7 0.1 stack.37.bounds
  6.7 0.8 collective-permute-done.chips
  7.5 0.3 collective-permute-done.1.cores
  7.9 0.7 shard_map.82
  8.6 3.2 %collective-permute-start.3 = (bf16[520,128]{1,0:T(8,128)(2,1)S(1)}, bf16[520,128]{1,0:T(8,128)(2,1)S(1)}, u32[]{:S(2)}, u32[]{:S(2)}) collective-permute-start(bf16[520,128]{1,0:T(8,128)(2,1)S(1)} %get-tuple-element.27), channel_id=1, source_target_pairs={{0,16},{32,48},{64,80},{96,112},{128,144},{160,176},{192,208},{224... | collective-permute-start | bytes 399368 | tf_op jit(solution)/shard_map/ppermute | solution.py:319
  11.8 0.1 pad.3.clone
  11.9 0.0 copy-done.2
  11.9 0.0 copy-done.3
  11.9 1.1 %shard_map.83 = (bf16[9,256,256]{2,1,0:T(8,128)(2,1)S(1)}, bf16[3,256,256]{2,1,0:T(8,128)(2,1)S(1)}, bf16[16,128,128]{2,1,0:T(8,128)(2,1)S(1)}) custom-call(bf16[27,32,32]{2,1,0:T(8,128)(2,1)S(1)} %copy-done.3, bf16[2048,128]{1,0:T(8,128)(2,1)S(1)} %copy-done.2), custom_call_target="tpu_custom_call" | custom-call | flops 134217728 | bytes 4194304 | tf_op jit(solution)/shard_map/pallas_call | solution.py:356
  13.0 0.0 copy-start.1
  13.0 2.0 %copy-done.1 = bf16[4,27,128,128]{3,2,1,0:T(8,128)(2,1)S(1)} copy-done((bf16[4,27,128,128]{3,2,1,0:T(8,128)(2,1)S(1)}, bf16[4,27,128,128]{3,2,1,0:T(8,128)(2,1)}, u32[]{:S(2)}) %copy-start.1) | copy-done | bytes 3538968
  15.0 0.0 copy-start.4
  15.0 0.0 copy-start.5
  15.0 0.0 copy-start.6
  15.0 0.6 shard_map.86.w_coarse
  15.6 0.4 copy-done.4
  16.0 0.1 copy-done.5
  16.1 1.7 %shard_map.87 = (bf16[9,256,256]{2,1,0:T(8,128)(2,1)S(1)}, bf16[3,256,256]{2,1,0:T(8,128)(2,1)S(1)}, bf16[9,256,256]{2,1,0:T(8,128)(2,1)S(1)}, bf16[3,256,256]{2,1,0:T(8,128)(2,1)S(1)}, bf16[16,128,128]{2,1,0:T(8,128)(2,1)S(1)}) custom-call(bf16[27,32,64]{2,1,0:T(8,128)(2,1)S(1)} %copy-done.5, bf16[128,2048]{1,0:T(8,128)(2,1)S(1)} %copy-done.4), custom_call_target="tpu_custom_call" | custom-call | flops 268435456 | bytes 4194304 | tf_op jit(solution)/shard_map/pallas_call | solution.py:381
  17.8 4.2 %collective-permute-start.2 = (bf16[520,128]{1,0:T(8,128)(2,1)S(1)}, bf16[520,128]{1,0:T(8,128)(2,1)S(1)}, u32[]{:S(2)}, u32[]{:S(2)}) collective-permute-start(bf16[520,128]{1,0:T(8,128)(2,1)S(1)} %get-tuple-element.23), channel_id=1, source_target_pairs={{16,32},{48,64},{80,96},{112,128},{144,160},{176,192},{208,224},{2... | collective-permute-start | bytes 399368 | tf_op jit(solution)/shard_map/ppermute | solution.py:319
  22.0 0.0 collective-permute-done.3.near
  22.0 0.0 copy-done.6
  22.0 2.9 %shard_map.84 = (bf16[384,256]{1,0:T(8,128)(2,1)S(1)}, bf16[384,256]{1,0:T(8,128)(2,1)S(1)}, bf16[4,8,512]{2,1,0:T(8,128)(2,1)S(1)}, bf16[2,8,512]{2,1,0:T(8,128)(2,1)S(1)}) custom-call(s32[10]{0:T(128)S(1)} %stack.37.bounds, bf16[416,512]{1,0:T(8,128)(2,1)S(1)} %get-tuple-element.22.own, bf16[520,128]{1,0:T(8,128)(2,1)S(1)} %collective-permute-done.3.near, ...), custom_call_target="tpu_custom_call" | custom-call | flops 2147483648 | bytes 4194304 | tf_op jit(solution)/shard_map/pallas_call | solution.py:361
  24.9 21.0 %collective-permute-done.2.far = bf16[520,128]{1,0:T(8,128)(2,1)S(1)} collective-permute-done((bf16[520,128]{1,0:T(8,128)(2,1)S(1)}, bf16[520,128]{1,0:T(8,128)(2,1)S(1)}, u32[]{:S(2)}, u32[]{:S(2)}) %collective-permute-start.2) | collective-permute-done | bytes 133152 | tf_op jit(solution)/shard_map/ppermute | solution.py:319
  45.9 2.4 %shard_map.85 = (bf16[384,256]{1,0:T(8,128)(2,1)S(1)}, bf16[4,8,512]{2,1,0:T(8,128)(2,1)S(1)}) custom-call(s32[10]{0:T(128)S(1)} %stack.37.bounds, bf16[416,512]{1,0:T(8,128)(2,1)S(1)} %get-tuple-element.22.own, bf16[520,128]{1,0:T(8,128)(2,1)S(1)} %collective-permute-done.2.far, bf16[512,384]{1,0:T(8,128)(2,1)S(1)} %copy-done.6, ...), custom_call_target="tpu_custom_call" | custom-call | flops 1073741824 | bytes 4194304 | tf_op jit(solution)/shard_map/pallas_call | solution.py:371
  48.2 1.9 %collective-permute-start.4 = (bf16[4,8,512]{2,1,0:T(8,128)(2,1)S(1)}, bf16[4,8,512]{2,1,0:T(8,128)(2,1)S(1)}, u32[]{:S(2)}, u32[]{:S(2)}) collective-permute-start(bf16[4,8,512]{2,1,0:T(8,128)(2,1)S(1)} %get-tuple-element.29), channel_id=1, source_target_pairs={{0,16},{32,48},{64,80},{96,112},{128,144},{160,176},{192,208},{224... | collective-permute-start | bytes 98312 | tf_op jit(solution)/shard_map/ppermute | solution.py:319
  50.2 1.9 %collective-permute-start.5 = (bf16[4,8,512]{2,1,0:T(8,128)(2,1)S(1)}, bf16[4,8,512]{2,1,0:T(8,128)(2,1)S(1)}, u32[]{:S(2)}, u32[]{:S(2)}) collective-permute-start(bf16[4,8,512]{2,1,0:T(8,128)(2,1)S(1)} %get-tuple-element.30), channel_id=1, source_target_pairs={{16,32},{48,64},{80,96},{112,128},{144,160},{176,192},{208,224},{2... | collective-permute-start | bytes 98312 | tf_op jit(solution)/shard_map/ppermute | solution.py:319
  52.1 0.8 collective-permute-done.4
  52.9 14.9 %collective-permute-done.5 = bf16[4,8,512]{2,1,0:T(8,128)(2,1)S(1)} collective-permute-done((bf16[4,8,512]{2,1,0:T(8,128)(2,1)S(1)}, bf16[4,8,512]{2,1,0:T(8,128)(2,1)S(1)}, u32[]{:S(2)}, u32[]{:S(2)}) %collective-permute-start.5) | collective-permute-done | bytes 32800 | tf_op jit(solution)/shard_map/ppermute | solution.py:319
  67.8 0.1 broadcast_select_fusion.5
  67.9 4.4 %collective-permute-start.6 = (bf16[14,4,512]{2,1,0:T(4,128)(2,1)S(1)}, bf16[14,4,512]{2,1,0:T(4,128)(2,1)S(1)}, u32[]{:S(2)}, u32[]{:S(2)}) collective-permute-start(bf16[14,4,512]{2,1,0:T(4,128)(2,1)S(1)} %get-tuple-element.43), channel_id=1, source_target_pairs={{0,1},{2,3},{4,5},{6,7},{8,9},{10,11},{12,13},{14,15},{1,0},{3,2},... | collective-permute-start | bytes 172040 | tf_op jit(solution)/shard_map/ppermute | solution.py:319
  72.3 2.1 %collective-permute-start.7 = (bf16[14,4,512]{2,1,0:T(4,128)(2,1)S(1)}, bf16[14,4,512]{2,1,0:T(4,128)(2,1)S(1)}, u32[]{:S(2)}, u32[]{:S(2)}) collective-permute-start(bf16[14,4,512]{2,1,0:T(4,128)(2,1)S(1)} %get-tuple-element.44), channel_id=1, source_target_pairs={{1,2},{3,4},{5,6},{7,8},{9,10},{11,12},{13,14},{2,1},{4,3},{6,5},{... | collective-permute-start | bytes 172040 | tf_op jit(solution)/shard_map/ppermute | solution.py:319
  74.4 0.0 copy-start.7
  74.4 1.8 %shard_map.89.part_ref = f32[2,256,256]{2,1,0:T(8,128)S(1)} custom-call(s32[10]{0:T(128)S(1)} %stack.37.bounds, bf16[384,256]{1,0:T(8,128)(2,1)S(1)} %get-tuple-element.34.near, bf16[384,256]{1,0:T(8,128)(2,1)S(1)} %get-tuple-element.35.own, bf16[384,256]{1,0:T(8,128)(2,1)S(1)} %get-tuple-element.36.far, bf16[9,256,256]{2,1,0:T(8,128)(2,1)S(1)} %get-tuple-element.37.weight, ...), custom_call_target="tpu_custom_call" | custom-call | flops 2147483648 | bytes 4194304 | tf_op jit(solution)/shard_map/pallas_call | solution.py:389
  76.2 0.0 collective-permute-done.6
  76.2 1.6 %collective-permute-done.7 = bf16[14,4,512]{2,1,0:T(4,128)(2,1)S(1)} collective-permute-done((bf16[14,4,512]{2,1,0:T(4,128)(2,1)S(1)}, bf16[14,4,512]{2,1,0:T(4,128)(2,1)S(1)}, u32[]{:S(2)}, u32[]{:S(2)}) %collective-permute-start.7) | collective-permute-done | bytes 57376 | tf_op jit(solution)/shard_map/ppermute | solution.py:319
  77.8 0.1 maximum_maximum_fusion.coarse_ref
  77.9 0.0 copy-done.7
  78.0 4.8 %shard_map.88.up = bf16[288,768]{1,0:T(8,128)(2,1)S(1)} custom-call(s32[10]{0:T(128)S(1)} %stack.37.bounds, bf16[14,16,512]{2,1,0:T(8,128)(2,1)S(1)} %maximum_maximum_fusion.coarse_ref, bf16[108,128,128]{2,1,0:T(8,128)(2,1)S(1)} %shard_map.86.w_coarse, bf16[16,128,128]{2,1,0:T(8,128)(2,1)S(1)} %get-tuple-element.31.wupr, bf16[288,512]{1,0:T(8,128)(2,1)S(1)} %copy-done.7), custom_call_target="tpu_custom_call" | custom-call | flops 3221225472 | bytes 4194304 | tf_op jit(solution)/shard_map/pallas_call | solution.py:398
  82.7 2.1 %shard_map.90 = bf16[32,16,256]{2,1,0:T(8,128)(2,1)} custom-call(bf16[288,768]{1,0:T(8,128)(2,1)S(1)} %shard_map.88.up, bf16[9,256,256]{2,1,0:T(8,128)(2,1)S(1)} %get-tuple-element.32.weight, bf16[3,256,256]{2,1,0:T(8,128)(2,1)S(1)} %get-tuple-element.33.weight_edge, f32[2,256,256]{2,1,0:T(8,128)S(1)} %shard_map.89.part_ref), custom_call_target="tpu_custom_call" | custom-call | flops 2147483648 | bytes 4194304 | tf_op jit(solution)/shard_map/pallas_call | solution.py:401
  (7 shorter events, 0.1 us)
Async XLA Ops:
  0.0 1.0 %copy-start = (bf16[32,16,256]{2,1,0:T(8,128)(2,1)S(1)}, bf16[32,16,256]{2,1,0:T(8,128)(2,1)}, u32[]{:S(2)}) copy-start(bf16[32,16,256]{2,1,0:T(8,128)(2,1)} %param.8) | copy-start | bytes 786436
  1.0 10.9 %copy-start.2 = (bf16[2048,128]{1,0:T(8,128)(2,1)S(1)}, bf16[2048,128]{1,0:T(8,128)(2,1)}, u32[]{:S(2)}) copy-start(bf16[2048,128]{1,0:T(8,128)(2,1)} %down.1) | copy-start | bytes 1572868
  1.0 10.9 %copy-start.3 = (bf16[27,32,32]{2,1,0:T(8,128)(2,1)S(1)}, bf16[27,32,32]{2,1,0:T(8,128)(2,1)}, u32[]{:S(2)}) copy-start(bf16[27,32,32]{2,1,0:T(8,128)(2,1)} %first.1) | copy-start | bytes 165892
  1.5 6.0 %collective-permute-start = (bf16[80,512]{1,0:T(8,128)(2,1)S(1)}, bf16[80,512]{1,0:T(8,128)(2,1)S(1)}, u32[]{:S(2)}, u32[]{:S(2)}) collective-permute-start(bf16[80,512]{1,0:T(8,128)(2,1)S(1)} %get-tuple-element.40), channel_id=1, source_target_pairs={{1,2},{3,4},{5,6},{7,8},{9,10},{11,12},{13,14},{2,1},{4,3},{6,5},{... | collective-permute-start | bytes 245768 | tf_op jit(solution)/shard_map/ppermute | solution.py:319
  4.7 3.2 %collective-permute-start.1 = (bf16[80,512]{1,0:T(8,128)(2,1)S(1)}, bf16[80,512]{1,0:T(8,128)(2,1)S(1)}, u32[]{:S(2)}, u32[]{:S(2)}) collective-permute-start(bf16[80,512]{1,0:T(8,128)(2,1)S(1)} %get-tuple-element.39), channel_id=1, source_target_pairs={{0,1},{2,3},{4,5},{6,7},{8,9},{10,11},{12,13},{14,15},{1,0},{3,2},... | collective-permute-start | bytes 245768 | tf_op jit(solution)/shard_map/ppermute | solution.py:319
  8.6 13.4 %collective-permute-start.3 = (bf16[520,128]{1,0:T(8,128)(2,1)S(1)}, bf16[520,128]{1,0:T(8,128)(2,1)S(1)}, u32[]{:S(2)}, u32[]{:S(2)}) collective-permute-start(bf16[520,128]{1,0:T(8,128)(2,1)S(1)} %get-tuple-element.27), channel_id=1, source_target_pairs={{0,16},{32,48},{64,80},{96,112},{128,144},{160,176},{192,208},{224... | collective-permute-start | bytes 399368 | tf_op jit(solution)/shard_map/ppermute | solution.py:319
  13.0 2.0 %copy-start.1 = (bf16[4,27,128,128]{3,2,1,0:T(8,128)(2,1)S(1)}, bf16[4,27,128,128]{3,2,1,0:T(8,128)(2,1)}, u32[]{:S(2)}) copy-start(bf16[4,27,128,128]{3,2,1,0:T(8,128)(2,1)} %param.11) | copy-start | bytes 10616836
  15.0 1.0 %copy-start.4 = (bf16[128,2048]{1,0:T(8,128)(2,1)S(1)}, bf16[128,2048]{1,0:T(8,128)(2,1)}, u32[]{:S(2)}) copy-start(bf16[128,2048]{1,0:T(8,128)(2,1)} %up.1) | copy-start | bytes 1572868
  15.0 1.1 %copy-start.5 = (bf16[27,32,64]{2,1,0:T(8,128)(2,1)S(1)}, bf16[27,32,64]{2,1,0:T(8,128)(2,1)}, u32[]{:S(2)}) copy-start(bf16[27,32,64]{2,1,0:T(8,128)(2,1)} %closing.1) | copy-start | bytes 331780
  15.0 7.0 %copy-start.6 = (bf16[512,384]{1,0:T(8,128)(2,1)S(1)}, bf16[512,384]{1,0:T(8,128)(2,1)}, u32[]{:S(2)}) copy-start(bf16[512,384]{1,0:T(8,128)(2,1)} %constant.39.clone.groups) | copy-start | bytes 1179652
  17.8 28.1 %collective-permute-start.2 = (bf16[520,128]{1,0:T(8,128)(2,1)S(1)}, bf16[520,128]{1,0:T(8,128)(2,1)S(1)}, u32[]{:S(2)}, u32[]{:S(2)}) collective-permute-start(bf16[520,128]{1,0:T(8,128)(2,1)S(1)} %get-tuple-element.23), channel_id=1, source_target_pairs={{16,32},{48,64},{80,96},{112,128},{144,160},{176,192},{208,224},{2... | collective-permute-start | bytes 399368 | tf_op jit(solution)/shard_map/ppermute | solution.py:319
  48.2 4.7 %collective-permute-start.4 = (bf16[4,8,512]{2,1,0:T(8,128)(2,1)S(1)}, bf16[4,8,512]{2,1,0:T(8,128)(2,1)S(1)}, u32[]{:S(2)}, u32[]{:S(2)}) collective-permute-start(bf16[4,8,512]{2,1,0:T(8,128)(2,1)S(1)} %get-tuple-element.29), channel_id=1, source_target_pairs={{0,16},{32,48},{64,80},{96,112},{128,144},{160,176},{192,208},{224... | collective-permute-start | bytes 98312 | tf_op jit(solution)/shard_map/ppermute | solution.py:319
  50.2 17.6 %collective-permute-start.5 = (bf16[4,8,512]{2,1,0:T(8,128)(2,1)S(1)}, bf16[4,8,512]{2,1,0:T(8,128)(2,1)S(1)}, u32[]{:S(2)}, u32[]{:S(2)}) collective-permute-start(bf16[4,8,512]{2,1,0:T(8,128)(2,1)S(1)} %get-tuple-element.30), channel_id=1, source_target_pairs={{16,32},{48,64},{80,96},{112,128},{144,160},{176,192},{208,224},{2... | collective-permute-start | bytes 98312 | tf_op jit(solution)/shard_map/ppermute | solution.py:319
  67.9 8.3 %collective-permute-start.6 = (bf16[14,4,512]{2,1,0:T(4,128)(2,1)S(1)}, bf16[14,4,512]{2,1,0:T(4,128)(2,1)S(1)}, u32[]{:S(2)}, u32[]{:S(2)}) collective-permute-start(bf16[14,4,512]{2,1,0:T(4,128)(2,1)S(1)} %get-tuple-element.43), channel_id=1, source_target_pairs={{0,1},{2,3},{4,5},{6,7},{8,9},{10,11},{12,13},{14,15},{1,0},{3,2},... | collective-permute-start | bytes 172040 | tf_op jit(solution)/shard_map/ppermute | solution.py:319
  72.3 5.5 %collective-permute-start.7 = (bf16[14,4,512]{2,1,0:T(4,128)(2,1)S(1)}, bf16[14,4,512]{2,1,0:T(4,128)(2,1)S(1)}, u32[]{:S(2)}, u32[]{:S(2)}) collective-permute-start(bf16[14,4,512]{2,1,0:T(4,128)(2,1)S(1)} %get-tuple-element.44), channel_id=1, source_target_pairs={{1,2},{3,4},{5,6},{7,8},{9,10},{11,12},{13,14},{2,1},{4,3},{6,5},{... | collective-permute-start | bytes 172040 | tf_op jit(solution)/shard_map/ppermute | solution.py:319
  74.4 3.5 %copy-start.7 = (bf16[288,512]{1,0:T(8,128)(2,1)S(1)}, bf16[288,512]{1,0:T(8,128)(2,1)}, u32[]{:S(2)}) copy-start(bf16[288,512]{1,0:T(8,128)(2,1)} %constant.40.clone.from_groups) | copy-start | bytes 884740

commit v11 on v10

--- a/solution.py
+++ b/solution.py
@@ -275,8 +275,11 @@
             target[i, 32 * x : 32 * x + 32] = tall[pl.ds(16 * x + i, 32, stride=64), :].astype(BF)
 
 
-def prepare_first_kernel(first, down, w1, w1_edge, dwr, tall):
+def prepare_first_kernel(first, w1, w1_edge):
     banded(first, w1, w1_edge, 0)
+
+
+def prepare_down_kernel(down, dwr, tall):
     tall[...] = down[...].astype(F32)
     by_offset(tall, dwr)
 
@@ -353,9 +356,8 @@
     near = swap(to_near, "sx", 0)
     far = swap(to_far, "sx", 1)
     weight, edge, offsets = ((9, 256, 256), BF), ((3, 256, 256), BF), ((16, 128, 128), BF)
-    w1, w1_edge, dwr = call(
-        prepare_first_kernel, [weight, edge, offsets], [((2048, 128), F32)], 2, False, 1 << 27, 8
-    )(w_first, down_weight)
+    (dwr,) = call(prepare_down_kernel, [offsets], [((2048, 128), F32)], 1, False, 1 << 26, 8)(down_weight)
+    w1, w1_edge = call(prepare_first_kernel, [weight, edge], [], 1, False, 1 << 27, 8)(w_first)
     skip, cells = ((384, 256), BF), ((4, 8, 512), BF)
     groups = jnp.asarray(regroup(), BF)
     skip_near, skip_own, to_far, coarse_own = call(

time: 85.2 us -> 85.4 us (level)
  no operation moved by 1% of the time
where the time goes in v11:
time: 85.4 us; the launch traced here: 85 us
  waiting for transfers between devices  39.4 us (46%)
  starting transfers between devices  23 us (27%)
  Pallas kernels  18 us (21%)
  local copies, waits for them, and re-layouts  3.58 us (4%)
    ppermute x8, waiting for transfers between devices, swap(): return lax.ppermute(array, axis, pairs + [(j, i) for i, j in pairs])  39.4 us
    ppermute x8, starting transfers between devices, swap(): return lax.ppermute(array, axis, pairs + [(j, i) for i, j in pairs])  23 us
    pallas_call x1, Pallas kernels, local(): call(coarse_kernel, [((288, 768), BF)], [((3, 224, 512), BF), ((512, 768)...  4.76 us
    unnamed x16, local copies, waits for them, and re-layouts  3.41 us
    pallas_call x1, Pallas kernels, local(): call(near_kernel, [skip, skip, cells, ((2, 8, 512), BF)], [((2, 3, 416, 2...  2.89 us
    pallas_call x1, Pallas kernels, local(): call(far_kernel, [skip, cells], [((1, 3, 416, 256), BF), ((1, 416, 256),...  2.35 us
    pallas_call x1, Pallas kernels, local(): call(last_kernel, [((32, 16, 256), BF)], shifts, 4, False, 2 << 30, 12)  2.07 us
    pallas_call x1, Pallas kernels, local(): call(skip_kernel, [((2, 256, 256), F32)], shifts, 5, True, 2 << 30, 8)  1.75 us
  transfers between devices with their start and end apart: 8, of which 6 were waited for; matrix products, arithmetic and copies ran while one was open for 0% of the time, Pallas kernels for 10%

profile of v11, /device:TPU:289, one launch (start us, length us, event | category | flops | bytes accessed | tf_op | source)
XLA Modules:
  0.0 85.0 jit_solution(17519507589317361221)
XLA Ops:
  0.0 0.0 copy-start
  0.0 0.9 %copy-done = bf16[32,16,256]{2,1,0:T(8,128)(2,1)S(1)} copy-done((bf16[32,16,256]{2,1,0:T(8,128)(2,1)S(1)}, bf16[32,16,256]{2,1,0:T(8,128)(2,1)}, u32[]{:S(2)}) %copy-start) | copy-done | bytes 262168
  1.0 0.0 copy-start.2
  1.0 0.5 fusion.own
  1.5 0.0 copy-start.4
  1.5 3.3 %collective-permute-start = (bf16[80,512]{1,0:T(8,128)(2,1)S(1)}, bf16[80,512]{1,0:T(8,128)(2,1)S(1)}, u32[]{:S(2)}, u32[]{:S(2)}) collective-permute-start(bf16[80,512]{1,0:T(8,128)(2,1)S(1)} %get-tuple-element.38), channel_id=1, source_target_pairs={{1,2},{3,4},{5,6},{7,8},{9,10},{11,12},{13,14},{2,1},{4,3},{6,5},{... | collective-permute-start | bytes 245768 | tf_op jit(solution)/shard_map/ppermute | solution.py:322
  4.8 1.9 %collective-permute-start.1 = (bf16[80,512]{1,0:T(8,128)(2,1)S(1)}, bf16[80,512]{1,0:T(8,128)(2,1)S(1)}, u32[]{:S(2)}, u32[]{:S(2)}) collective-permute-start(bf16[80,512]{1,0:T(8,128)(2,1)S(1)} %get-tuple-element.37), channel_id=1, source_target_pairs={{0,1},{2,3},{4,5},{6,7},{8,9},{10,11},{12,13},{14,15},{1,0},{3,2},... | collective-permute-start | bytes 245768 | tf_op jit(solution)/shard_map/ppermute | solution.py:322
  6.8 0.1 stack.37.bounds
  6.9 0.8 collective-permute-done.chips
  7.7 0.3 collective-permute-done.1.cores
  8.0 0.7 shard_map.82
  8.7 3.2 %collective-permute-start.3 = (bf16[520,128]{1,0:T(8,128)(2,1)S(1)}, bf16[520,128]{1,0:T(8,128)(2,1)S(1)}, u32[]{:S(2)}, u32[]{:S(2)}) collective-permute-start(bf16[520,128]{1,0:T(8,128)(2,1)S(1)} %get-tuple-element.25), channel_id=1, source_target_pairs={{0,16},{32,48},{64,80},{96,112},{128,144},{160,176},{192,208},{224... | collective-permute-start | bytes 399368 | tf_op jit(solution)/shard_map/ppermute | solution.py:322
  11.9 0.1 pad.3.clone
  12.0 0.0 copy-done.2
  12.0 0.6 shard_map.84.dwr
  12.7 0.0 copy-done.4
  12.7 0.5 shard_map.83
  13.2 0.0 copy-start.1
  13.2 2.0 %copy-done.1 = bf16[4,27,128,128]{3,2,1,0:T(8,128)(2,1)S(1)} copy-done((bf16[4,27,128,128]{3,2,1,0:T(8,128)(2,1)S(1)}, bf16[4,27,128,128]{3,2,1,0:T(8,128)(2,1)}, u32[]{:S(2)}) %copy-start.1) | copy-done | bytes 3538968
  15.2 0.0 copy-start.3
  15.2 0.0 copy-start.5
  15.2 0.0 copy-start.6
  15.2 0.6 shard_map.87.w_coarse
  15.8 0.4 copy-done.3
  16.2 0.1 copy-done.5
  16.3 1.7 %shard_map.88 = (bf16[9,256,256]{2,1,0:T(8,128)(2,1)S(1)}, bf16[3,256,256]{2,1,0:T(8,128)(2,1)S(1)}, bf16[9,256,256]{2,1,0:T(8,128)(2,1)S(1)}, bf16[3,256,256]{2,1,0:T(8,128)(2,1)S(1)}, bf16[16,128,128]{2,1,0:T(8,128)(2,1)S(1)}) custom-call(bf16[27,32,64]{2,1,0:T(8,128)(2,1)S(1)} %copy-done.5, bf16[128,2048]{1,0:T(8,128)(2,1)S(1)} %copy-done.3), custom_call_target="tpu_custom_call" | custom-call | flops 268435456 | bytes 4194304 | tf_op jit(solution)/shard_map/pallas_call | solution.py:383
  18.0 4.2 %collective-permute-start.2 = (bf16[520,128]{1,0:T(8,128)(2,1)S(1)}, bf16[520,128]{1,0:T(8,128)(2,1)S(1)}, u32[]{:S(2)}, u32[]{:S(2)}) collective-permute-start(bf16[520,128]{1,0:T(8,128)(2,1)S(1)} %get-tuple-element.22), channel_id=1, source_target_pairs={{16,32},{48,64},{80,96},{112,128},{144,160},{176,192},{208,224},{2... | collective-permute-start | bytes 399368 | tf_op jit(solution)/shard_map/ppermute | solution.py:322
  22.1 0.0 collective-permute-done.3.near
  22.1 0.0 copy-done.6
  22.1 2.9 %shard_map.85 = (bf16[384,256]{1,0:T(8,128)(2,1)S(1)}, bf16[384,256]{1,0:T(8,128)(2,1)S(1)}, bf16[4,8,512]{2,1,0:T(8,128)(2,1)S(1)}, bf16[2,8,512]{2,1,0:T(8,128)(2,1)S(1)}) custom-call(s32[10]{0:T(128)S(1)} %stack.37.bounds, bf16[416,512]{1,0:T(8,128)(2,1)S(1)} %get-tuple-element.21.own, bf16[520,128]{1,0:T(8,128)(2,1)S(1)} %collective-permute-done.3.near, ...), custom_call_target="tpu_custom_call" | custom-call | flops 2147483648 | bytes 4194304 | tf_op jit(solution)/shard_map/pallas_call | solution.py:363
  25.0 21.0 %collective-permute-done.2.far = bf16[520,128]{1,0:T(8,128)(2,1)S(1)} collective-permute-done((bf16[520,128]{1,0:T(8,128)(2,1)S(1)}, bf16[520,128]{1,0:T(8,128)(2,1)S(1)}, u32[]{:S(2)}, u32[]{:S(2)}) %collective-permute-start.2) | collective-permute-done | bytes 133152 | tf_op jit(solution)/shard_map/ppermute | solution.py:322
  46.0 2.4 %shard_map.86 = (bf16[384,256]{1,0:T(8,128)(2,1)S(1)}, bf16[4,8,512]{2,1,0:T(8,128)(2,1)S(1)}) custom-call(s32[10]{0:T(128)S(1)} %stack.37.bounds, bf16[416,512]{1,0:T(8,128)(2,1)S(1)} %get-tuple-element.21.own, bf16[520,128]{1,0:T(8,128)(2,1)S(1)} %collective-permute-done.2.far, bf16[512,384]{1,0:T(8,128)(2,1)S(1)} %copy-done.6, ...), custom_call_target="tpu_custom_call" | custom-call | flops 1073741824 | bytes 4194304 | tf_op jit(solution)/shard_map/pallas_call | solution.py:373
  48.4 1.9 %collective-permute-start.4 = (bf16[4,8,512]{2,1,0:T(8,128)(2,1)S(1)}, bf16[4,8,512]{2,1,0:T(8,128)(2,1)S(1)}, u32[]{:S(2)}, u32[]{:S(2)}) collective-permute-start(bf16[4,8,512]{2,1,0:T(8,128)(2,1)S(1)} %get-tuple-element.27), channel_id=1, source_target_pairs={{0,16},{32,48},{64,80},{96,112},{128,144},{160,176},{192,208},{224... | collective-permute-start | bytes 98312 | tf_op jit(solution)/shard_map/ppermute | solution.py:322
  50.3 1.9 %collective-permute-start.5 = (bf16[4,8,512]{2,1,0:T(8,128)(2,1)S(1)}, bf16[4,8,512]{2,1,0:T(8,128)(2,1)S(1)}, u32[]{:S(2)}, u32[]{:S(2)}) collective-permute-start(bf16[4,8,512]{2,1,0:T(8,128)(2,1)S(1)} %get-tuple-element.28), channel_id=1, source_target_pairs={{16,32},{48,64},{80,96},{112,128},{144,160},{176,192},{208,224},{2... | collective-permute-start | bytes 98312 | tf_op jit(solution)/shard_map/ppermute | solution.py:322
  52.2 0.8 collective-permute-done.4
  53.0 14.9 %collective-permute-done.5 = bf16[4,8,512]{2,1,0:T(8,128)(2,1)S(1)} collective-permute-done((bf16[4,8,512]{2,1,0:T(8,128)(2,1)S(1)}, bf16[4,8,512]{2,1,0:T(8,128)(2,1)S(1)}, u32[]{:S(2)}, u32[]{:S(2)}) %collective-permute-start.5) | collective-permute-done | bytes 32800 | tf_op jit(solution)/shard_map/ppermute | solution.py:322
  67.9 0.1 broadcast_select_fusion.5
  68.0 4.5 %collective-permute-start.6 = (bf16[14,4,512]{2,1,0:T(4,128)(2,1)S(1)}, bf16[14,4,512]{2,1,0:T(4,128)(2,1)S(1)}, u32[]{:S(2)}, u32[]{:S(2)}) collective-permute-start(bf16[14,4,512]{2,1,0:T(4,128)(2,1)S(1)} %get-tuple-element.41), channel_id=1, source_target_pairs={{0,1},{2,3},{4,5},{6,7},{8,9},{10,11},{12,13},{14,15},{1,0},{3,2},... | collective-permute-start | bytes 172040 | tf_op jit(solution)/shard_map/ppermute | solution.py:322
  72.5 2.1 %collective-permute-start.7 = (bf16[14,4,512]{2,1,0:T(4,128)(2,1)S(1)}, bf16[14,4,512]{2,1,0:T(4,128)(2,1)S(1)}, u32[]{:S(2)}, u32[]{:S(2)}) collective-permute-start(bf16[14,4,512]{2,1,0:T(4,128)(2,1)S(1)} %get-tuple-element.42), channel_id=1, source_target_pairs={{1,2},{3,4},{5,6},{7,8},{9,10},{11,12},{13,14},{2,1},{4,3},{6,5},{... | collective-permute-start | bytes 172040 | tf_op jit(solution)/shard_map/ppermute | solution.py:322
  74.6 0.0 copy-start.7
  74.6 1.8 %shard_map.90.part_ref = f32[2,256,256]{2,1,0:T(8,128)S(1)} custom-call(s32[10]{0:T(128)S(1)} %stack.37.bounds, bf16[384,256]{1,0:T(8,128)(2,1)S(1)} %get-tuple-element.32.near, bf16[384,256]{1,0:T(8,128)(2,1)S(1)} %get-tuple-element.33.own, bf16[384,256]{1,0:T(8,128)(2,1)S(1)} %get-tuple-element.34.far, bf16[9,256,256]{2,1,0:T(8,128)(2,1)S(1)} %get-tuple-element.35.weight, ...), custom_call_target="tpu_custom_call" | custom-call | flops 2147483648 | bytes 4194304 | tf_op jit(solution)/shard_map/pallas_call | solution.py:391
  76.4 0.0 collective-permute-done.6
  76.4 1.6 %collective-permute-done.7 = bf16[14,4,512]{2,1,0:T(4,128)(2,1)S(1)} collective-permute-done((bf16[14,4,512]{2,1,0:T(4,128)(2,1)S(1)}, bf16[14,4,512]{2,1,0:T(4,128)(2,1)S(1)}, u32[]{:S(2)}, u32[]{:S(2)}) %collective-permute-start.7) | collective-permute-done | bytes 57376 | tf_op jit(solution)/shard_map/ppermute | solution.py:322
  78.0 0.1 maximum_maximum_fusion.coarse_ref
  78.1 0.0 copy-done.7
  78.1 4.8 %shard_map.89.up = bf16[288,768]{1,0:T(8,128)(2,1)S(1)} custom-call(s32[10]{0:T(128)S(1)} %stack.37.bounds, bf16[14,16,512]{2,1,0:T(8,128)(2,1)S(1)} %maximum_maximum_fusion.coarse_ref, bf16[108,128,128]{2,1,0:T(8,128)(2,1)S(1)} %shard_map.87.w_coarse, bf16[16,128,128]{2,1,0:T(8,128)(2,1)S(1)} %get-tuple-element.29.wupr, bf16[288,512]{1,0:T(8,128)(2,1)S(1)} %copy-done.7), custom_call_target="tpu_custom_call" | custom-call | flops 3221225472 | bytes 4194304 | tf_op jit(solution)/shard_map/pallas_call | solution.py:400
  82.9 2.1 %shard_map.91 = bf16[32,16,256]{2,1,0:T(8,128)(2,1)} custom-call(bf16[288,768]{1,0:T(8,128)(2,1)S(1)} %shard_map.89.up, bf16[9,256,256]{2,1,0:T(8,128)(2,1)S(1)} %get-tuple-element.30.weight, bf16[3,256,256]{2,1,0:T(8,128)(2,1)S(1)} %get-tuple-element.31.weight_edge, f32[2,256,256]{2,1,0:T(8,128)S(1)} %shard_map.90.part_ref), custom_call_target="tpu_custom_call" | custom-call | flops 2147483648 | bytes 4194304 | tf_op jit(solution)/shard_map/pallas_call | solution.py:403
  (7 shorter events, 0.1 us)
Async XLA Ops:
  0.0 1.0 %copy-start = (bf16[32,16,256]{2,1,0:T(8,128)(2,1)S(1)}, bf16[32,16,256]{2,1,0:T(8,128)(2,1)}, u32[]{:S(2)}) copy-start(bf16[32,16,256]{2,1,0:T(8,128)(2,1)} %param.8) | copy-start | bytes 786436
  1.0 11.1 %copy-start.2 = (bf16[2048,128]{1,0:T(8,128)(2,1)S(1)}, bf16[2048,128]{1,0:T(8,128)(2,1)}, u32[]{:S(2)}) copy-start(bf16[2048,128]{1,0:T(8,128)(2,1)} %down.1) | copy-start | bytes 1572868
  1.5 11.2 %copy-start.4 = (bf16[27,32,32]{2,1,0:T(8,128)(2,1)S(1)}, bf16[27,32,32]{2,1,0:T(8,128)(2,1)}, u32[]{:S(2)}) copy-start(bf16[27,32,32]{2,1,0:T(8,128)(2,1)} %first.1) | copy-start | bytes 165892
  1.5 6.2 %collective-permute-start = (bf16[80,512]{1,0:T(8,128)(2,1)S(1)}, bf16[80,512]{1,0:T(8,128)(2,1)S(1)}, u32[]{:S(2)}, u32[]{:S(2)}) collective-permute-start(bf16[80,512]{1,0:T(8,128)(2,1)S(1)} %get-tuple-element.38), channel_id=1, source_target_pairs={{1,2},{3,4},{5,6},{7,8},{9,10},{11,12},{13,14},{2,1},{4,3},{6,5},{... | collective-permute-start | bytes 245768 | tf_op jit(solution)/shard_map/ppermute | solution.py:322
  4.8 3.2 %collective-permute-start.1 = (bf16[80,512]{1,0:T(8,128)(2,1)S(1)}, bf16[80,512]{1,0:T(8,128)(2,1)S(1)}, u32[]{:S(2)}, u32[]{:S(2)}) collective-permute-start(bf16[80,512]{1,0:T(8,128)(2,1)S(1)} %get-tuple-element.37), channel_id=1, source_target_pairs={{0,1},{2,3},{4,5},{6,7},{8,9},{10,11},{12,13},{14,15},{1,0},{3,2},... | collective-permute-start | bytes 245768 | tf_op jit(solution)/shard_map/ppermute | solution.py:322
  8.7 13.4 %collective-permute-start.3 = (bf16[520,128]{1,0:T(8,128)(2,1)S(1)}, bf16[520,128]{1,0:T(8,128)(2,1)S(1)}, u32[]{:S(2)}, u32[]{:S(2)}) collective-permute-start(bf16[520,128]{1,0:T(8,128)(2,1)S(1)} %get-tuple-element.25), channel_id=1, source_target_pairs={{0,16},{32,48},{64,80},{96,112},{128,144},{160,176},{192,208},{224... | collective-permute-start | bytes 399368 | tf_op jit(solution)/shard_map/ppermute | solution.py:322
  13.2 2.0 %copy-start.1 = (bf16[4,27,128,128]{3,2,1,0:T(8,128)(2,1)S(1)}, bf16[4,27,128,128]{3,2,1,0:T(8,128)(2,1)}, u32[]{:S(2)}) copy-start(bf16[4,27,128,128]{3,2,1,0:T(8,128)(2,1)} %param.11) | copy-start | bytes 10616836
  15.2 1.0 %copy-start.3 = (bf16[128,2048]{1,0:T(8,128)(2,1)S(1)}, bf16[128,2048]{1,0:T(8,128)(2,1)}, u32[]{:S(2)}) copy-start(bf16[128,2048]{1,0:T(8,128)(2,1)} %up.1) | copy-start | bytes 1572868
  15.2 1.1 %copy-start.5 = (bf16[27,32,64]{2,1,0:T(8,128)(2,1)S(1)}, bf16[27,32,64]{2,1,0:T(8,128)(2,1)}, u32[]{:S(2)}) copy-start(bf16[27,32,64]{2,1,0:T(8,128)(2,1)} %closing.1) | copy-start | bytes 331780
  15.2 7.0 %copy-start.6 = (bf16[512,384]{1,0:T(8,128)(2,1)S(1)}, bf16[512,384]{1,0:T(8,128)(2,1)}, u32[]{:S(2)}) copy-start(bf16[512,384]{1,0:T(8,128)(2,1)} %constant.39.clone.groups) | copy-start | bytes 1179652
  18.0 28.1 %collective-permute-start.2 = (bf16[520,128]{1,0:T(8,128)(2,1)S(1)}, bf16[520,128]{1,0:T(8,128)(2,1)S(1)}, u32[]{:S(2)}, u32[]{:S(2)}) collective-permute-start(bf16[520,128]{1,0:T(8,128)(2,1)S(1)} %get-tuple-element.22), channel_id=1, source_target_pairs={{16,32},{48,64},{80,96},{112,128},{144,160},{176,192},{208,224},{2... | collective-permute-start | bytes 399368 | tf_op jit(solution)/shard_map/ppermute | solution.py:322
  48.4 4.7 %collective-permute-start.4 = (bf16[4,8,512]{2,1,0:T(8,128)(2,1)S(1)}, bf16[4,8,512]{2,1,0:T(8,128)(2,1)S(1)}, u32[]{:S(2)}, u32[]{:S(2)}) collective-permute-start(bf16[4,8,512]{2,1,0:T(8,128)(2,1)S(1)} %get-tuple-element.27), channel_id=1, source_target_pairs={{0,16},{32,48},{64,80},{96,112},{128,144},{160,176},{192,208},{224... | collective-permute-start | bytes 98312 | tf_op jit(solution)/shard_map/ppermute | solution.py:322
  50.3 17.6 %collective-permute-start.5 = (bf16[4,8,512]{2,1,0:T(8,128)(2,1)S(1)}, bf16[4,8,512]{2,1,0:T(8,128)(2,1)S(1)}, u32[]{:S(2)}, u32[]{:S(2)}) collective-permute-start(bf16[4,8,512]{2,1,0:T(8,128)(2,1)S(1)} %get-tuple-element.28), channel_id=1, source_target_pairs={{16,32},{48,64},{80,96},{112,128},{144,160},{176,192},{208,224},{2... | collective-permute-start | bytes 98312 | tf_op jit(solution)/shard_map/ppermute | solution.py:322
  68.0 8.4 %collective-permute-start.6 = (bf16[14,4,512]{2,1,0:T(4,128)(2,1)S(1)}, bf16[14,4,512]{2,1,0:T(4,128)(2,1)S(1)}, u32[]{:S(2)}, u32[]{:S(2)}) collective-permute-start(bf16[14,4,512]{2,1,0:T(4,128)(2,1)S(1)} %get-tuple-element.41), channel_id=1, source_target_pairs={{0,1},{2,3},{4,5},{6,7},{8,9},{10,11},{12,13},{14,15},{1,0},{3,2},... | collective-permute-start | bytes 172040 | tf_op jit(solution)/shard_map/ppermute | solution.py:322
  72.5 5.5 %collective-permute-start.7 = (bf16[14,4,512]{2,1,0:T(4,128)(2,1)S(1)}, bf16[14,4,512]{2,1,0:T(4,128)(2,1)S(1)}, u32[]{:S(2)}, u32[]{:S(2)}) collective-permute-start(bf16[14,4,512]{2,1,0:T(4,128)(2,1)S(1)} %get-tuple-element.42), channel_id=1, source_target_pairs={{1,2},{3,4},{5,6},{7,8},{9,10},{11,12},{13,14},{2,1},{4,3},{6,5},{... | collective-permute-start | bytes 172040 | tf_op jit(solution)/shard_map/ppermute | solution.py:322
  74.6 3.6 %copy-start.7 = (bf16[288,512]{1,0:T(8,128)(2,1)S(1)}, bf16[288,512]{1,0:T(8,128)(2,1)}, u32[]{:S(2)}) copy-start(bf16[288,512]{1,0:T(8,128)(2,1)} %constant.40.clone.from_groups) | copy-start | bytes 884740
